TPU v7x, 256 devices: a whole 4x4x8 slice. The times are simulated.
256 devices in a mesh: ta: 16 (over y, x), sa: 16 (over z, core).
Axes of the slice: x: 4, y: 4, z: 8, core: 2. Of those that a mesh axis runs over, the one named last changes fastest.
Arguments:
- perambulator: bfloat16 [2, 16, 16, 384, 384], P(None, None, 'sa', 'ta'), may hold values from -6 to 6
- meson_ops: bfloat16 [2, 8, 16, 384, 384], P(None, None, 'ta'), may hold values from -0.21875 to 0.21875
- diagram_lists: int32 [16, 128, 2], P('ta', 'sa'), may hold values from 0 to 127, as said below
Outputs:
- correlators: float32 [2, 16, 16, 384, 384], P(None, 'ta', 'sa')
Inputs may be any that keep to these rules, and one draw needn't show every extreme that they name: `diagram_lists`: every id lies in 0 to 127. Among the 16 ids of one owner's list, no spin pair (id // 8) occurs more than 2 times, and at least one spin pair occurs exactly 2 times; several may.
All inputs are finite; a program needn't handle non-finite values.
Results may differ from a plain program's by a relative error of at most 0.004.
Values may be sent and summed in bfloat16 or wider, within the bound.
No kernel may reach another device: no remote copies, remote signals or barrier semaphores. Data moves between devices by JAX's collectives and lax.ppermute only.
A program may use at most 128 MiB of HBM per device.

v0:
```python
import jax
import jax.numpy as jnp
from jax import lax
from jax.sharding import PartitionSpec as P

CAP = 2


def contract(first, second):
    return lax.dot_general(
        first, second, (((0, 2), (0, 1)), ((), ())), preferred_element_type=jnp.float32
    )


def body(perambulator, meson_ops, diagram_lists):
    regrouped = lax.all_to_all(perambulator, "ta", split_axis=1, concat_axis=3, tiled=True)
    operators = meson_ops[:, :, 0]
    ops_count = operators.shape[1]
    eig_count = operators.shape[2]
    pair_count = diagram_lists.shape[1]
    own_ids = diagram_lists[0].reshape(2 * pair_count)
    spin_ids = own_ids // ops_count
    peram_real = regrouped[0, 0, 0]
    peram_imag = regrouped[1, 0, 0]
    block_real = jnp.einsum(
        "oik,jk->oij", operators[0], peram_real, preferred_element_type=jnp.float32
    ) - jnp.einsum("oik,jk->oij", operators[1], peram_imag, preferred_element_type=jnp.float32)
    block_imag = jnp.einsum(
        "oik,jk->oij", operators[0], peram_imag, preferred_element_type=jnp.float32
    ) + jnp.einsum("oik,jk->oij", operators[1], peram_real, preferred_element_type=jnp.float32)
    blocks = jnp.stack([block_real, block_imag], axis=1).astype(jnp.bfloat16)
    requested = lax.all_gather(diagram_lists, "sa", axis=1, tiled=True)
    owner_count = lax.axis_size("sa")
    holder = lax.axis_index("sa")
    requested = requested[0].reshape(owner_count, 2 * pair_count)
    local_mask = requested // ops_count == holder
    slot_rank = jnp.cumsum(local_mask.astype(jnp.int32), axis=1) - 1
    chooser = local_mask[:, None, :] & (
        slot_rank[:, None, :] == jnp.arange(CAP, dtype=jnp.int32)[None, :, None]
    )
    slot_ops = jnp.sum(jnp.where(chooser, (requested % ops_count)[:, None, :], 0), axis=2)
    outgoing = jnp.take(blocks, slot_ops.reshape(-1), axis=0).reshape(
        owner_count, CAP, 2, eig_count, eig_count
    )
    incoming = lax.all_to_all(outgoing, "sa", split_axis=0, concat_axis=0, tiled=True)
    positions = jnp.arange(2 * pair_count, dtype=jnp.int32)
    earlier = jnp.sum(
        (
            (spin_ids[None, :] == spin_ids[:, None]) & (positions[None, :] < positions[:, None])
        ).astype(jnp.int32),
        axis=1,
    )
    flat_slots = incoming.reshape(owner_count * CAP, 2, eig_count, eig_count)
    factors = jnp.take(flat_slots, spin_ids * CAP + earlier, axis=0)
    paired = factors.reshape(pair_count, 2, 2, eig_count, eig_count)
    left_real = paired[:, 0, 0]
    left_imag = paired[:, 0, 1]
    right_real = paired[:, 1, 0]
    right_imag = paired[:, 1, 1]
    real_sum = contract(left_real, right_real) - contract(left_imag, right_imag)
    imag_sum = contract(left_real, right_imag) + contract(left_imag, right_real)
    normalizer = 1.0 / jnp.sqrt(jnp.float32(2 * eig_count * pair_count))
    return (jnp.stack([real_sum, imag_sum]) * normalizer)[:, None, None]


def solution(mesh):
    in_specs = (
        P(None, None, "sa", "ta", None),
        P(None, None, "ta", None, None),
        P("ta", "sa", None),
    )
    out_specs = P(None, "ta", "sa", None, None)
    return jax.shard_map(body, mesh=mesh, in_specs=in_specs, out_specs=out_specs, check_vma=False)
```

profile of v0, /device:TPU:1, one launch (start us, length us, event | category | flops | bytes accessed | tf_op | source)
XLA Modules:
  0.0 517.9 jit_solution(5601614755968271136)
XLA Ops:
  0.0 1.9 copy.30
  1.9 7.6 %all-to-all-start = ((bf16[2,16,1,24,384]{4,3,2,0,1:T(8,128)(2,1)}), bf16[2,16,1,24,384]{4,3,2,0,1:T(8,128)(2,1)S(1)}, u32[]{:S(2)}, u32[]{:S(2)}) async-start(bf16[2,16,1,24,384]{4,3,2,0,1:T(8,128)(2,1)} %copy.30), calls=%async_computation | async-start | bytes 1179648 | tf_op jit(solution)/shard_map/all_to_all | solution.py:16
  9.5 0.8 copy.27
  10.3 20.9 %all_gather.3 = s32[1,128,2]{2,0,1:T(1,128)S(1)} all-gather(s32[1,8,2]{2,0,1:T(1,128)S(1)} %copy.27), channel_id=1, replica_groups=mesh['ta'=16,'sa'=16] {'sa'}, dimensions={1}, use_global_device_ids=true | all-gather | bytes 1088 | tf_op jit(solution)/shard_map/all_gather | solution.py:32
  31.2 0.6 broadcast.345
  31.8 0.8 reduce.3
  32.6 0.1 reshape_squeeze.12
  32.7 0.2 reduce_window_sum.11
  32.9 0.1 select_reduce_fusion
  33.0 0.1 copy.32
  33.1 0.1 reshape.311
  33.2 0.1 copy.28
  33.3 0.0 all-to-all-done
  33.4 0.0 copy-start
  33.4 0.1 fusion.25
  33.4 3.4 fusion.3
  36.9 0.0 copy-done
  36.9 1.6 fusion.2
  38.5 1.6 fusion
  40.1 1.6 fusion.1
  41.7 2.7 pad_maximum_fusion
  44.4 10.7 %gather_fusion = bf16[32,2,384,384]{3,2,1,0:T(8,128)(2,1)} fusion(bf16[8,2,384,384]{3,2,0,1:T(8,128)(2,1)} %pad_maximum_fusion, s32[1024]{0:T(1024)S(1)} %pad_clamp_fusion.1), kind=kCustom, calls=%fused_computation | custom fusion | bytes 37748864 | tf_op jit(solution)/shard_map/jit(_take)/gather | solution.py:42
  55.1 17.1 %broadcast_select_fusion = bf16[16,2,2,384,384]{4,3,2,1,0:T(8,128)(2,1)} fusion(bf16[16,2,2,384,384]{4,3,2,1,0:T(8,128)(2,1)} %bitcast.114, pred[16,2]{1,0:T(8,128)(4,1)S(1)} %copy.28), kind=kLoop, calls=%fused_computation.2 | loop fusion | flops 9437184 | bytes 37748768 | tf_op jit(solution)/shard_map/jit(_take)/select_n | solution.py:42
  72.1 0.0 copy-start.2
  72.1 5.5 %all-to-all-start.1 = ((bf16[16,2,2,384,384]{4,3,2,1,0:T(8,128)(2,1)}), bf16[16,2,2,384,384]{4,3,2,1,0:T(8,128)(2,1)}, u32[]{:S(2)}, u32[]{:S(2)}) async-start(bf16[16,2,2,384,384]{4,3,2,1,0:T(8,128)(2,1)} %broadcast_select_fusion), calls=%async_computation.1 | async-start | bytes 37748736 | tf_op jit(solution)/shard_map/all_to_all | solution.py:45
  77.6 0.0 copy-done.2
  77.6 0.1 copy.25
  77.7 0.1 reshape_squeeze.11
  77.8 0.1 reshape_squeeze.13
  77.9 0.2 convert_reduce_fusion
  78.1 0.1 reduce_sum.23
  78.1 0.1 copy.26
  78.3 407.3 %all-to-all-done.1 = bf16[16,2,2,384,384]{4,3,2,1,0:T(8,128)(2,1)} async-done(((bf16[16,2,2,384,384]{4,3,2,1,0:T(8,128)(2,1)}), bf16[16,2,2,384,384]{4,3,2,1,0:T(8,128)(2,1)}, u32[]{:S(2)}, u32[]{:S(2)}) %all-to-all-start.1) | async-done | bytes 18874400 | tf_op jit(solution)/shard_map/all_to_all | solution.py:45
  485.6 12.1 %gather_fusion.1 = bf16[16,2,384,384]{3,2,1,0:T(8,128)(2,1)} fusion(bf16[32,2,384,384]{3,2,1,0:T(8,128)(2,1)} %bitcast.15, s32[1024]{0:T(1024)S(1)} %pad_clamp_fusion), kind=kCustom, calls=%fused_computation.1 | custom fusion | bytes 18874432 | tf_op jit(solution)/shard_map/jit(_take)/gather | solution.py:54
  497.7 8.5 %copy_select_fusion = bf16[8,2,2,384,384]{4,3,0,2,1:T(8,128)(2,1)} fusion(bf16[8,2,2,384,384]{4,3,2,1,0:T(8,128)(2,1)} %bitcast.115, pred[8,2]{0,1:T(4,128)(4,1)S(1)} %compare_and_fusion.1), kind=kLoop, calls=%fused_computation.3 | loop fusion | flops 4718592 | bytes 18874384 | tf_op jit(solution)/shard_map/jit(_take)/select_n | solution.py:54
  506.1 0.0 copy-start.1
  506.2 3.9 fusion.8
  510.1 3.9 fusion.9
  514.0 0.0 copy-done.1
  514.0 1.4 fusion.15
  515.4 1.4 fusion.13
  516.8 1.1 maximum_multiply_fusion
  (9 shorter events, 0.1 us)
Async XLA Ops:
  1.9 31.4 %all-to-all-start = ((bf16[2,16,1,24,384]{4,3,2,0,1:T(8,128)(2,1)}), bf16[2,16,1,24,384]{4,3,2,0,1:T(8,128)(2,1)S(1)}, u32[]{:S(2)}, u32[]{:S(2)}) async-start(bf16[2,16,1,24,384]{4,3,2,0,1:T(8,128)(2,1)} %copy.30), calls=%async_computation | async-start | bytes 1179648 | tf_op jit(solution)/shard_map/all_to_all | solution.py:16
  33.4 3.5 copy-start
  72.1 5.5 %copy-start.2 = (s32[1,8,2]{1,2,0:T(2,128)S(1)}, s32[1,8,2]{1,2,0:T(2,128)}, u32[]{:S(2)}) copy-start(s32[1,8,2]{1,2,0:T(2,128)} %param.5) | copy-start | bytes 196
  72.1 413.5 %all-to-all-start.1 = ((bf16[16,2,2,384,384]{4,3,2,1,0:T(8,128)(2,1)}), bf16[16,2,2,384,384]{4,3,2,1,0:T(8,128)(2,1)}, u32[]{:S(2)}, u32[]{:S(2)}) async-start(bf16[16,2,2,384,384]{4,3,2,1,0:T(8,128)(2,1)} %broadcast_select_fusion), calls=%async_computation.1 | async-start | bytes 37748736 | tf_op jit(solution)/shard_map/all_to_all | solution.py:45
  506.1 7.9 %copy-start.1 = (bf16[8,2,2,384,384]{4,3,0,2,1:T(8,128)(2,1)S(1)}, bf16[8,2,2,384,384]{4,3,0,2,1:T(8,128)(2,1)}, u32[]{:S(2)}) copy-start(bf16[8,2,2,384,384]{4,3,0,2,1:T(8,128)(2,1)} %copy_select_fusion) | copy-start | bytes 28311556
where the time goes:
time: 518 us
  waiting for transfers between devices  407 us (79%)
  other arithmetic  30.8 us (6%)
  local copies, waits for them, and re-layouts  26.9 us (5%)
  blocking collectives  20.9 us (4%)
  matrix products  18.8 us (4%)
  starting transfers between devices  13 us (3%)
    all_to_all x1, waiting for transfers between devices, body(): lax.all_to_all(outgoing, 'sa', split_axis=0, concat_axis=0, tiled=True)  407 us
    all_gather x1, blocking collectives, body(): requested = lax.all_gather(diagram_lists, 'sa', axis=1, tiled=True)  20.9 us
    select_n x2, other arithmetic, body(): jnp.take(blocks, slot_ops.reshape(-1), axis=0)  17.1 us
    gather x1, local copies, waits for them, and re-layouts, body(): factors = jnp.take(flat_slots, spin_ids * CAP + earlier, axis=0)  12.1 us
    gather x1, local copies, waits for them, and re-layouts, body(): jnp.take(blocks, slot_ops.reshape(-1), axis=0)  10.7 us
    dot_general x4, matrix products, contract(): lax.dot_general(first, second, (((0, 2), (0, 1)), ((), ())), preferred_el...  10.6 us
  transfers between devices with their start and end apart: 2, of which 1 were waited for; matrix products, arithmetic and copies ran while one was open for 1% of the time, Pallas kernels for 0%

commit v1 on v0

v1 whole, which is shorter than its diff:
```python
import jax
import jax.numpy as jnp
from jax import lax
from jax.experimental import pallas as pl
from jax.experimental.pallas import tpu as pltpu
from jax.sharding import PartitionSpec as P


def block_step_kernel(slots, ids_ref, me_ref, ops_hbm, *refs):
    count = len(slots)
    peram_refs = refs[: 2 * count]
    out_hbm = refs[2 * count + 1]
    op_buf, weight, result, op_sem, out_sem = refs[2 * count + 2 :]
    half = op_buf.shape[-1]
    ops_count = ops_hbm.shape[1]
    sa_count = 2 * (me_ref.shape[0] * 8)
    me = me_ref[0]
    positions = out_hbm.shape[0]
    for at, (behind, other) in enumerate(slots):
        zpos = lax.rem(me // 2 - behind + sa_count // 2, sa_count // 2)
        core = lax.rem(me + other, 2)
        spin = 2 * zpos + core
        real = peram_refs[2 * at]
        imag = peram_refs[2 * at + 1]
        weight[:half, :half] = real[...]
        weight[:half, half:] = -imag[...]
        weight[half:, :half] = imag[...]
        weight[half:, half:] = real[...]

        def one(q, carry):
            ident = ids_ref[q]

            @pl.when(ident // ops_count == spin)
            def _():
                op = lax.rem(ident, ops_count)
                loads = [
                    pltpu.make_async_copy(ops_hbm.at[part, op], op_buf.at[part], op_sem.at[part])
                    for part in range(2)
                ]
                for load in loads:
                    load.start()
                for load in loads:
                    load.wait()
                left = jnp.concatenate([op_buf[0], op_buf[1]], axis=1)
                product = lax.dot_general(
                    left, weight[...], (((1,), (1,)), ((), ())), preferred_element_type=jnp.float32
                )
                result[0] = product[:, :half].astype(jnp.bfloat16)
                result[1] = product[:, half:].astype(jnp.bfloat16)
                store = pltpu.make_async_copy(result, out_hbm.at[q], out_sem)
                store.start()
                store.wait()

            return carry

        lax.fori_loop(0, positions, one, 0)


def block_step(slots, ids, me, ops, perams, blocks):
    count = len(slots)
    half = ops.shape[-1]
    smem = pl.BlockSpec(memory_space=pltpu.SMEM)
    vmem = pl.BlockSpec(memory_space=pltpu.VMEM)
    hbm = pl.BlockSpec(memory_space=pl.ANY)
    return pl.pallas_call(
        lambda *refs: block_step_kernel(slots, *refs),
        out_shape=jax.ShapeDtypeStruct(blocks.shape, blocks.dtype),
        in_specs=[smem, smem, hbm] + [vmem] * (2 * count) + [hbm],
        out_specs=hbm,
        scratch_shapes=[
            pltpu.VMEM((2, half, half), jnp.bfloat16),
            pltpu.VMEM((2 * half, 2 * half), jnp.bfloat16),
            pltpu.VMEM((2, half, half), jnp.bfloat16),
            pltpu.SemaphoreType.DMA((2,)),
            pltpu.SemaphoreType.DMA,
        ],
        input_output_aliases={3 + 2 * count: 0},
        name="block_step",
    )(ids, me, ops, *perams, blocks)


def pair_kernel(blocks_ref, out_ref, right):
    pair = pl.program_id(0)
    half = out_ref.shape[-1]
    right[:half, :half] = blocks_ref[1, 0]
    right[:half, half:] = blocks_ref[1, 1]
    right[half:, :half] = -blocks_ref[1, 1]
    right[half:, half:] = blocks_ref[1, 0]
    left = jnp.concatenate([blocks_ref[0, 0], blocks_ref[0, 1]], axis=1)
    product = lax.dot_general(
        left, right[...], (((1,), (0,)), ((), ())), preferred_element_type=jnp.float32
    )

    @pl.when(pair == 0)
    def _():
        out_ref[0] = product[:, :half]
        out_ref[1] = product[:, half:]

    @pl.when(pair > 0)
    def _():
        out_ref[0] += product[:, :half]
        out_ref[1] += product[:, half:]

    @pl.when(pair == pl.num_programs(0) - 1)
    def _():
        pairs = pl.num_programs(0)
        scale = 1.0 / jnp.sqrt(jnp.float32(2 * half * 8))
        out_ref[...] = out_ref[...] * scale


def pair_sum(blocks):
    half = blocks.shape[-1]
    pairs = blocks.shape[0] // 2
    return pl.pallas_call(
        pair_kernel,
        out_shape=jax.ShapeDtypeStruct((2, half, half), jnp.float32),
        grid=(pairs,),
        in_specs=[pl.BlockSpec((2, 2, half, half), lambda p: (p, 0, 0, 0))],
        out_specs=pl.BlockSpec((2, half, half), lambda p: (0, 0, 0)),
        scratch_shapes=[pltpu.VMEM((2 * half, 2 * half), jnp.bfloat16)],
        name="pair_sum",
    )(blocks)


def uninitialised(shape, dtype):
    return pl.pallas_call(
        lambda out: None,
        out_shape=jax.ShapeDtypeStruct(shape, dtype),
        out_specs=pl.BlockSpec(memory_space=pl.ANY),
        name="block_room",
    )()


def body(perambulator, meson_ops, diagram_lists):
    eig_count = perambulator.shape[-1]
    sa_count = lax.axis_size("sa")
    ring = sa_count // 2

    def owned(part):
        sent = perambulator[part, :, 0]
        got = lax.all_to_all(sent, "ta", split_axis=0, concat_axis=0, tiled=True)
        return got.reshape(eig_count, eig_count)

    def hop(value, step):
        return lax.ppermute(value, "sa", [(i, (i + 2 * step) % sa_count) for i in range(sa_count)])

    def swap(value):
        return lax.ppermute(value, "sa", [(i, i ^ 1) for i in range(sa_count)])

    ids = diagram_lists.reshape(-1)
    me = lax.axis_index("sa").astype(jnp.int32).reshape(1)
    ops = meson_ops[:, :, 0]
    real, imag = owned(0), owned(1)
    far = ring // 2
    reals = {0: real}
    imags = {0: imag}
    up = down = real
    iup = idown = imag
    for d in range(1, far + 1):
        up = hop(up, 1)
        reals[d] = up
        if d < far:
            down = hop(down, -1)
            reals[ring - d] = down
            iup = hop(iup, 1)
            imags[d] = iup
        idown = hop(idown, -1)
        imags[(ring - d) % ring] = idown
    blocks = uninitialised((ids.shape[0], 2, eig_count, eig_count), jnp.bfloat16)
    for d in range(far + 1):
        where = [d] if d in (0, far) else [d, ring - d]
        slots, perams = [], []
        for behind in where:
            slots += [(behind, 0), (behind, 1)]
            perams += [reals[behind], imags[behind], swap(reals[behind]), swap(imags[behind])]
        blocks = block_step(slots, ids, me, ops, perams, blocks)
    return pair_sum(blocks)[:, None, None]


def solution(mesh):
    in_specs = (
        P(None, None, "sa", "ta", None),
        P(None, None, "ta", None, None),
        P("ta", "sa", None),
    )
    out_specs = P(None, "ta", "sa", None, None)
    return jax.shard_map(body, mesh=mesh, in_specs=in_specs, out_specs=out_specs, check_vma=False)
```

time: 518 us -> 152 us (0.29)
  waiting for transfers between devices: 407 us -> 20.8 us
  Pallas kernels: 0 us -> 62.8 us
  starting transfers between devices: 13 us -> 48.7 us
  other arithmetic: 30.8 us -> 0 us
  local copies, waits for them, and re-layouts: 26.9 us -> 2.67 us
  matrix products: 18.8 us -> 0 us
  blocking collectives: 20.9 us -> 15.5 us
    all_to_all x2 -> x1, waiting for transfers between devices: 407 us -> 4.31 us  [owned(): got = lax.all_to_all(sent, 'ta', split_axis=0, concat_axis=0, tiled=True)]
    pallas_call x0 -> x7, Pallas kernels: none -> 62.8 us  [the longest x5 52.6 us: block_step(): pl.pallas_call(lambda *refs: block_step_kernel(slots, *refs), out_shape=j...]
    ppermute x0 -> x30, starting transfers between devices: none -> 45.2 us  [the longest x14 23.9 us: hop(): lax.ppermute(value, 'sa', [(i, (i + 2 * step) % sa_count) for i in range(...]
    select_n x6 -> x0, other arithmetic: 25.6 us -> none  [the longest x2 17.1 us: body(): jnp.take(blocks, slot_ops.reshape(-1), axis=0)]
    gather x2 -> x0, local copies, waits for them, and re-layouts: 22.8 us -> none  [the longest x1 12.1 us: body(): factors = jnp.take(flat_slots, spin_ids * CAP + earlier, axis=0)]
    all_gather x1 -> x0, blocking collectives: 20.9 us -> none  [body(): requested = lax.all_gather(diagram_lists, 'sa', axis=1, tiled=True)]
    dot_general x8 -> x0, matrix products: 18.8 us -> none  [the longest x4 10.6 us: contract(): lax.dot_general(first, second, (((0, 2), (0, 1)), ((), ())), preferred_el...]
    ppermute x0 -> x30, waiting for transfers between devices: none -> 16.4 us  [the longest x14 16.4 us: hop(): lax.ppermute(value, 'sa', [(i, (i + 2 * step) % sa_count) for i in range(...]
  transfers between devices with their start and end apart: 2 -> 31, of which waited for: 1 -> 12; matrix products, arithmetic and copies ran while one was open for 1% -> 0% of each run, Pallas kernels for 0% -> 33%
where the time goes in v1:
time: 152 us; the launch traced here: 151 us
  Pallas kernels  62.8 us (41%)
  starting transfers between devices  48.7 us (32%)
  waiting for transfers between devices  20.8 us (14%)
  blocking collectives  15.5 us (10%)
  local copies, waits for them, and re-layouts  2.67 us (2%)
    pallas_call x5, Pallas kernels, block_step(): pl.pallas_call(lambda *refs: block_step_kernel(slots, *refs), out_shape=j...  52.6 us
    ppermute x14, starting transfers between devices, hop(): lax.ppermute(value, 'sa', [(i, (i + 2 * step) % sa_count) for i in range(...  23.9 us
    ppermute x16, starting transfers between devices, swap(): return lax.ppermute(value, 'sa', [(i, i ^ 1) for i in range(sa_count)])  21.3 us
    ppermute x14, waiting for transfers between devices, hop(): lax.ppermute(value, 'sa', [(i, (i + 2 * step) % sa_count) for i in range(...  16.4 us
    all_to_all x1, blocking collectives, owned(): got = lax.all_to_all(sent, 'ta', split_axis=0, concat_axis=0, tiled=True)  15.5 us
    pallas_call x1, Pallas kernels, pair_sum(): pl.pallas_call(pair_kernel, out_shape=jax.ShapeDtypeStruct((2, half, half...  10.2 us
    all_to_all x1, waiting for transfers between devices, owned(): got = lax.all_to_all(sent, 'ta', split_axis=0, concat_axis=0, tiled=True)  4.31 us
    all_to_all x1, starting transfers between devices, owned(): got = lax.all_to_all(sent, 'ta', split_axis=0, concat_axis=0, tiled=True)  3.54 us
  transfers between devices with their start and end apart: 31, of which 12 were waited for; matrix products, arithmetic and copies ran while one was open for 0% of the time, Pallas kernels for 33%

profile of v1, /device:TPU:1, one launch (start us, length us, event | category | flops | bytes accessed | tf_op | source)
XLA Modules:
  0.0 150.8 jit_solution(5801730911182509219)
XLA Ops:
  0.0 1.8 %slice_bitcast_fusion = (bf16[16,24,384]{2,1,0:T(8,128)(2,1)}, bf16[16,24,384]{2,1,0:T(8,128)(2,1)S(1)}) fusion(bf16[2,16,1,24,384]{4,3,2,1,0:T(8,128)(2,1)} %param.3), kind=kLoop, calls=%fused_computation | loop fusion | bytes 1179648 | tf_op jit(solution)/shard_map/squeeze | solution.py:140
  1.8 15.5 %all_to_all.10 = bf16[16,24,384]{2,1,0:T(8,128)(2,1)S(1)} all-to-all(bf16[16,24,384]{2,1,0:T(8,128)(2,1)S(1)} %get-tuple-element.6), channel_id=1, replica_groups=mesh['ta'=16,'sa'=16] {'ta'}, dimensions={0} | all-to-all | bytes 589824 | tf_op jit(solution)/shard_map/all_to_all | solution.py:141
  17.4 3.5 %all-to-all-start.1 = ((bf16[16,24,384]{2,1,0:T(8,128)(2,1)}), bf16[16,24,384]{2,1,0:T(8,128)(2,1)S(1)}, u32[]{:S(2)}, u32[]{:S(2)}) async-start(bf16[16,24,384]{2,1,0:T(8,128)(2,1)} %get-tuple-element.5), calls=%async_computation.1 | async-start | bytes 589824 | tf_op jit(solution)/shard_map/all_to_all | solution.py:141
  20.9 1.9 %collective-permute-start.28 = (bf16[384,384]{1,0:T(8,128)(2,1)S(1)}, bf16[384,384]{1,0:T(8,128)(2,1)S(1)}, u32[]{:S(2)}, u32[]{:S(2)}) collective-permute-start(bf16[384,384]{1,0:T(8,128)(2,1)S(1)} %bitcast.16), channel_id=1, source_target_pairs={{0,1},{1,0},{2,3},{3,2},{4,5},{5,4},{6,7},{7,6},{8,9},{9,8},{10,11... | collective-permute-start | bytes 884744 | tf_op jit(solution)/shard_map/ppermute | solution.py:148
  22.8 1.6 %collective-permute-start = (bf16[384,384]{1,0:T(8,128)(2,1)S(1)}, bf16[384,384]{1,0:T(8,128)(2,1)S(1)}, u32[]{:S(2)}, u32[]{:S(2)}) collective-permute-start(bf16[384,384]{1,0:T(8,128)(2,1)S(1)} %bitcast.17), channel_id=1, source_target_pairs={{0,2},{1,3},{2,4},{3,5},{4,6},{5,7},{6,8},{7,9},{8,10},{9,11},{10,... | collective-permute-start | bytes 884744 | tf_op jit(solution)/shard_map/ppermute | solution.py:145
  24.5 4.3 %all-to-all-done.1 = bf16[16,24,384]{2,1,0:T(8,128)(2,1)S(1)} async-done(((bf16[16,24,384]{2,1,0:T(8,128)(2,1)}), bf16[16,24,384]{2,1,0:T(8,128)(2,1)S(1)}, u32[]{:S(2)}, u32[]{:S(2)}) %all-to-all-start.1) | async-done | bytes 294944 | tf_op jit(solution)/shard_map/all_to_all | solution.py:141
  28.8 1.6 %collective-permute-start.10 = (bf16[384,384]{1,0:T(8,128)(2,1)S(1)}, bf16[384,384]{1,0:T(8,128)(2,1)S(1)}, u32[]{:S(2)}, u32[]{:S(2)}) collective-permute-start(bf16[384,384]{1,0:T(8,128)(2,1)S(1)} %bitcast.20), channel_id=1, source_target_pairs={{0,2},{1,3},{2,4},{3,5},{4,6},{5,7},{6,8},{7,9},{8,10},{9,11},{10,... | collective-permute-start | bytes 884744 | tf_op jit(solution)/shard_map/ppermute | solution.py:145
  30.4 3.9 %collective-permute-start.15 = (bf16[384,384]{1,0:T(8,128)(2,1)S(1)}, bf16[384,384]{1,0:T(8,128)(2,1)S(1)}, u32[]{:S(2)}, u32[]{:S(2)}) collective-permute-start(bf16[384,384]{1,0:T(8,128)(2,1)S(1)} %bitcast.18), channel_id=1, source_target_pairs={{0,14},{1,15},{2,0},{3,1},{4,2},{5,3},{6,4},{7,5},{8,6},{9,7},{10,... | collective-permute-start | bytes 884744 | tf_op jit(solution)/shard_map/ppermute | solution.py:145
  34.4 3.1 %collective-permute-start.29 = (bf16[384,384]{1,0:T(8,128)(2,1)S(1)}, bf16[384,384]{1,0:T(8,128)(2,1)S(1)}, u32[]{:S(2)}, u32[]{:S(2)}) collective-permute-start(bf16[384,384]{1,0:T(8,128)(2,1)S(1)} %bitcast.21), channel_id=1, source_target_pairs={{0,1},{1,0},{2,3},{3,2},{4,5},{5,4},{6,7},{7,6},{8,9},{9,8},{10,11... | collective-permute-start | bytes 884744 | tf_op jit(solution)/shard_map/ppermute | solution.py:148
  37.4 1.7 %collective-permute-start.4 = (bf16[384,384]{1,0:T(8,128)(2,1)S(1)}, bf16[384,384]{1,0:T(8,128)(2,1)S(1)}, u32[]{:S(2)}, u32[]{:S(2)}) collective-permute-start(bf16[384,384]{1,0:T(8,128)(2,1)S(1)} %bitcast.22), channel_id=1, source_target_pairs={{0,14},{1,15},{2,0},{3,1},{4,2},{5,3},{6,4},{7,5},{8,6},{9,7},{10,... | collective-permute-start | bytes 884744 | tf_op jit(solution)/shard_map/ppermute | solution.py:145
  39.2 0.4 collective-permute-start.24
  39.5 0.1 collective-permute-done.10.refs_4_
  39.7 3.0 %collective-permute-start.25 = (bf16[384,384]{1,0:T(8,128)(2,1)S(1)}, bf16[384,384]{1,0:T(8,128)(2,1)S(1)}, u32[]{:S(2)}, u32[]{:S(2)}) collective-permute-start(bf16[384,384]{1,0:T(8,128)(2,1)S(1)} %collective-permute-done.10.refs_4_), channel_id=1, source_target_pairs={{0,1},{1,0},{2,3},{3,2},{4,5},{5,4},{6,7},{7,6},{8,9},{9,8},{10,11... | collective-permute-start | bytes 884744 | tf_op jit(solution)/shard_map/ppermute | solution.py:148
  42.7 0.6 collective-permute-start.26
  43.3 1.6 %collective-permute-start.1 = (bf16[384,384]{1,0:T(8,128)(2,1)S(1)}, bf16[384,384]{1,0:T(8,128)(2,1)S(1)}, u32[]{:S(2)}, u32[]{:S(2)}) collective-permute-start(bf16[384,384]{1,0:T(8,128)(2,1)S(1)} %collective-permute-done.refs_3_), channel_id=1, source_target_pairs={{0,2},{1,3},{2,4},{3,5},{4,6},{5,7},{6,8},{7,9},{8,10},{9,11},{10,... | collective-permute-start | bytes 884744 | tf_op jit(solution)/shard_map/ppermute | solution.py:145
  44.8 1.2 collective-permute-done.4.refs_8_
  46.0 1.7 %collective-permute-start.11 = (bf16[384,384]{1,0:T(8,128)(2,1)S(1)}, bf16[384,384]{1,0:T(8,128)(2,1)S(1)}, u32[]{:S(2)}, u32[]{:S(2)}) collective-permute-start(bf16[384,384]{1,0:T(8,128)(2,1)S(1)} %collective-permute-done.10.refs_4_), channel_id=1, source_target_pairs={{0,2},{1,3},{2,4},{3,5},{4,6},{5,7},{6,8},{7,9},{8,10},{9,11},{10,... | collective-permute-start | bytes 884744 | tf_op jit(solution)/shard_map/ppermute | solution.py:145
  47.7 1.8 %collective-permute-start.16 = (bf16[384,384]{1,0:T(8,128)(2,1)S(1)}, bf16[384,384]{1,0:T(8,128)(2,1)S(1)}, u32[]{:S(2)}, u32[]{:S(2)}) collective-permute-start(bf16[384,384]{1,0:T(8,128)(2,1)S(1)} %collective-permute-done.15.refs_7_), channel_id=1, source_target_pairs={{0,14},{1,15},{2,0},{3,1},{4,2},{5,3},{6,4},{7,5},{8,6},{9,7},{10,... | collective-permute-start | bytes 884744 | tf_op jit(solution)/shard_map/ppermute | solution.py:145
  49.5 2.3 %collective-permute-start.27 = (bf16[384,384]{1,0:T(8,128)(2,1)S(1)}, bf16[384,384]{1,0:T(8,128)(2,1)S(1)}, u32[]{:S(2)}, u32[]{:S(2)}) collective-permute-start(bf16[384,384]{1,0:T(8,128)(2,1)S(1)} %collective-permute-done.4.refs_8_), channel_id=1, source_target_pairs={{0,1},{1,0},{2,3},{3,2},{4,5},{5,4},{6,7},{7,6},{8,9},{9,8},{10,11... | collective-permute-start | bytes 884744 | tf_op jit(solution)/shard_map/ppermute | solution.py:148
  51.8 1.7 %collective-permute-start.5 = (bf16[384,384]{1,0:T(8,128)(2,1)S(1)}, bf16[384,384]{1,0:T(8,128)(2,1)S(1)}, u32[]{:S(2)}, u32[]{:S(2)}) collective-permute-start(bf16[384,384]{1,0:T(8,128)(2,1)S(1)} %collective-permute-done.4.refs_8_), channel_id=1, source_target_pairs={{0,14},{1,15},{2,0},{3,1},{4,2},{5,3},{6,4},{7,5},{8,6},{9,7},{10,... | collective-permute-start | bytes 884744 | tf_op jit(solution)/shard_map/ppermute | solution.py:145
  53.4 0.5 collective-permute-done.1.refs_3_
  54.0 0.9 collective-permute-start.20
  54.9 5.4 %collective-permute-done.11.refs_4_ = bf16[384,384]{1,0:T(8,128)(2,1)S(1)} collective-permute-done((bf16[384,384]{1,0:T(8,128)(2,1)S(1)}, bf16[384,384]{1,0:T(8,128)(2,1)S(1)}, u32[]{:S(2)}, u32[]{:S(2)}) %collective-permute-start.11) | collective-permute-done | bytes 294944 | tf_op jit(solution)/shard_map/ppermute | solution.py:145
  60.3 0.7 collective-permute-start.21
  61.1 1.1 collective-permute-start.2
  62.1 1.5 collective-permute-done.5.refs_8_
  63.6 1.2 collective-permute-start.23
  64.8 1.6 %collective-permute-start.6 = (bf16[384,384]{1,0:T(8,128)(2,1)S(1)}, bf16[384,384]{1,0:T(8,128)(2,1)}, u32[]{:S(2)}, u32[]{:S(2)}) collective-permute-start(bf16[384,384]{1,0:T(8,128)(2,1)S(1)} %collective-permute-done.5.refs_8_), channel_id=1, source_target_pairs={{0,14},{1,15},{2,0},{3,1},{4,2},{5,3},{6,4},{7,5},{8,6},{9,7},{10,... | collective-permute-start | bytes 884744 | tf_op jit(solution)/shard_map/ppermute | solution.py:145
  66.5 2.7 %collective-permute-start.17 = (bf16[384,384]{1,0:T(8,128)(2,1)S(1)}, bf16[384,384]{1,0:T(8,128)(2,1)}, u32[]{:S(2)}, u32[]{:S(2)}) collective-permute-start(bf16[384,384]{1,0:T(8,128)(2,1)S(1)} %collective-permute-done.16.refs_7_), channel_id=1, source_target_pairs={{0,14},{1,15},{2,0},{3,1},{4,2},{5,3},{6,4},{7,5},{8,6},{9,7},{10,... | collective-permute-start | bytes 884744 | tf_op jit(solution)/shard_map/ppermute | solution.py:145
  69.2 1.6 %collective-permute-done.2.refs_3_ = bf16[384,384]{1,0:T(8,128)(2,1)S(1)} collective-permute-done((bf16[384,384]{1,0:T(8,128)(2,1)S(1)}, bf16[384,384]{1,0:T(8,128)(2,1)S(1)}, u32[]{:S(2)}, u32[]{:S(2)}) %collective-permute-start.2) | collective-permute-done | bytes 294944 | tf_op jit(solution)/shard_map/ppermute | solution.py:145
  70.8 1.8 %collective-permute-start.13 = (bf16[384,384]{1,0:T(8,128)(2,1)S(1)}, bf16[384,384]{1,0:T(8,128)(2,1)S(1)}, u32[]{:S(2)}, u32[]{:S(2)}) collective-permute-start(bf16[384,384]{1,0:T(8,128)(2,1)S(1)} %collective-permute-done.2.refs_3_), channel_id=1, source_target_pairs={{0,1},{1,0},{2,3},{3,2},{4,5},{5,4},{6,7},{7,6},{8,9},{9,8},{10,11... | collective-permute-start | bytes 884744 | tf_op jit(solution)/shard_map/ppermute | solution.py:148
  72.6 0.8 collective-permute-done.6.refs_8_
  73.4 2.8 %collective-permute-start.7 = (bf16[384,384]{1,0:T(8,128)(2,1)}, bf16[384,384]{1,0:T(8,128)(2,1)}, u32[]{:S(2)}, u32[]{:S(2)}) collective-permute-start(bf16[384,384]{1,0:T(8,128)(2,1)} %collective-permute-done.6.refs_8_), channel_id=1, source_target_pairs={{0,14},{1,15},{2,0},{3,1},{4,2},{5,3},{6,4},{7,5},{8,6},{9,7},{10,... | collective-permute-start | bytes 884744 | tf_op jit(solution)/shard_map/ppermute | solution.py:145
  76.3 0.9 collective-permute-done.12.refs_4_
  77.2 1.8 %collective-permute-start.19 = (bf16[384,384]{1,0:T(8,128)(2,1)}, bf16[384,384]{1,0:T(8,128)(2,1)}, u32[]{:S(2)}, u32[]{:S(2)}) collective-permute-start(bf16[384,384]{1,0:T(8,128)(2,1)} %collective-permute-done.6.refs_8_), channel_id=1, source_target_pairs={{0,1},{1,0},{2,3},{3,2},{4,5},{5,4},{6,7},{7,6},{8,9},{9,8},{10,11... | collective-permute-start | bytes 884744 | tf_op jit(solution)/shard_map/ppermute | solution.py:148
  79.0 0.7 collective-permute-done.17.refs_7_
  79.7 1.5 collective-permute-start.14
  81.4 2.2 %collective-permute-done.3.refs_3_ = bf16[384,384]{1,0:T(8,128)(2,1)} collective-permute-done((bf16[384,384]{1,0:T(8,128)(2,1)S(1)}, bf16[384,384]{1,0:T(8,128)(2,1)}, u32[]{:S(2)}, u32[]{:S(2)}) %collective-permute-start.3) | collective-permute-done | bytes 294944 | tf_op jit(solution)/shard_map/ppermute | solution.py:145
  83.5 1.1 collective-permute-start.8
  84.6 1.4 collective-permute-done.7.refs_4_
  86.1 0.9 collective-permute-start.9
  87.1 0.7 reshape.12.refs_0_
  87.8 2.1 %block_step.5.refs_11_ = bf16[16,2,384,384]{3,2,1,0:T(8,128)(2,1)} custom-call(s32[16]{0:T(128)} %reshape.12.refs_0_, s32[1]{0:T(128)} %bitcast.refs_1_, bf16[2,8,384,384]{3,2,1,0:T(8,128)(2,1)} %bitcast.11, bf16[384,384]{1,0:T(8,128)(2,1)} %bitcast.19, bf16[384,384]{1,0:T(8,128)(2,1)} %bitcast.23, ...), custom_call_target="tpu_custom_call", output_to_operand_aliasing={{}: (7, {})} | custom-call | tf_op jit(solution)/shard_map/block_step/pallas_call | solution.py:65
  90.0 20.6 %block_step.6.refs_11_ = bf16[16,2,384,384]{3,2,1,0:T(8,128)(2,1)} custom-call(s32[16]{0:T(128)} %reshape.12.refs_0_, s32[1]{0:T(128)} %bitcast.refs_1_, bf16[2,8,384,384]{3,2,1,0:T(8,128)(2,1)} %bitcast.12, bf16[384,384]{1,0:T(8,128)(2,1)} %copy-done.3, bf16[384,384]{1,0:T(8,128)(2,1)} %copy-done.4, ...), custom_call_target="tpu_custom_call", output_to_operand_aliasing={{}: (11, {})} | custom-call | tf_op jit(solution)/shard_map/block_step/pallas_call | solution.py:65
  110.6 12.9 %block_step.7.refs_11_ = bf16[16,2,384,384]{3,2,1,0:T(8,128)(2,1)} custom-call(s32[16]{0:T(128)} %reshape.12.refs_0_, s32[1]{0:T(128)} %bitcast.refs_1_, bf16[2,8,384,384]{3,2,1,0:T(8,128)(2,1)} %bitcast.13, bf16[384,384]{1,0:T(8,128)(2,1)} %copy-done.11, bf16[384,384]{1,0:T(8,128)(2,1)} %copy-done.12, ...), custom_call_target="tpu_custom_call", output_to_operand_aliasing={{}: (11, {})} | custom-call | tf_op jit(solution)/shard_map/block_step/pallas_call | solution.py:65
  123.5 14.9 %block_step.8.refs_7_ = bf16[16,2,384,384]{3,2,1,0:T(8,128)(2,1)} custom-call(s32[16]{0:T(128)} %reshape.12.refs_0_, s32[1]{0:T(128)} %bitcast.refs_1_, bf16[2,8,384,384]{3,2,1,0:T(8,128)(2,1)} %bitcast.14, bf16[384,384]{1,0:T(8,128)(2,1)} %copy-done.18, bf16[384,384]{1,0:T(8,128)(2,1)} %collective-permute-done.12.refs_4_, ...), custom_call_target="tpu_custom_call", output_to_operand_aliasing={{}: (11, {})} | custom-call | tf_op jit(solution)/shard_map/block_step/pallas_call | solution.py:65
  138.5 2.1 %block_step.9.blocks_ref = bf16[16,2,384,384]{3,2,1,0:T(8,128)(2,1)} custom-call(s32[16]{0:T(128)} %reshape.12.refs_0_, s32[1]{0:T(128)} %bitcast.refs_1_, bf16[2,8,384,384]{3,2,1,0:T(8,128)(2,1)} %bitcast.15, bf16[384,384]{1,0:T(8,128)(2,1)} %collective-permute-done.3.refs_3_, ...), custom_call_target="tpu_custom_call", output_to_operand_aliasing={{}: (7, {})} | custom-call | tf_op jit(solution)/shard_map/block_step/pallas_call | solution.py:65
  140.6 10.2 %pair_sum.1 = f32[2,384,384]{2,1,0:T(8,128)} custom-call(bf16[16,2,384,384]{3,2,1,0:T(8,128)(2,1)} %block_step.9.blocks_ref), custom_call_target="tpu_custom_call" | custom-call | tf_op jit(solution)/shard_map/pair_sum/pallas_call | solution.py:114
  (71 shorter events, 0.4 us)
Async XLA Ops:
  0.0 87.0 %copy-start.22 = (s32[1,8,2]{1,2,0:T(2,128)S(1)}, s32[1,8,2]{1,2,0:T(2,128)}, u32[]{:S(2)}) copy-start(s32[1,8,2]{1,2,0:T(2,128)} %param.5) | copy-start | bytes 196
  17.4 70.4 %copy-start = (bf16[16,24,384]{2,1,0:T(8,128)(2,1)}, bf16[16,24,384]{2,1,0:T(8,128)(2,1)S(1)}, u32[]{:S(2)}) copy-start(bf16[16,24,384]{2,1,0:T(8,128)(2,1)S(1)} %all_to_all.10) | copy-start | bytes 884740
  17.4 11.4 %all-to-all-start.1 = ((bf16[16,24,384]{2,1,0:T(8,128)(2,1)}), bf16[16,24,384]{2,1,0:T(8,128)(2,1)S(1)}, u32[]{:S(2)}, u32[]{:S(2)}) async-start(bf16[16,24,384]{2,1,0:T(8,128)(2,1)} %get-tuple-element.5), calls=%async_computation.1 | async-start | bytes 589824 | tf_op jit(solution)/shard_map/all_to_all | solution.py:141
  20.9 16.5 %collective-permute-start.28 = (bf16[384,384]{1,0:T(8,128)(2,1)S(1)}, bf16[384,384]{1,0:T(8,128)(2,1)S(1)}, u32[]{:S(2)}, u32[]{:S(2)}) collective-permute-start(bf16[384,384]{1,0:T(8,128)(2,1)S(1)} %bitcast.16), channel_id=1, source_target_pairs={{0,1},{1,0},{2,3},{3,2},{4,5},{5,4},{6,7},{7,6},{8,9},{9,8},{10,11... | collective-permute-start | bytes 884744 | tf_op jit(solution)/shard_map/ppermute | solution.py:148
  22.8 16.4 %collective-permute-start = (bf16[384,384]{1,0:T(8,128)(2,1)S(1)}, bf16[384,384]{1,0:T(8,128)(2,1)S(1)}, u32[]{:S(2)}, u32[]{:S(2)}) collective-permute-start(bf16[384,384]{1,0:T(8,128)(2,1)S(1)} %bitcast.17), channel_id=1, source_target_pairs={{0,2},{1,3},{2,4},{3,5},{4,6},{5,7},{6,8},{7,9},{8,10},{9,11},{10,... | collective-permute-start | bytes 884744 | tf_op jit(solution)/shard_map/ppermute | solution.py:145
  28.8 59.0 %copy-start.1 = (bf16[16,24,384]{2,1,0:T(8,128)(2,1)}, bf16[16,24,384]{2,1,0:T(8,128)(2,1)S(1)}, u32[]{:S(2)}) copy-start(bf16[16,24,384]{2,1,0:T(8,128)(2,1)S(1)} %all-to-all-done.1) | copy-start | bytes 884740
  28.8 10.9 %collective-permute-start.10 = (bf16[384,384]{1,0:T(8,128)(2,1)S(1)}, bf16[384,384]{1,0:T(8,128)(2,1)S(1)}, u32[]{:S(2)}, u32[]{:S(2)}) collective-permute-start(bf16[384,384]{1,0:T(8,128)(2,1)S(1)} %bitcast.20), channel_id=1, source_target_pairs={{0,2},{1,3},{2,4},{3,5},{4,6},{5,7},{6,8},{7,9},{8,10},{9,11},{10,... | collective-permute-start | bytes 884744 | tf_op jit(solution)/shard_map/ppermute | solution.py:145
  30.4 12.3 %collective-permute-start.15 = (bf16[384,384]{1,0:T(8,128)(2,1)S(1)}, bf16[384,384]{1,0:T(8,128)(2,1)S(1)}, u32[]{:S(2)}, u32[]{:S(2)}) collective-permute-start(bf16[384,384]{1,0:T(8,128)(2,1)S(1)} %bitcast.18), channel_id=1, source_target_pairs={{0,14},{1,15},{2,0},{3,1},{4,2},{5,3},{6,4},{7,5},{8,6},{9,7},{10,... | collective-permute-start | bytes 884744 | tf_op jit(solution)/shard_map/ppermute | solution.py:145
  34.4 8.9 %collective-permute-start.29 = (bf16[384,384]{1,0:T(8,128)(2,1)S(1)}, bf16[384,384]{1,0:T(8,128)(2,1)S(1)}, u32[]{:S(2)}, u32[]{:S(2)}) collective-permute-start(bf16[384,384]{1,0:T(8,128)(2,1)S(1)} %bitcast.21), channel_id=1, source_target_pairs={{0,1},{1,0},{2,3},{3,2},{4,5},{5,4},{6,7},{7,6},{8,9},{9,8},{10,11... | collective-permute-start | bytes 884744 | tf_op jit(solution)/shard_map/ppermute | solution.py:148
  37.4 50.4 %copy-start.2 = (bf16[384,384]{1,0:T(8,128)(2,1)}, bf16[384,384]{1,0:T(8,128)(2,1)S(1)}, u32[]{:S(2)}) copy-start(bf16[384,384]{1,0:T(8,128)(2,1)S(1)} %collective-permute-done.28.refs_5_) | copy-start | bytes 884740
  37.4 8.6 %collective-permute-start.4 = (bf16[384,384]{1,0:T(8,128)(2,1)S(1)}, bf16[384,384]{1,0:T(8,128)(2,1)S(1)}, u32[]{:S(2)}, u32[]{:S(2)}) collective-permute-start(bf16[384,384]{1,0:T(8,128)(2,1)S(1)} %bitcast.22), channel_id=1, source_target_pairs={{0,14},{1,15},{2,0},{3,1},{4,2},{5,3},{6,4},{7,5},{8,6},{9,7},{10,... | collective-permute-start | bytes 884744 | tf_op jit(solution)/shard_map/ppermute | solution.py:145
  39.2 50.7 %copy-start.3 = (bf16[384,384]{1,0:T(8,128)(2,1)}, bf16[384,384]{1,0:T(8,128)(2,1)S(1)}, u32[]{:S(2)}) copy-start(bf16[384,384]{1,0:T(8,128)(2,1)S(1)} %collective-permute-done.refs_3_) | copy-start | bytes 884740
  39.2 8.5 %collective-permute-start.24 = (bf16[384,384]{1,0:T(8,128)(2,1)S(1)}, bf16[384,384]{1,0:T(8,128)(2,1)S(1)}, u32[]{:S(2)}, u32[]{:S(2)}) collective-permute-start(bf16[384,384]{1,0:T(8,128)(2,1)S(1)} %collective-permute-done.refs_3_), channel_id=1, source_target_pairs={{0,1},{1,0},{2,3},{3,2},{4,5},{5,4},{6,7},{7,6},{8,9},{9,8},{10,11... | collective-permute-start | bytes 884744 | tf_op jit(solution)/shard_map/ppermute | solution.py:148
  39.7 50.2 %copy-start.4 = (bf16[384,384]{1,0:T(8,128)(2,1)}, bf16[384,384]{1,0:T(8,128)(2,1)S(1)}, u32[]{:S(2)}) copy-start(bf16[384,384]{1,0:T(8,128)(2,1)S(1)} %collective-permute-done.10.refs_4_) | copy-start | bytes 884740
  39.7 9.8 %collective-permute-start.25 = (bf16[384,384]{1,0:T(8,128)(2,1)S(1)}, bf16[384,384]{1,0:T(8,128)(2,1)S(1)}, u32[]{:S(2)}, u32[]{:S(2)}) collective-permute-start(bf16[384,384]{1,0:T(8,128)(2,1)S(1)} %collective-permute-done.10.refs_4_), channel_id=1, source_target_pairs={{0,1},{1,0},{2,3},{3,2},{4,5},{5,4},{6,7},{7,6},{8,9},{9,8},{10,11... | collective-permute-start | bytes 884744 | tf_op jit(solution)/shard_map/ppermute | solution.py:148
  42.7 47.2 %copy-start.5 = (bf16[384,384]{1,0:T(8,128)(2,1)}, bf16[384,384]{1,0:T(8,128)(2,1)S(1)}, u32[]{:S(2)}) copy-start(bf16[384,384]{1,0:T(8,128)(2,1)S(1)} %collective-permute-done.15.refs_7_) | copy-start | bytes 884740
  42.7 9.1 %collective-permute-start.26 = (bf16[384,384]{1,0:T(8,128)(2,1)S(1)}, bf16[384,384]{1,0:T(8,128)(2,1)S(1)}, u32[]{:S(2)}, u32[]{:S(2)}) collective-permute-start(bf16[384,384]{1,0:T(8,128)(2,1)S(1)} %collective-permute-done.15.refs_7_), channel_id=1, source_target_pairs={{0,1},{1,0},{2,3},{3,2},{4,5},{5,4},{6,7},{7,6},{8,9},{9,8},{10,11... | collective-permute-start | bytes 884744 | tf_op jit(solution)/shard_map/ppermute | solution.py:148
  43.3 44.5 %copy-start.6 = (bf16[384,384]{1,0:T(8,128)(2,1)}, bf16[384,384]{1,0:T(8,128)(2,1)S(1)}, u32[]{:S(2)}) copy-start(bf16[384,384]{1,0:T(8,128)(2,1)S(1)} %collective-permute-done.29.refs_6_) | copy-start | bytes 884740
  43.3 10.7 %collective-permute-start.1 = (bf16[384,384]{1,0:T(8,128)(2,1)S(1)}, bf16[384,384]{1,0:T(8,128)(2,1)S(1)}, u32[]{:S(2)}, u32[]{:S(2)}) collective-permute-start(bf16[384,384]{1,0:T(8,128)(2,1)S(1)} %collective-permute-done.refs_3_), channel_id=1, source_target_pairs={{0,2},{1,3},{2,4},{3,5},{4,6},{5,7},{6,8},{7,9},{8,10},{9,11},{10,... | collective-permute-start | bytes 884744 | tf_op jit(solution)/shard_map/ppermute | solution.py:145
  46.0 43.9 %copy-start.7 = (bf16[384,384]{1,0:T(8,128)(2,1)}, bf16[384,384]{1,0:T(8,128)(2,1)S(1)}, u32[]{:S(2)}) copy-start(bf16[384,384]{1,0:T(8,128)(2,1)S(1)} %collective-permute-done.4.refs_8_) | copy-start | bytes 884740
  46.0 14.3 %collective-permute-start.11 = (bf16[384,384]{1,0:T(8,128)(2,1)S(1)}, bf16[384,384]{1,0:T(8,128)(2,1)S(1)}, u32[]{:S(2)}, u32[]{:S(2)}) collective-permute-start(bf16[384,384]{1,0:T(8,128)(2,1)S(1)} %collective-permute-done.10.refs_4_), channel_id=1, source_target_pairs={{0,2},{1,3},{2,4},{3,5},{4,6},{5,7},{6,8},{7,9},{8,10},{9,11},{10,... | collective-permute-start | bytes 884744 | tf_op jit(solution)/shard_map/ppermute | solution.py:145
  47.7 42.2 %copy-start.8 = (bf16[384,384]{1,0:T(8,128)(2,1)}, bf16[384,384]{1,0:T(8,128)(2,1)S(1)}, u32[]{:S(2)}) copy-start(bf16[384,384]{1,0:T(8,128)(2,1)S(1)} %collective-permute-done.24.refs_5_) | copy-start | bytes 884740
  47.7 13.3 %collective-permute-start.16 = (bf16[384,384]{1,0:T(8,128)(2,1)S(1)}, bf16[384,384]{1,0:T(8,128)(2,1)S(1)}, u32[]{:S(2)}, u32[]{:S(2)}) collective-permute-start(bf16[384,384]{1,0:T(8,128)(2,1)S(1)} %collective-permute-done.15.refs_7_), channel_id=1, source_target_pairs={{0,14},{1,15},{2,0},{3,1},{4,2},{5,3},{6,4},{7,5},{8,6},{9,7},{10,... | collective-permute-start | bytes 884744 | tf_op jit(solution)/shard_map/ppermute | solution.py:145
  49.5 40.4 %copy-start.9 = (bf16[384,384]{1,0:T(8,128)(2,1)}, bf16[384,384]{1,0:T(8,128)(2,1)S(1)}, u32[]{:S(2)}) copy-start(bf16[384,384]{1,0:T(8,128)(2,1)S(1)} %collective-permute-done.25.refs_6_) | copy-start | bytes 884740
  49.5 11.5 %collective-permute-start.27 = (bf16[384,384]{1,0:T(8,128)(2,1)S(1)}, bf16[384,384]{1,0:T(8,128)(2,1)S(1)}, u32[]{:S(2)}, u32[]{:S(2)}) collective-permute-start(bf16[384,384]{1,0:T(8,128)(2,1)S(1)} %collective-permute-done.4.refs_8_), channel_id=1, source_target_pairs={{0,1},{1,0},{2,3},{3,2},{4,5},{5,4},{6,7},{7,6},{8,9},{9,8},{10,11... | collective-permute-start | bytes 884744 | tf_op jit(solution)/shard_map/ppermute | solution.py:148
  51.8 38.2 %copy-start.10 = (bf16[384,384]{1,0:T(8,128)(2,1)}, bf16[384,384]{1,0:T(8,128)(2,1)S(1)}, u32[]{:S(2)}) copy-start(bf16[384,384]{1,0:T(8,128)(2,1)S(1)} %collective-permute-done.26.refs_9_) | copy-start | bytes 884740
  51.8 11.8 %collective-permute-start.5 = (bf16[384,384]{1,0:T(8,128)(2,1)S(1)}, bf16[384,384]{1,0:T(8,128)(2,1)S(1)}, u32[]{:S(2)}, u32[]{:S(2)}) collective-permute-start(bf16[384,384]{1,0:T(8,128)(2,1)S(1)} %collective-permute-done.4.refs_8_), channel_id=1, source_target_pairs={{0,14},{1,15},{2,0},{3,1},{4,2},{5,3},{6,4},{7,5},{8,6},{9,7},{10,... | collective-permute-start | bytes 884744 | tf_op jit(solution)/shard_map/ppermute | solution.py:145
  54.0 36.0 %copy-start.11 = (bf16[384,384]{1,0:T(8,128)(2,1)}, bf16[384,384]{1,0:T(8,128)(2,1)S(1)}, u32[]{:S(2)}) copy-start(bf16[384,384]{1,0:T(8,128)(2,1)S(1)} %collective-permute-done.1.refs_3_) | copy-start | bytes 884740
  54.0 10.9 %collective-permute-start.20 = (bf16[384,384]{1,0:T(8,128)(2,1)S(1)}, bf16[384,384]{1,0:T(8,128)(2,1)S(1)}, u32[]{:S(2)}, u32[]{:S(2)}) collective-permute-start(bf16[384,384]{1,0:T(8,128)(2,1)S(1)} %collective-permute-done.1.refs_3_), channel_id=1, source_target_pairs={{0,1},{1,0},{2,3},{3,2},{4,5},{5,4},{6,7},{7,6},{8,9},{9,8},{10,11... | collective-permute-start | bytes 884744 | tf_op jit(solution)/shard_map/ppermute | solution.py:148
  60.3 6.2 %collective-permute-start.21 = (bf16[384,384]{1,0:T(8,128)(2,1)S(1)}, bf16[384,384]{1,0:T(8,128)(2,1)S(1)}, u32[]{:S(2)}, u32[]{:S(2)}) collective-permute-start(bf16[384,384]{1,0:T(8,128)(2,1)S(1)} %collective-permute-done.11.refs_4_), channel_id=1, source_target_pairs={{0,1},{1,0},{2,3},{3,2},{4,5},{5,4},{6,7},{7,6},{8,9},{9,8},{10,11... | collective-permute-start | bytes 884744 | tf_op jit(solution)/shard_map/ppermute | solution.py:148
  61.0 5.5 %collective-permute-start.22 = (bf16[384,384]{1,0:T(8,128)(2,1)S(1)}, bf16[384,384]{1,0:T(8,128)(2,1)S(1)}, u32[]{:S(2)}, u32[]{:S(2)}) collective-permute-start(bf16[384,384]{1,0:T(8,128)(2,1)S(1)} %collective-permute-done.16.refs_7_), channel_id=1, source_target_pairs={{0,1},{1,0},{2,3},{3,2},{4,5},{5,4},{6,7},{7,6},{8,9},{9,8},{10,11... | collective-permute-start | bytes 884744 | tf_op jit(solution)/shard_map/ppermute | solution.py:148
  61.1 18.7 %copy-start.14 = (bf16[384,384]{1,0:T(8,128)(2,1)}, bf16[384,384]{1,0:T(8,128)(2,1)S(1)}, u32[]{:S(2)}) copy-start(bf16[384,384]{1,0:T(8,128)(2,1)S(1)} %collective-permute-done.27.refs_10_) | copy-start | bytes 884740
  61.1 9.7 %collective-permute-start.2 = (bf16[384,384]{1,0:T(8,128)(2,1)S(1)}, bf16[384,384]{1,0:T(8,128)(2,1)S(1)}, u32[]{:S(2)}, u32[]{:S(2)}) collective-permute-start(bf16[384,384]{1,0:T(8,128)(2,1)S(1)} %collective-permute-done.1.refs_3_), channel_id=1, source_target_pairs={{0,2},{1,3},{2,4},{3,5},{4,6},{5,7},{6,8},{7,9},{8,10},{9,11},{10,... | collective-permute-start | bytes 884744 | tf_op jit(solution)/shard_map/ppermute | solution.py:145
  63.6 17.6 %copy-start.15 = (bf16[384,384]{1,0:T(8,128)(2,1)}, bf16[384,384]{1,0:T(8,128)(2,1)S(1)}, u32[]{:S(2)}) copy-start(bf16[384,384]{1,0:T(8,128)(2,1)S(1)} %collective-permute-done.5.refs_8_) | copy-start | bytes 884740
  63.6 9.0 %collective-permute-start.23 = (bf16[384,384]{1,0:T(8,128)(2,1)S(1)}, bf16[384,384]{1,0:T(8,128)(2,1)S(1)}, u32[]{:S(2)}, u32[]{:S(2)}) collective-permute-start(bf16[384,384]{1,0:T(8,128)(2,1)S(1)} %collective-permute-done.5.refs_8_), channel_id=1, source_target_pairs={{0,1},{1,0},{2,3},{3,2},{4,5},{5,4},{6,7},{7,6},{8,9},{9,8},{10,11... | collective-permute-start | bytes 884744 | tf_op jit(solution)/shard_map/ppermute | solution.py:148
  64.8 16.4 %copy-start.16 = (bf16[384,384]{1,0:T(8,128)(2,1)}, bf16[384,384]{1,0:T(8,128)(2,1)S(1)}, u32[]{:S(2)}) copy-start(bf16[384,384]{1,0:T(8,128)(2,1)S(1)} %collective-permute-done.20.refs_5_) | copy-start | bytes 884740
  64.8 8.6 %collective-permute-start.6 = (bf16[384,384]{1,0:T(8,128)(2,1)S(1)}, bf16[384,384]{1,0:T(8,128)(2,1)}, u32[]{:S(2)}, u32[]{:S(2)}) collective-permute-start(bf16[384,384]{1,0:T(8,128)(2,1)S(1)} %collective-permute-done.5.refs_8_), channel_id=1, source_target_pairs={{0,14},{1,15},{2,0},{3,1},{4,2},{5,3},{6,4},{7,5},{8,6},{9,7},{10,... | collective-permute-start | bytes 884744 | tf_op jit(solution)/shard_map/ppermute | solution.py:145
  66.5 10.7 %collective-permute-start.12 = (bf16[384,384]{1,0:T(8,128)(2,1)S(1)}, bf16[384,384]{1,0:T(8,128)(2,1)}, u32[]{:S(2)}, u32[]{:S(2)}) collective-permute-start(bf16[384,384]{1,0:T(8,128)(2,1)S(1)} %collective-permute-done.11.refs_4_), channel_id=1, source_target_pairs={{0,2},{1,3},{2,4},{3,5},{4,6},{5,7},{6,8},{7,9},{8,10},{9,11},{10,... | collective-permute-start | bytes 884744 | tf_op jit(solution)/shard_map/ppermute | solution.py:145
  66.5 18.1 %copy-start.19 = (bf16[384,384]{1,0:T(8,128)(2,1)}, bf16[384,384]{1,0:T(8,128)(2,1)S(1)}, u32[]{:S(2)}) copy-start(bf16[384,384]{1,0:T(8,128)(2,1)S(1)} %collective-permute-done.22.refs_9_) | copy-start | bytes 884740
  66.5 13.2 %collective-permute-start.17 = (bf16[384,384]{1,0:T(8,128)(2,1)S(1)}, bf16[384,384]{1,0:T(8,128)(2,1)}, u32[]{:S(2)}, u32[]{:S(2)}) collective-permute-start(bf16[384,384]{1,0:T(8,128)(2,1)S(1)} %collective-permute-done.16.refs_7_), channel_id=1, source_target_pairs={{0,14},{1,15},{2,0},{3,1},{4,2},{5,3},{6,4},{7,5},{8,6},{9,7},{10,... | collective-permute-start | bytes 884744 | tf_op jit(solution)/shard_map/ppermute | solution.py:145
  70.8 10.5 %collective-permute-start.13 = (bf16[384,384]{1,0:T(8,128)(2,1)S(1)}, bf16[384,384]{1,0:T(8,128)(2,1)S(1)}, u32[]{:S(2)}, u32[]{:S(2)}) collective-permute-start(bf16[384,384]{1,0:T(8,128)(2,1)S(1)} %collective-permute-done.2.refs_3_), channel_id=1, source_target_pairs={{0,1},{1,0},{2,3},{3,2},{4,5},{5,4},{6,7},{7,6},{8,9},{9,8},{10,11... | collective-permute-start | bytes 884744 | tf_op jit(solution)/shard_map/ppermute | solution.py:148
  72.6 11.0 %collective-permute-start.3 = (bf16[384,384]{1,0:T(8,128)(2,1)S(1)}, bf16[384,384]{1,0:T(8,128)(2,1)}, u32[]{:S(2)}, u32[]{:S(2)}) collective-permute-start(bf16[384,384]{1,0:T(8,128)(2,1)S(1)} %collective-permute-done.2.refs_3_), channel_id=1, source_target_pairs={{0,2},{1,3},{2,4},{3,5},{4,6},{5,7},{6,8},{7,9},{8,10},{9,11},{10,... | collective-permute-start | bytes 884744 | tf_op jit(solution)/shard_map/ppermute | solution.py:145
  73.4 12.6 %collective-permute-start.7 = (bf16[384,384]{1,0:T(8,128)(2,1)}, bf16[384,384]{1,0:T(8,128)(2,1)}, u32[]{:S(2)}, u32[]{:S(2)}) collective-permute-start(bf16[384,384]{1,0:T(8,128)(2,1)} %collective-permute-done.6.refs_8_), channel_id=1, source_target_pairs={{0,14},{1,15},{2,0},{3,1},{4,2},{5,3},{6,4},{7,5},{8,6},{9,7},{10,... | collective-permute-start | bytes 884744 | tf_op jit(solution)/shard_map/ppermute | solution.py:145
  77.2 46.3 %collective-permute-start.19 = (bf16[384,384]{1,0:T(8,128)(2,1)}, bf16[384,384]{1,0:T(8,128)(2,1)}, u32[]{:S(2)}, u32[]{:S(2)}) collective-permute-start(bf16[384,384]{1,0:T(8,128)(2,1)} %collective-permute-done.6.refs_8_), channel_id=1, source_target_pairs={{0,1},{1,0},{2,3},{3,2},{4,5},{5,4},{6,7},{7,6},{8,9},{9,8},{10,11... | collective-permute-start | bytes 884744 | tf_op jit(solution)/shard_map/ppermute | solution.py:148
  79.7 43.7 %collective-permute-start.14 = (bf16[384,384]{1,0:T(8,128)(2,1)}, bf16[384,384]{1,0:T(8,128)(2,1)}, u32[]{:S(2)}, u32[]{:S(2)}) collective-permute-start(bf16[384,384]{1,0:T(8,128)(2,1)} %collective-permute-done.12.refs_4_), channel_id=1, source_target_pairs={{0,1},{1,0},{2,3},{3,2},{4,5},{5,4},{6,7},{7,6},{8,9},{9,8},{10,11... | collective-permute-start | bytes 884744 | tf_op jit(solution)/shard_map/ppermute | solution.py:148
  81.3 42.2 %collective-permute-start.18 = (bf16[384,384]{1,0:T(8,128)(2,1)}, bf16[384,384]{1,0:T(8,128)(2,1)}, u32[]{:S(2)}, u32[]{:S(2)}) collective-permute-start(bf16[384,384]{1,0:T(8,128)(2,1)} %collective-permute-done.17.refs_7_), channel_id=1, source_target_pairs={{0,1},{1,0},{2,3},{3,2},{4,5},{5,4},{6,7},{7,6},{8,9},{9,8},{10,11... | collective-permute-start | bytes 884744 | tf_op jit(solution)/shard_map/ppermute | solution.py:148
  83.5 54.9 %collective-permute-start.8 = (bf16[384,384]{1,0:T(8,128)(2,1)}, bf16[384,384]{1,0:T(8,128)(2,1)}, u32[]{:S(2)}, u32[]{:S(2)}) collective-permute-start(bf16[384,384]{1,0:T(8,128)(2,1)} %collective-permute-done.3.refs_3_), channel_id=1, source_target_pairs={{0,1},{1,0},{2,3},{3,2},{4,5},{5,4},{6,7},{7,6},{8,9},{9,8},{10,11... | collective-permute-start | bytes 884744 | tf_op jit(solution)/shard_map/ppermute | solution.py:148
  86.1 52.4 %collective-permute-start.9 = (bf16[384,384]{1,0:T(8,128)(2,1)}, bf16[384,384]{1,0:T(8,128)(2,1)}, u32[]{:S(2)}, u32[]{:S(2)}) collective-permute-start(bf16[384,384]{1,0:T(8,128)(2,1)} %collective-permute-done.7.refs_4_), channel_id=1, source_target_pairs={{0,1},{1,0},{2,3},{3,2},{4,5},{5,4},{6,7},{7,6},{8,9},{9,8},{10,11... | collective-permute-start | bytes 884744 | tf_op jit(solution)/shard_map/ppermute | solution.py:148
  (6 other events, 73.6 us)

commit v2 on v1

v2 whole, which is shorter than its diff:
```python
import jax
import jax.numpy as jnp
from jax import lax
from jax.experimental import pallas as pl
from jax.experimental.pallas import tpu as pltpu
from jax.sharding import PartitionSpec as P


MIB = 1 << 20
LIMIT = 16


def dot(left, right, dims):
    return lax.dot_general(left, right, (dims, ((), ())), preferred_element_type=jnp.float32)


def block_step_kernel(slots, ids_ref, me_ref, ops_ref, *refs):
    count = len(slots)
    peram_refs = refs[: 2 * count]
    out_ref, weight = refs[-2:]
    half = ops_ref.shape[-1]
    ops_count = ops_ref.shape[1]
    positions = out_ref.shape[0]
    ring = 8
    me = me_ref[0]
    for at, (behind, other) in enumerate(slots):
        zpos = lax.rem(me // 2 + (ring - behind), ring)
        core = lax.rem(me + other, 2)
        spin = 2 * zpos + core
        real = peram_refs[2 * at]
        imag = peram_refs[2 * at + 1]
        weight[:half, :half] = real[...]
        weight[:half, half:] = -imag[...]
        weight[half:, :half] = imag[...]
        weight[half:, half:] = real[...]

        def one(q, carry):
            ident = ids_ref[q]

            @pl.when(ident // ops_count == spin)
            def _():
                op = lax.rem(ident, ops_count)
                left = jnp.concatenate([ops_ref[0, op], ops_ref[1, op]], axis=1)
                product = dot(left, weight[...], ((1,), (1,)))
                out_ref[q, 0] = product[:, :half].astype(jnp.bfloat16)
                out_ref[q, 1] = product[:, half:].astype(jnp.bfloat16)

            return carry

        lax.fori_loop(0, positions, one, 0)


def block_step(slots, ids, me, ops, perams, blocks):
    count = len(slots)
    half = ops.shape[-1]
    smem = pl.BlockSpec(memory_space=pltpu.SMEM)
    vmem = pl.BlockSpec(memory_space=pltpu.VMEM)
    earlier = [] if blocks is None else [blocks]
    return pl.pallas_call(
        lambda *refs: block_step_kernel(slots, *refs),
        out_shape=jax.ShapeDtypeStruct((ids.shape[0], 2, half, half), jnp.bfloat16),
        in_specs=[smem, smem] + [vmem] * (1 + 2 * count + len(earlier)),
        out_specs=vmem,
        scratch_shapes=[pltpu.VMEM((2 * half, 2 * half), jnp.bfloat16)],
        input_output_aliases={3 + 2 * count: 0} if earlier else {},
        compiler_params=pltpu.CompilerParams(vmem_limit_bytes=LIMIT * MIB),
        cost_estimate=pl.CostEstimate(
            flops=count * 8 * half**3, transcendentals=0, bytes_accessed=count * 4 * half**2
        ),
        name="block_step",
    )(ids, me, ops, *perams, *earlier)


def pair_kernel(blocks_ref, out_ref, right):
    half = out_ref.shape[-1]
    pairs = blocks_ref.shape[0] // 2
    for pair in range(pairs):
        right[:half, :half] = blocks_ref[2 * pair + 1, 0]
        right[:half, half:] = blocks_ref[2 * pair + 1, 1]
        right[half:, :half] = -blocks_ref[2 * pair + 1, 1]
        right[half:, half:] = blocks_ref[2 * pair + 1, 0]
        left = jnp.concatenate([blocks_ref[2 * pair, 0], blocks_ref[2 * pair, 1]], axis=1)
        product = dot(left, right[...], ((1,), (0,)))
        scale = 1.0 / jnp.sqrt(jnp.float32(2 * half * pairs))
        for part in range(2):
            term = product[:, part * half : (part + 1) * half]
            if pair:
                term = out_ref[part] + term
            if pair == pairs - 1:
                term = term * scale
            out_ref[part] = term


def pair_sum(blocks):
    half = blocks.shape[-1]
    vmem = pl.BlockSpec(memory_space=pltpu.VMEM)
    return pl.pallas_call(
        pair_kernel,
        out_shape=jax.ShapeDtypeStruct((2, half, half), jnp.float32),
        in_specs=[vmem],
        out_specs=vmem,
        scratch_shapes=[pltpu.VMEM((2 * half, 2 * half), jnp.bfloat16)],
        compiler_params=pltpu.CompilerParams(vmem_limit_bytes=LIMIT * MIB),
        name="pair_sum",
    )(blocks)


def placed(perambulator, meson_ops, diagram_lists):
    sa_count = lax.axis_size("sa")
    ring = sa_count // 2
    far = ring // 2

    def hop(value, step):
        return lax.ppermute(value, "sa", [(i, (i + 2 * step) % sa_count) for i in range(sa_count)])

    def swap(value):
        return lax.ppermute(value, "sa", [(i, i ^ 1) for i in range(sa_count)])

    ids = diagram_lists.reshape(-1)
    me = lax.axis_index("sa").astype(jnp.int32).reshape(1)
    ops = meson_ops[:, :, 0]
    owned = lax.all_to_all(perambulator, "ta", split_axis=1, concat_axis=3, tiled=True)
    real, imag = owned[0, 0, 0], owned[1, 0, 0]
    reals, imags = {0: real}, {0: imag}
    up = down = real
    iup = idown = imag
    for d in range(1, far + 1):
        up = hop(up, 1)
        reals[d] = up
        if d < far:
            down = hop(down, -1)
            reals[ring - d] = down
            iup = hop(iup, 1)
            imags[d] = iup
        idown = hop(idown, -1)
        imags[(ring - d) % ring] = idown
    blocks = None
    for d in range(far + 1):
        where = [d] if d in (0, far) else [d, ring - d]
        slots, perams = [], []
        for behind in where:
            slots += [(behind, 0), (behind, 1)]
            perams += [reals[behind], imags[behind], swap(reals[behind]), swap(imags[behind])]
        blocks = block_step(slots, ids, me, ops, perams, blocks)
    return pair_sum(blocks)[:, None, None]


def solution(mesh):
    in_specs = (
        P(None, None, "sa", "ta", None),
        P(None, None, "ta", None, None),
        P("ta", "sa", None),
    )
    out_specs = P(None, "ta", "sa", None, None)
    return jax.shard_map(placed, mesh=mesh, in_specs=in_specs, out_specs=out_specs, check_vma=False)
```

time: 152 us -> 109 us (0.72)
  Pallas kernels: 62.8 us -> 27.2 us
  starting transfers between devices: 48.7 us -> 33.4 us
  local copies, waits for them, and re-layouts: 2.67 us -> 10.3 us
  blocking collectives: 15.5 us -> 18.7 us
  waiting for transfers between devices: 20.8 us -> 18.7 us
    pallas_call x5, Pallas kernels: 52.6 us -> 21.6 us  [block_step(): pl.pallas_call(lambda *refs: block_step_kernel(slots, *refs), out_shape=j...]
    unnamed x47 -> x32, local copies, waits for them, and re-layouts: 0.17 us -> 10.2 us
    ppermute x16, starting transfers between devices: 21.3 us -> 13.4 us  [swap(): return lax.ppermute(value, 'sa', [(i, i ^ 1) for i in range(sa_count)])]
    pallas_call x1, Pallas kernels: 10.2 us -> 5.63 us  [pair_sum(): pl.pallas_call(pair_kernel, out_shape=jax.ShapeDtypeStruct((2, half, half...]
    all_to_all x1 -> x0, waiting for transfers between devices: 4.31 us -> none  [owned(): got = lax.all_to_all(sent, 'ta', split_axis=0, concat_axis=0, tiled=True)]
    ppermute x14, starting transfers between devices: 23.9 us -> 20 us  [hop(): lax.ppermute(value, 'sa', [(i, (i + 2 * step) % sa_count) for i in range(...]
    all_to_all x1 -> x0, starting transfers between devices: 3.54 us -> none  [owned(): got = lax.all_to_all(sent, 'ta', split_axis=0, concat_axis=0, tiled=True)]
    all_to_all x1, blocking collectives: 15.5 us -> 18.7 us  [placed(): lax.all_to_all(perambulator, 'ta', split_axis=1, concat_axis=3, tiled=True)]
  transfers between devices with their start and end apart: 31 -> 30, of which waited for: 12 -> 5; matrix products, arithmetic and copies ran while one was open for 0% -> 1% of each run, Pallas kernels for 33% -> 17%
where the time goes in v2:
time: 109 us
  starting transfers between devices  33.4 us (31%)
  Pallas kernels  27.2 us (25%)
  blocking collectives  18.7 us (17%)
  waiting for transfers between devices  18.7 us (17%)
  local copies, waits for them, and re-layouts  10.3 us (9%)
    pallas_call x5, Pallas kernels, block_step(): pl.pallas_call(lambda *refs: block_step_kernel(slots, *refs), out_shape=j...  21.6 us
    ppermute x14, starting transfers between devices, hop(): lax.ppermute(value, 'sa', [(i, (i + 2 * step) % sa_count) for i in range(...  20 us
    all_to_all x1, blocking collectives, placed(): lax.all_to_all(perambulator, 'ta', split_axis=1, concat_axis=3, tiled=True)  18.7 us
    ppermute x14, waiting for transfers between devices, hop(): lax.ppermute(value, 'sa', [(i, (i + 2 * step) % sa_count) for i in range(...  18.6 us
    ppermute x16, starting transfers between devices, swap(): return lax.ppermute(value, 'sa', [(i, i ^ 1) for i in range(sa_count)])  13.4 us
    unnamed x32, local copies, waits for them, and re-layouts  10.2 us
    pallas_call x1, Pallas kernels, pair_sum(): pl.pallas_call(pair_kernel, out_shape=jax.ShapeDtypeStruct((2, half, half...  5.63 us
  transfers between devices with their start and end apart: 30, of which 5 were waited for; matrix products, arithmetic and copies ran while one was open for 1% of the time, Pallas kernels for 17%

profile of v2, /device:TPU:1, one launch (start us, length us, event | category | flops | bytes accessed | tf_op | source)
XLA Modules:
  0.0 108.6 jit_solution(6704707475282995812)
XLA Ops:
  0.0 1.1 %copy.13 = bf16[2,16,1,24,384]{4,3,2,0,1:T(8,128)(2,1)S(1)} copy(bf16[2,16,1,24,384]{4,3,2,1,0:T(8,128)(2,1)} %param.3) | data formatting | bytes 1179648 | tf_op args[0]
  1.1 18.7 %all_to_all.4 = bf16[2,16,1,24,384]{4,3,2,0,1:T(8,128)(2,1)S(1)} all-to-all(bf16[2,16,1,24,384]{4,3,2,0,1:T(8,128)(2,1)S(1)} %copy.13), channel_id=1, replica_groups=mesh['ta'=16,'sa'=16] {'ta'}, dimensions={1} | all-to-all | bytes 1179648 | tf_op jit(solution)/shard_map/all_to_all | solution.py:122
  19.9 2.0 %collective-permute-start.28 = (bf16[384,384]{1,0:T(8,128)(2,1)S(1)}, bf16[384,384]{1,0:T(8,128)(2,1)S(1)}, u32[]{:S(2)}, u32[]{:S(2)}) collective-permute-start(bf16[384,384]{1,0:T(8,128)(2,1)S(1)} %bitcast.16), channel_id=1, source_target_pairs={{0,1},{1,0},{2,3},{3,2},{4,5},{5,4},{6,7},{7,6},{8,9},{9,8},{10,11... | collective-permute-start | bytes 884744 | tf_op jit(solution)/shard_map/ppermute | solution.py:117
  21.9 1.6 %collective-permute-start = (bf16[384,384]{1,0:T(8,128)(2,1)S(1)}, bf16[384,384]{1,0:T(8,128)(2,1)S(1)}, u32[]{:S(2)}, u32[]{:S(2)}) collective-permute-start(bf16[384,384]{1,0:T(8,128)(2,1)S(1)} %bitcast.17), channel_id=1, source_target_pairs={{0,2},{1,3},{2,4},{3,5},{4,6},{5,7},{6,8},{7,9},{8,10},{9,11},{10,... | collective-permute-start | bytes 884744 | tf_op jit(solution)/shard_map/ppermute | solution.py:114
  23.5 1.6 %collective-permute-start.10 = (bf16[384,384]{1,0:T(8,128)(2,1)S(1)}, bf16[384,384]{1,0:T(8,128)(2,1)S(1)}, u32[]{:S(2)}, u32[]{:S(2)}) collective-permute-start(bf16[384,384]{1,0:T(8,128)(2,1)S(1)} %bitcast.12), channel_id=1, source_target_pairs={{0,2},{1,3},{2,4},{3,5},{4,6},{5,7},{6,8},{7,9},{8,10},{9,11},{10,... | collective-permute-start | bytes 884744 | tf_op jit(solution)/shard_map/ppermute | solution.py:114
  25.1 2.3 %collective-permute-start.15 = (bf16[384,384]{1,0:T(8,128)(2,1)S(1)}, bf16[384,384]{1,0:T(8,128)(2,1)S(1)}, u32[]{:S(2)}, u32[]{:S(2)}) collective-permute-start(bf16[384,384]{1,0:T(8,128)(2,1)S(1)} %bitcast.18), channel_id=1, source_target_pairs={{0,14},{1,15},{2,0},{3,1},{4,2},{5,3},{6,4},{7,5},{8,6},{9,7},{10,... | collective-permute-start | bytes 884744 | tf_op jit(solution)/shard_map/ppermute | solution.py:114
  27.5 0.5 collective-permute-start.29
  28.0 1.7 %collective-permute-start.4 = (bf16[384,384]{1,0:T(8,128)(2,1)S(1)}, bf16[384,384]{1,0:T(8,128)(2,1)S(1)}, u32[]{:S(2)}, u32[]{:S(2)}) collective-permute-start(bf16[384,384]{1,0:T(8,128)(2,1)S(1)} %bitcast.14), channel_id=1, source_target_pairs={{0,14},{1,15},{2,0},{3,1},{4,2},{5,3},{6,4},{7,5},{8,6},{9,7},{10,... | collective-permute-start | bytes 884744 | tf_op jit(solution)/shard_map/ppermute | solution.py:114
  29.7 5.1 %collective-permute-done.refs_3_ = bf16[384,384]{1,0:T(8,128)(2,1)S(1)} collective-permute-done((bf16[384,384]{1,0:T(8,128)(2,1)S(1)}, bf16[384,384]{1,0:T(8,128)(2,1)S(1)}, u32[]{:S(2)}, u32[]{:S(2)}) %collective-permute-start) | collective-permute-done | bytes 294944 | tf_op jit(solution)/shard_map/ppermute | solution.py:114
  34.7 0.9 collective-permute-start.24
  35.7 5.4 %collective-permute-done.10.refs_4_ = bf16[384,384]{1,0:T(8,128)(2,1)S(1)} collective-permute-done((bf16[384,384]{1,0:T(8,128)(2,1)S(1)}, bf16[384,384]{1,0:T(8,128)(2,1)S(1)}, u32[]{:S(2)}, u32[]{:S(2)}) %collective-permute-start.10) | collective-permute-done | bytes 294944 | tf_op jit(solution)/shard_map/ppermute | solution.py:114
  41.1 0.7 collective-permute-start.25
  41.8 0.7 copy-done.1
  42.5 0.2 collective-permute-start.11
  42.7 2.6 %collective-permute-start.16 = (bf16[384,384]{1,0:T(8,128)(2,1)S(1)}, bf16[384,384]{1,0:T(8,128)(2,1)}, u32[]{:S(2)}, u32[]{:S(2)}) collective-permute-start(bf16[384,384]{1,0:T(8,128)(2,1)S(1)} %collective-permute-done.15.refs_7_), channel_id=1, source_target_pairs={{0,14},{1,15},{2,0},{3,1},{4,2},{5,3},{6,4},{7,5},{8,6},{9,7},{10,... | collective-permute-start | bytes 884744 | tf_op jit(solution)/shard_map/ppermute | solution.py:114
  45.2 1.1 collective-permute-start.27
  46.3 1.7 %collective-permute-start.5 = (bf16[384,384]{1,0:T(8,128)(2,1)S(1)}, bf16[384,384]{1,0:T(8,128)(2,1)S(1)}, u32[]{:S(2)}, u32[]{:S(2)}) collective-permute-start(bf16[384,384]{1,0:T(8,128)(2,1)S(1)} %collective-permute-done.4.refs_8_), channel_id=1, source_target_pairs={{0,14},{1,15},{2,0},{3,1},{4,2},{5,3},{6,4},{7,5},{8,6},{9,7},{10,... | collective-permute-start | bytes 884744 | tf_op jit(solution)/shard_map/ppermute | solution.py:114
  48.0 3.8 %collective-permute-done.1.refs_3_ = bf16[384,384]{1,0:T(8,128)(2,1)S(1)} collective-permute-done((bf16[384,384]{1,0:T(8,128)(2,1)S(1)}, bf16[384,384]{1,0:T(8,128)(2,1)S(1)}, u32[]{:S(2)}, u32[]{:S(2)}) %collective-permute-start.1) | collective-permute-done | bytes 294944 | tf_op jit(solution)/shard_map/ppermute | solution.py:114
  51.8 2.3 %collective-permute-start.20 = (bf16[384,384]{1,0:T(8,128)(2,1)S(1)}, bf16[384,384]{1,0:T(8,128)(2,1)S(1)}, u32[]{:S(2)}, u32[]{:S(2)}) collective-permute-start(bf16[384,384]{1,0:T(8,128)(2,1)S(1)} %collective-permute-done.1.refs_3_), channel_id=1, source_target_pairs={{0,1},{1,0},{2,3},{3,2},{4,5},{5,4},{6,7},{7,6},{8,9},{9,8},{10,11... | collective-permute-start | bytes 884744 | tf_op jit(solution)/shard_map/ppermute | solution.py:117
  54.1 4.0 %collective-permute-done.11.refs_4_ = bf16[384,384]{1,0:T(8,128)(2,1)S(1)} collective-permute-done((bf16[384,384]{1,0:T(8,128)(2,1)S(1)}, bf16[384,384]{1,0:T(8,128)(2,1)S(1)}, u32[]{:S(2)}, u32[]{:S(2)}) %collective-permute-start.11) | collective-permute-done | bytes 294944 | tf_op jit(solution)/shard_map/ppermute | solution.py:114
  58.1 1.4 %collective-permute-start.21 = (bf16[384,384]{1,0:T(8,128)(2,1)S(1)}, bf16[384,384]{1,0:T(8,128)(2,1)S(1)}, u32[]{:S(2)}, u32[]{:S(2)}) collective-permute-start(bf16[384,384]{1,0:T(8,128)(2,1)S(1)} %collective-permute-done.11.refs_4_), channel_id=1, source_target_pairs={{0,1},{1,0},{2,3},{3,2},{4,5},{5,4},{6,7},{7,6},{8,9},{9,8},{10,11... | collective-permute-start | bytes 884744 | tf_op jit(solution)/shard_map/ppermute | solution.py:117
  59.5 0.7 copy-done.9
  60.2 0.5 collective-permute-start.23
  60.7 0.7 copy-done.5
  61.4 3.0 %collective-permute-start.6 = (bf16[384,384]{1,0:T(8,128)(2,1)S(1)}, bf16[384,384]{1,0:T(8,128)(2,1)}, u32[]{:S(2)}, u32[]{:S(2)}) collective-permute-start(bf16[384,384]{1,0:T(8,128)(2,1)S(1)} %collective-permute-done.5.refs_8_), channel_id=1, source_target_pairs={{0,14},{1,15},{2,0},{3,1},{4,2},{5,3},{6,4},{7,5},{8,6},{9,7},{10,... | collective-permute-start | bytes 884744 | tf_op jit(solution)/shard_map/ppermute | solution.py:114
  64.3 0.7 copy-done.3
  65.1 0.7 copy-done.7
  65.8 0.7 copy-done.11
  66.5 2.7 %collective-permute-start.17 = (bf16[384,384]{1,0:T(8,128)(2,1)}, bf16[384,384]{1,0:T(8,128)(2,1)}, u32[]{:S(2)}, u32[]{:S(2)}) collective-permute-start(bf16[384,384]{1,0:T(8,128)(2,1)} %collective-permute-done.16.refs_7_), channel_id=1, source_target_pairs={{0,14},{1,15},{2,0},{3,1},{4,2},{5,3},{6,4},{7,5},{8,6},{9,7},{10,... | collective-permute-start | bytes 884744 | tf_op jit(solution)/shard_map/ppermute | solution.py:114
  69.2 0.4 collective-permute-done.2.refs_3_
  69.5 2.1 %collective-permute-start.13 = (bf16[384,384]{1,0:T(8,128)(2,1)}, bf16[384,384]{1,0:T(8,128)(2,1)}, u32[]{:S(2)}, u32[]{:S(2)}) collective-permute-start(bf16[384,384]{1,0:T(8,128)(2,1)} %collective-permute-done.2.refs_3_), channel_id=1, source_target_pairs={{0,1},{1,0},{2,3},{3,2},{4,5},{5,4},{6,7},{7,6},{8,9},{9,8},{10,11... | collective-permute-start | bytes 884744 | tf_op jit(solution)/shard_map/ppermute | solution.py:117
  71.6 0.7 copy-done.13
  72.4 2.7 %collective-permute-start.7 = (bf16[384,384]{1,0:T(8,128)(2,1)}, bf16[384,384]{1,0:T(8,128)(2,1)}, u32[]{:S(2)}, u32[]{:S(2)}) collective-permute-start(bf16[384,384]{1,0:T(8,128)(2,1)} %collective-permute-done.6.refs_8_), channel_id=1, source_target_pairs={{0,14},{1,15},{2,0},{3,1},{4,2},{5,3},{6,4},{7,5},{8,6},{9,7},{10,... | collective-permute-start | bytes 884744 | tf_op jit(solution)/shard_map/ppermute | solution.py:114
  75.0 0.8 copy.12
  75.8 0.1 reshape.15.refs_0_
  75.9 2.3 %copy-done = bf16[2,8,1,384,384]{4,3,2,1,0:T(8,128)(2,1)S(1)} copy-done((bf16[2,8,1,384,384]{4,3,2,1,0:T(8,128)(2,1)S(1)}, bf16[2,8,1,384,384]{4,3,2,1,0:T(8,128)(2,1)}, u32[]{:S(2)}) %copy-start) | copy-done | bytes 4718616
  78.2 1.0 copy-done.2
  79.2 2.7 %block_step.5.refs_11_ = bf16[16,2,384,384]{3,2,1,0:T(8,128)(2,1)S(1)} custom-call(s32[16]{0:T(128)S(1)} %reshape.15.refs_0_, s32[1]{0:T(128)} %bitcast.refs_1_, bf16[2,8,384,384]{3,2,1,0:T(8,128)(2,1)S(1)} %bitcast.7, bf16[384,384]{1,0:T(8,128)(2,1)S(1)} %bitcast.19, bf16[384,384]{1,0:T(8,128)(2,1)S(1)} %bitcast.15, ...), custom_call_target="tpu_custom_call" | custom-call | flops 905969664 | bytes 1179648 | tf_op jit(solution)/shard_map/block_step/pallas_call | solution.py:59
  81.9 0.9 collective-permute-start.19
  82.8 0.1 collective-permute-start.14
  82.9 0.4 collective-permute-start.18
  83.3 6.8 %block_step.6.refs_11_ = bf16[16,2,384,384]{3,2,1,0:T(8,128)(2,1)S(1)} custom-call(s32[16]{0:T(128)S(1)} %reshape.15.refs_0_, s32[1]{0:T(128)} %bitcast.refs_1_, bf16[2,8,384,384]{3,2,1,0:T(8,128)(2,1)S(1)} %bitcast.8, bf16[384,384]{1,0:T(8,128)(2,1)S(1)} %collective-permute-done.refs_3_, ...), custom_call_target="tpu_custom_call", output_to_operand_aliasing={{}: (11, {})} | custom-call | flops 1811939328 | bytes 2359296 | tf_op jit(solution)/shard_map/block_step/pallas_call | solution.py:59
  90.2 0.1 collective-permute-start.8
  90.3 0.5 collective-permute-start.9
  90.8 3.9 %block_step.7.refs_11_ = bf16[16,2,384,384]{3,2,1,0:T(8,128)(2,1)S(1)} custom-call(s32[16]{0:T(128)S(1)} %reshape.15.refs_0_, s32[1]{0:T(128)} %bitcast.refs_1_, bf16[2,8,384,384]{3,2,1,0:T(8,128)(2,1)S(1)} %bitcast.9, bf16[384,384]{1,0:T(8,128)(2,1)S(1)} %collective-permute-done.1.refs_3_, ...), custom_call_target="tpu_custom_call", output_to_operand_aliasing={{}: (11, {})} | custom-call | flops 1811939328 | bytes 2359296 | tf_op jit(solution)/shard_map/block_step/pallas_call | solution.py:59
  94.8 4.9 %block_step.8.refs_7_ = bf16[16,2,384,384]{3,2,1,0:T(8,128)(2,1)S(1)} custom-call(s32[16]{0:T(128)S(1)} %reshape.15.refs_0_, s32[1]{0:T(128)} %bitcast.refs_1_, bf16[2,8,384,384]{3,2,1,0:T(8,128)(2,1)S(1)} %bitcast.10, bf16[384,384]{1,0:T(8,128)(2,1)} %collective-permute-done.2.refs_3_, ...), custom_call_target="tpu_custom_call", output_to_operand_aliasing={{}: (11, {})} | custom-call | flops 1811939328 | bytes 2359296 | tf_op jit(solution)/shard_map/block_step/pallas_call | solution.py:59
  99.7 3.2 %block_step.9.blocks_ref = bf16[16,2,384,384]{3,2,1,0:T(8,128)(2,1)S(1)} custom-call(s32[16]{0:T(128)S(1)} %reshape.15.refs_0_, s32[1]{0:T(128)} %bitcast.refs_1_, bf16[2,8,384,384]{3,2,1,0:T(8,128)(2,1)S(1)} %bitcast.11, bf16[384,384]{1,0:T(8,128)(2,1)} %collective-permute-done.3.refs_3_, ...), custom_call_target="tpu_custom_call", output_to_operand_aliasing={{}: (7, {})} | custom-call | flops 905969664 | bytes 1179648 | tf_op jit(solution)/shard_map/block_step/pallas_call | solution.py:59
  103.0 5.6 %pair_sum.1 = f32[2,384,384]{2,1,0:T(8,128)} custom-call(bf16[16,2,384,384]{3,2,1,0:T(8,128)(2,1)S(1)} %block_step.9.blocks_ref), custom_call_target="tpu_custom_call" | custom-call | tf_op jit(solution)/shard_map/pair_sum/pallas_call | solution.py:97
  (53 shorter events, 0.2 us)
Async XLA Ops:
  19.9 8.1 %collective-permute-start.28 = (bf16[384,384]{1,0:T(8,128)(2,1)S(1)}, bf16[384,384]{1,0:T(8,128)(2,1)S(1)}, u32[]{:S(2)}, u32[]{:S(2)}) collective-permute-start(bf16[384,384]{1,0:T(8,128)(2,1)S(1)} %bitcast.16), channel_id=1, source_target_pairs={{0,1},{1,0},{2,3},{3,2},{4,5},{5,4},{6,7},{7,6},{8,9},{9,8},{10,11... | collective-permute-start | bytes 884744 | tf_op jit(solution)/shard_map/ppermute | solution.py:117
  21.9 12.9 %collective-permute-start = (bf16[384,384]{1,0:T(8,128)(2,1)S(1)}, bf16[384,384]{1,0:T(8,128)(2,1)S(1)}, u32[]{:S(2)}, u32[]{:S(2)}) collective-permute-start(bf16[384,384]{1,0:T(8,128)(2,1)S(1)} %bitcast.17), channel_id=1, source_target_pairs={{0,2},{1,3},{2,4},{3,5},{4,6},{5,7},{6,8},{7,9},{8,10},{9,11},{10,... | collective-permute-start | bytes 884744 | tf_op jit(solution)/shard_map/ppermute | solution.py:114
  23.5 17.5 %collective-permute-start.10 = (bf16[384,384]{1,0:T(8,128)(2,1)S(1)}, bf16[384,384]{1,0:T(8,128)(2,1)S(1)}, u32[]{:S(2)}, u32[]{:S(2)}) collective-permute-start(bf16[384,384]{1,0:T(8,128)(2,1)S(1)} %bitcast.12), channel_id=1, source_target_pairs={{0,2},{1,3},{2,4},{3,5},{4,6},{5,7},{6,8},{7,9},{8,10},{9,11},{10,... | collective-permute-start | bytes 884744 | tf_op jit(solution)/shard_map/ppermute | solution.py:114
  25.1 16.6 %collective-permute-start.15 = (bf16[384,384]{1,0:T(8,128)(2,1)S(1)}, bf16[384,384]{1,0:T(8,128)(2,1)S(1)}, u32[]{:S(2)}, u32[]{:S(2)}) collective-permute-start(bf16[384,384]{1,0:T(8,128)(2,1)S(1)} %bitcast.18), channel_id=1, source_target_pairs={{0,14},{1,15},{2,0},{3,1},{4,2},{5,3},{6,4},{7,5},{8,6},{9,7},{10,... | collective-permute-start | bytes 884744 | tf_op jit(solution)/shard_map/ppermute | solution.py:114
  27.5 14.3 %collective-permute-start.29 = (bf16[384,384]{1,0:T(8,128)(2,1)S(1)}, bf16[384,384]{1,0:T(8,128)(2,1)S(1)}, u32[]{:S(2)}, u32[]{:S(2)}) collective-permute-start(bf16[384,384]{1,0:T(8,128)(2,1)S(1)} %bitcast.13), channel_id=1, source_target_pairs={{0,1},{1,0},{2,3},{3,2},{4,5},{5,4},{6,7},{7,6},{8,9},{9,8},{10,11... | collective-permute-start | bytes 884744 | tf_op jit(solution)/shard_map/ppermute | solution.py:117
  28.0 14.5 %collective-permute-start.4 = (bf16[384,384]{1,0:T(8,128)(2,1)S(1)}, bf16[384,384]{1,0:T(8,128)(2,1)S(1)}, u32[]{:S(2)}, u32[]{:S(2)}) collective-permute-start(bf16[384,384]{1,0:T(8,128)(2,1)S(1)} %bitcast.14), channel_id=1, source_target_pairs={{0,14},{1,15},{2,0},{3,1},{4,2},{5,3},{6,4},{7,5},{8,6},{9,7},{10,... | collective-permute-start | bytes 884744 | tf_op jit(solution)/shard_map/ppermute | solution.py:114
  34.7 7.9 %collective-permute-start.24 = (bf16[384,384]{1,0:T(8,128)(2,1)S(1)}, bf16[384,384]{1,0:T(8,128)(2,1)S(1)}, u32[]{:S(2)}, u32[]{:S(2)}) collective-permute-start(bf16[384,384]{1,0:T(8,128)(2,1)S(1)} %collective-permute-done.refs_3_), channel_id=1, source_target_pairs={{0,1},{1,0},{2,3},{3,2},{4,5},{5,4},{6,7},{7,6},{8,9},{9,8},{10,11... | collective-permute-start | bytes 884744 | tf_op jit(solution)/shard_map/ppermute | solution.py:117
  41.1 4.2 %collective-permute-start.25 = (bf16[384,384]{1,0:T(8,128)(2,1)S(1)}, bf16[384,384]{1,0:T(8,128)(2,1)S(1)}, u32[]{:S(2)}, u32[]{:S(2)}) collective-permute-start(bf16[384,384]{1,0:T(8,128)(2,1)S(1)} %collective-permute-done.10.refs_4_), channel_id=1, source_target_pairs={{0,1},{1,0},{2,3},{3,2},{4,5},{5,4},{6,7},{7,6},{8,9},{9,8},{10,11... | collective-permute-start | bytes 884744 | tf_op jit(solution)/shard_map/ppermute | solution.py:117
  41.7 4.6 %collective-permute-start.26 = (bf16[384,384]{1,0:T(8,128)(2,1)S(1)}, bf16[384,384]{1,0:T(8,128)(2,1)S(1)}, u32[]{:S(2)}, u32[]{:S(2)}) collective-permute-start(bf16[384,384]{1,0:T(8,128)(2,1)S(1)} %collective-permute-done.15.refs_7_), channel_id=1, source_target_pairs={{0,1},{1,0},{2,3},{3,2},{4,5},{5,4},{6,7},{7,6},{8,9},{9,8},{10,11... | collective-permute-start | bytes 884744 | tf_op jit(solution)/shard_map/ppermute | solution.py:117
  41.7 0.7 copy-start.1
  42.5 9.3 %collective-permute-start.1 = (bf16[384,384]{1,0:T(8,128)(2,1)S(1)}, bf16[384,384]{1,0:T(8,128)(2,1)S(1)}, u32[]{:S(2)}, u32[]{:S(2)}) collective-permute-start(bf16[384,384]{1,0:T(8,128)(2,1)S(1)} %collective-permute-done.refs_3_), channel_id=1, source_target_pairs={{0,2},{1,3},{2,4},{3,5},{4,6},{5,7},{6,8},{7,9},{8,10},{9,11},{10,... | collective-permute-start | bytes 884744 | tf_op jit(solution)/shard_map/ppermute | solution.py:114
  42.5 15.6 %collective-permute-start.11 = (bf16[384,384]{1,0:T(8,128)(2,1)S(1)}, bf16[384,384]{1,0:T(8,128)(2,1)S(1)}, u32[]{:S(2)}, u32[]{:S(2)}) collective-permute-start(bf16[384,384]{1,0:T(8,128)(2,1)S(1)} %collective-permute-done.10.refs_4_), channel_id=1, source_target_pairs={{0,2},{1,3},{2,4},{3,5},{4,6},{5,7},{6,8},{7,9},{8,10},{9,11},{10,... | collective-permute-start | bytes 884744 | tf_op jit(solution)/shard_map/ppermute | solution.py:114
  42.7 16.7 %collective-permute-start.16 = (bf16[384,384]{1,0:T(8,128)(2,1)S(1)}, bf16[384,384]{1,0:T(8,128)(2,1)}, u32[]{:S(2)}, u32[]{:S(2)}) collective-permute-start(bf16[384,384]{1,0:T(8,128)(2,1)S(1)} %collective-permute-done.15.refs_7_), channel_id=1, source_target_pairs={{0,14},{1,15},{2,0},{3,1},{4,2},{5,3},{6,4},{7,5},{8,6},{9,7},{10,... | collective-permute-start | bytes 884744 | tf_op jit(solution)/shard_map/ppermute | solution.py:114
  45.2 14.2 %collective-permute-start.27 = (bf16[384,384]{1,0:T(8,128)(2,1)S(1)}, bf16[384,384]{1,0:T(8,128)(2,1)S(1)}, u32[]{:S(2)}, u32[]{:S(2)}) collective-permute-start(bf16[384,384]{1,0:T(8,128)(2,1)S(1)} %collective-permute-done.4.refs_8_), channel_id=1, source_target_pairs={{0,1},{1,0},{2,3},{3,2},{4,5},{5,4},{6,7},{7,6},{8,9},{9,8},{10,11... | collective-permute-start | bytes 884744 | tf_op jit(solution)/shard_map/ppermute | solution.py:117
  46.3 13.8 %collective-permute-start.5 = (bf16[384,384]{1,0:T(8,128)(2,1)S(1)}, bf16[384,384]{1,0:T(8,128)(2,1)S(1)}, u32[]{:S(2)}, u32[]{:S(2)}) collective-permute-start(bf16[384,384]{1,0:T(8,128)(2,1)S(1)} %collective-permute-done.4.refs_8_), channel_id=1, source_target_pairs={{0,14},{1,15},{2,0},{3,1},{4,2},{5,3},{6,4},{7,5},{8,6},{9,7},{10,... | collective-permute-start | bytes 884744 | tf_op jit(solution)/shard_map/ppermute | solution.py:114
  51.8 8.9 %collective-permute-start.20 = (bf16[384,384]{1,0:T(8,128)(2,1)S(1)}, bf16[384,384]{1,0:T(8,128)(2,1)S(1)}, u32[]{:S(2)}, u32[]{:S(2)}) collective-permute-start(bf16[384,384]{1,0:T(8,128)(2,1)S(1)} %collective-permute-done.1.refs_3_), channel_id=1, source_target_pairs={{0,1},{1,0},{2,3},{3,2},{4,5},{5,4},{6,7},{7,6},{8,9},{9,8},{10,11... | collective-permute-start | bytes 884744 | tf_op jit(solution)/shard_map/ppermute | solution.py:117
  58.1 7.0 %collective-permute-start.21 = (bf16[384,384]{1,0:T(8,128)(2,1)S(1)}, bf16[384,384]{1,0:T(8,128)(2,1)S(1)}, u32[]{:S(2)}, u32[]{:S(2)}) collective-permute-start(bf16[384,384]{1,0:T(8,128)(2,1)S(1)} %collective-permute-done.11.refs_4_), channel_id=1, source_target_pairs={{0,1},{1,0},{2,3},{3,2},{4,5},{5,4},{6,7},{7,6},{8,9},{9,8},{10,11... | collective-permute-start | bytes 884744 | tf_op jit(solution)/shard_map/ppermute | solution.py:117
  59.4 6.3 %collective-permute-start.22 = (bf16[384,384]{1,0:T(8,128)(2,1)}, bf16[384,384]{1,0:T(8,128)(2,1)S(1)}, u32[]{:S(2)}, u32[]{:S(2)}) collective-permute-start(bf16[384,384]{1,0:T(8,128)(2,1)} %collective-permute-done.16.refs_7_), channel_id=1, source_target_pairs={{0,1},{1,0},{2,3},{3,2},{4,5},{5,4},{6,7},{7,6},{8,9},{9,8},{10,11... | collective-permute-start | bytes 884744 | tf_op jit(solution)/shard_map/ppermute | solution.py:117
  59.4 0.7 copy-start.9
  60.2 9.4 %collective-permute-start.2 = (bf16[384,384]{1,0:T(8,128)(2,1)S(1)}, bf16[384,384]{1,0:T(8,128)(2,1)}, u32[]{:S(2)}, u32[]{:S(2)}) collective-permute-start(bf16[384,384]{1,0:T(8,128)(2,1)S(1)} %collective-permute-done.1.refs_3_), channel_id=1, source_target_pairs={{0,2},{1,3},{2,4},{3,5},{4,6},{5,7},{6,8},{7,9},{8,10},{9,11},{10,... | collective-permute-start | bytes 884744 | tf_op jit(solution)/shard_map/ppermute | solution.py:114
  60.2 11.4 %collective-permute-start.23 = (bf16[384,384]{1,0:T(8,128)(2,1)S(1)}, bf16[384,384]{1,0:T(8,128)(2,1)S(1)}, u32[]{:S(2)}, u32[]{:S(2)}) collective-permute-start(bf16[384,384]{1,0:T(8,128)(2,1)S(1)} %collective-permute-done.5.refs_8_), channel_id=1, source_target_pairs={{0,1},{1,0},{2,3},{3,2},{4,5},{5,4},{6,7},{7,6},{8,9},{9,8},{10,11... | collective-permute-start | bytes 884744 | tf_op jit(solution)/shard_map/ppermute | solution.py:117
  60.7 0.7 copy-start.5
  61.4 11.0 %collective-permute-start.6 = (bf16[384,384]{1,0:T(8,128)(2,1)S(1)}, bf16[384,384]{1,0:T(8,128)(2,1)}, u32[]{:S(2)}, u32[]{:S(2)}) collective-permute-start(bf16[384,384]{1,0:T(8,128)(2,1)S(1)} %collective-permute-done.5.refs_8_), channel_id=1, source_target_pairs={{0,14},{1,15},{2,0},{3,1},{4,2},{5,3},{6,4},{7,5},{8,6},{9,7},{10,... | collective-permute-start | bytes 884744 | tf_op jit(solution)/shard_map/ppermute | solution.py:114
  64.3 0.7 copy-start.3
  65.1 0.7 copy-start.7
  65.8 16.1 %collective-permute-start.12 = (bf16[384,384]{1,0:T(8,128)(2,1)S(1)}, bf16[384,384]{1,0:T(8,128)(2,1)}, u32[]{:S(2)}, u32[]{:S(2)}) collective-permute-start(bf16[384,384]{1,0:T(8,128)(2,1)S(1)} %collective-permute-done.11.refs_4_), channel_id=1, source_target_pairs={{0,2},{1,3},{2,4},{3,5},{4,6},{5,7},{6,8},{7,9},{8,10},{9,11},{10,... | collective-permute-start | bytes 884744 | tf_op jit(solution)/shard_map/ppermute | solution.py:114
  65.8 0.7 copy-start.11
  66.5 16.3 %collective-permute-start.17 = (bf16[384,384]{1,0:T(8,128)(2,1)}, bf16[384,384]{1,0:T(8,128)(2,1)}, u32[]{:S(2)}, u32[]{:S(2)}) collective-permute-start(bf16[384,384]{1,0:T(8,128)(2,1)} %collective-permute-done.16.refs_7_), channel_id=1, source_target_pairs={{0,14},{1,15},{2,0},{3,1},{4,2},{5,3},{6,4},{7,5},{8,6},{9,7},{10,... | collective-permute-start | bytes 884744 | tf_op jit(solution)/shard_map/ppermute | solution.py:114
  69.5 13.4 %collective-permute-start.13 = (bf16[384,384]{1,0:T(8,128)(2,1)}, bf16[384,384]{1,0:T(8,128)(2,1)}, u32[]{:S(2)}, u32[]{:S(2)}) collective-permute-start(bf16[384,384]{1,0:T(8,128)(2,1)} %collective-permute-done.2.refs_3_), channel_id=1, source_target_pairs={{0,1},{1,0},{2,3},{3,2},{4,5},{5,4},{6,7},{7,6},{8,9},{9,8},{10,11... | collective-permute-start | bytes 884744 | tf_op jit(solution)/shard_map/ppermute | solution.py:117
  71.6 0.7 copy-start.13
  72.3 17.8 %collective-permute-start.3 = (bf16[384,384]{1,0:T(8,128)(2,1)}, bf16[384,384]{1,0:T(8,128)(2,1)}, u32[]{:S(2)}, u32[]{:S(2)}) collective-permute-start(bf16[384,384]{1,0:T(8,128)(2,1)} %collective-permute-done.2.refs_3_), channel_id=1, source_target_pairs={{0,2},{1,3},{2,4},{3,5},{4,6},{5,7},{6,8},{7,9},{8,10},{9,11},{10,... | collective-permute-start | bytes 884744 | tf_op jit(solution)/shard_map/ppermute | solution.py:114
  72.4 17.9 %collective-permute-start.7 = (bf16[384,384]{1,0:T(8,128)(2,1)}, bf16[384,384]{1,0:T(8,128)(2,1)}, u32[]{:S(2)}, u32[]{:S(2)}) collective-permute-start(bf16[384,384]{1,0:T(8,128)(2,1)} %collective-permute-done.6.refs_8_), channel_id=1, source_target_pairs={{0,14},{1,15},{2,0},{3,1},{4,2},{5,3},{6,4},{7,5},{8,6},{9,7},{10,... | collective-permute-start | bytes 884744 | tf_op jit(solution)/shard_map/ppermute | solution.py:114
  75.9 2.3 %copy-start = (bf16[2,8,1,384,384]{4,3,2,1,0:T(8,128)(2,1)S(1)}, bf16[2,8,1,384,384]{4,3,2,1,0:T(8,128)(2,1)}, u32[]{:S(2)}) copy-start(bf16[2,8,1,384,384]{4,3,2,1,0:T(8,128)(2,1)} %param.4) | copy-start | bytes 14155780
  78.2 1.0 copy-start.2
  79.2 4.2 %copy-start.10 = (bf16[384,384]{1,0:T(8,128)(2,1)S(1)}, bf16[384,384]{1,0:T(8,128)(2,1)}, u32[]{:S(2)}) copy-start(bf16[384,384]{1,0:T(8,128)(2,1)} %copy-done.9) | copy-start | bytes 884740
  81.9 8.9 %copy-start.4 = (bf16[384,384]{1,0:T(8,128)(2,1)S(1)}, bf16[384,384]{1,0:T(8,128)(2,1)}, u32[]{:S(2)}) copy-start(bf16[384,384]{1,0:T(8,128)(2,1)} %copy-done.3) | copy-start | bytes 884740
  81.9 8.9 %copy-start.6 = (bf16[384,384]{1,0:T(8,128)(2,1)S(1)}, bf16[384,384]{1,0:T(8,128)(2,1)}, u32[]{:S(2)}) copy-start(bf16[384,384]{1,0:T(8,128)(2,1)} %copy-done.5) | copy-start | bytes 884740
  81.9 8.9 %copy-start.8 = (bf16[384,384]{1,0:T(8,128)(2,1)S(1)}, bf16[384,384]{1,0:T(8,128)(2,1)}, u32[]{:S(2)}) copy-start(bf16[384,384]{1,0:T(8,128)(2,1)} %copy-done.7) | copy-start | bytes 884740
  81.9 8.9 %copy-start.12 = (bf16[384,384]{1,0:T(8,128)(2,1)S(1)}, bf16[384,384]{1,0:T(8,128)(2,1)}, u32[]{:S(2)}) copy-start(bf16[384,384]{1,0:T(8,128)(2,1)} %copy-done.11) | copy-start | bytes 884740
  81.9 8.9 %copy-start.14 = (bf16[384,384]{1,0:T(8,128)(2,1)S(1)}, bf16[384,384]{1,0:T(8,128)(2,1)}, u32[]{:S(2)}) copy-start(bf16[384,384]{1,0:T(8,128)(2,1)} %copy-done.13) | copy-start | bytes 884740
  81.9 12.8 %collective-permute-start.19 = (bf16[384,384]{1,0:T(8,128)(2,1)}, bf16[384,384]{1,0:T(8,128)(2,1)S(1)}, u32[]{:S(2)}, u32[]{:S(2)}) collective-permute-start(bf16[384,384]{1,0:T(8,128)(2,1)} %collective-permute-done.6.refs_8_), channel_id=1, source_target_pairs={{0,1},{1,0},{2,3},{3,2},{4,5},{5,4},{6,7},{7,6},{8,9},{9,8},{10,11... | collective-permute-start | bytes 884744 | tf_op jit(solution)/shard_map/ppermute | solution.py:117
  82.8 11.9 %collective-permute-start.14 = (bf16[384,384]{1,0:T(8,128)(2,1)}, bf16[384,384]{1,0:T(8,128)(2,1)S(1)}, u32[]{:S(2)}, u32[]{:S(2)}) collective-permute-start(bf16[384,384]{1,0:T(8,128)(2,1)} %collective-permute-done.12.refs_4_), channel_id=1, source_target_pairs={{0,1},{1,0},{2,3},{3,2},{4,5},{5,4},{6,7},{7,6},{8,9},{9,8},{10,11... | collective-permute-start | bytes 884744 | tf_op jit(solution)/shard_map/ppermute | solution.py:117
  82.9 11.8 %collective-permute-start.18 = (bf16[384,384]{1,0:T(8,128)(2,1)}, bf16[384,384]{1,0:T(8,128)(2,1)S(1)}, u32[]{:S(2)}, u32[]{:S(2)}) collective-permute-start(bf16[384,384]{1,0:T(8,128)(2,1)} %collective-permute-done.17.refs_7_), channel_id=1, source_target_pairs={{0,1},{1,0},{2,3},{3,2},{4,5},{5,4},{6,7},{7,6},{8,9},{9,8},{10,11... | collective-permute-start | bytes 884744 | tf_op jit(solution)/shard_map/ppermute | solution.py:117
  90.2 9.6 %collective-permute-start.8 = (bf16[384,384]{1,0:T(8,128)(2,1)}, bf16[384,384]{1,0:T(8,128)(2,1)S(1)}, u32[]{:S(2)}, u32[]{:S(2)}) collective-permute-start(bf16[384,384]{1,0:T(8,128)(2,1)} %collective-permute-done.3.refs_3_), channel_id=1, source_target_pairs={{0,1},{1,0},{2,3},{3,2},{4,5},{5,4},{6,7},{7,6},{8,9},{9,8},{10,11... | collective-permute-start | bytes 884744 | tf_op jit(solution)/shard_map/ppermute | solution.py:117
  90.3 9.5 %collective-permute-start.9 = (bf16[384,384]{1,0:T(8,128)(2,1)}, bf16[384,384]{1,0:T(8,128)(2,1)S(1)}, u32[]{:S(2)}, u32[]{:S(2)}) collective-permute-start(bf16[384,384]{1,0:T(8,128)(2,1)} %collective-permute-done.7.refs_4_), channel_id=1, source_target_pairs={{0,1},{1,0},{2,3},{3,2},{4,5},{5,4},{6,7},{7,6},{8,9},{9,8},{10,11... | collective-permute-start | bytes 884744 | tf_op jit(solution)/shard_map/ppermute | solution.py:117

commit v3 on v0

v3 whole, which is shorter than its diff:
```python
import jax
import jax.numpy as jnp
from jax import lax
from jax.experimental import pallas as pl
from jax.experimental.pallas import tpu as pltpu
from jax.sharding import PartitionSpec as P

LIMIT = 16 << 20
ROOM = (5, 10, 10, 8)
OPERATOR, FIRST, LAST, USES, WHEN, TABLE = 0, 16, 32, 48, 64, 128


def dot(left, right, dims):
    return lax.dot_general(left, right, (dims, ((), ())), preferred_element_type=jnp.float32)


def fill_table(table, ids_ref, me, ring, ops_count, positions):
    for slot in range(2 * ring):
        table[USES + slot] = 0
    arrival = []
    load = [jnp.int32(0) for _ in range(ring // 2 + 1)]
    for q in range(positions):
        ident = ids_ref[q]
        spin = lax.div(ident, ops_count)
        table[OPERATOR + q] = ident - spin * ops_count
        behind = jnp.bitwise_and((me >> 1) - (spin >> 1), ring - 1)
        slot = 2 * behind + jnp.bitwise_xor(jnp.bitwise_and(me, 1), jnp.bitwise_and(spin, 1))
        count = table[USES + slot]
        table[FIRST + slot] = jnp.where(count == 0, q, table[FIRST + slot])
        table[LAST + slot] = q
        table[USES + slot] = count + 1
        step = jnp.minimum(behind, ring - behind)
        arrival.append(step)
        load = [n + jnp.where(step == d, 1, 0) for d, n in enumerate(load)]
    final = ring // 2
    when = [jnp.int32(final) for _ in range(positions // 2)]
    for d in range(final):
        for p in range(positions // 2):
            ready = jnp.maximum(arrival[2 * p], arrival[2 * p + 1])
            take = (when[p] == final) & (ready <= d) & (load[d] < ROOM[d])
            when[p] = jnp.where(take, d, when[p])
            load[d] = load[d] + jnp.where(take, 1, 0)
    for p in range(positions // 2):
        table[WHEN + p] = when[p]


def make_blocks(slot, real, imag, table, ops_ref, left_ref, right_ref, weight):
    half = ops_ref.shape[-1]
    uses = table[USES + slot]

    @pl.when(uses > 0)
    def _():
        weight[:half, :half] = real[...]
        weight[:half, half:] = -imag[...]
        weight[half:, :half] = imag[...]
        weight[half:, half:] = real[...]

        def one(use, carry):
            q = jnp.where(use == 0, table[FIRST + slot], table[LAST + slot])
            op = table[OPERATOR + q]
            stacked = jnp.concatenate([ops_ref[0, op], ops_ref[1, op]], axis=1)
            block = dot(stacked, weight[...], ((1,), (1,))).astype(jnp.bfloat16)
            p = q >> 1

            @pl.when(jnp.bitwise_and(q, 1) == 0)
            def _():
                left_ref[p] = block

            @pl.when(jnp.bitwise_and(q, 1) == 1)
            def _():
                right_ref[p, :half] = block
                right_ref[p, half:, :half] = -block[:, half:]
                right_ref[p, half:, half:] = block[:, :half]

            return carry

        lax.fori_loop(0, uses, one, 0)


def add_pairs(step, table, left_ref, right_ref, sum_ref):
    half = sum_ref.shape[-1]

    def pair(p, carry):
        @pl.when(table[WHEN + p] == step)
        def _():
            product = dot(left_ref[p], right_ref[p], ((1,), (0,)))
            sum_ref[0] += product[:, :half]
            sum_ref[1] += product[:, half:]

        return carry

    lax.fori_loop(0, left_ref.shape[0], pair, 0)


def work(slots, parts, inputs, ops, step=None, final=False, ids=None, me=None, ring=None):
    half = ops.shape[-1]
    smem = pl.BlockSpec(memory_space=pltpu.SMEM)
    vmem = pl.BlockSpec(memory_space=pltpu.VMEM)
    arrays = [array for pair in parts for array in pair[:1 if pair[1] is None else 2]]
    starts = ids is not None
    table, left, right, total = inputs
    pairs = 8 if starts else left.shape[0]
    blocks_shape = (
        jax.ShapeDtypeStruct((pairs, half, 2 * half), jnp.bfloat16),
        jax.ShapeDtypeStruct((pairs, 2 * half, 2 * half), jnp.bfloat16),
    )
    sum_shape = jax.ShapeDtypeStruct((2, half, half), jnp.float32)
    scratch = [pltpu.VMEM((2 * half, 2 * half), jnp.bfloat16)]
    out_shape, out_specs, aliases = [], [], {}
    operands = [ids, me] if starts else [table]
    in_specs = [smem] * len(operands)
    operands += [ops, *arrays]
    if starts:
        out_shape += [jax.ShapeDtypeStruct((TABLE,), jnp.int32), *blocks_shape]
        out_specs += [smem, vmem, vmem]
    else:
        kept = [left, right]
        aliases = {len(operands): 0, len(operands) + 1: 1}
        out_shape += blocks_shape
        out_specs += [vmem, vmem]
        if step is not None:
            if total is not None:
                kept.append(total)
                if not final:
                    aliases[len(operands) + 2] = len(out_shape)
            out_shape.append(sum_shape)
            out_specs.append(vmem)
        operands += kept
    in_specs += [vmem] * (len(operands) - len(in_specs))

    def kernel(*refs):
        given, outs, weight = refs[: len(operands)], refs[len(operands) : -1], refs[-1]
        if starts:
            ids_ref, me_ref, ops_ref = given[:3]
            at = 3
            table_ref, left_ref, right_ref = outs
            fill_table(table_ref, ids_ref, me_ref[0], ring, ops_ref.shape[1], ids_ref.shape[0])
        else:
            table_ref, ops_ref = given[:2]
            at = 2
            left_ref, right_ref = outs[:2]
        for slot, pair in zip(slots, parts, strict=True):
            if pair[1] is None:
                real, imag = given[at].at[0], given[at].at[1]
                at += 1
            else:
                real, imag = given[at], given[at + 1]
                at += 2
            make_blocks(slot, real, imag, table_ref, ops_ref, left_ref, right_ref, weight)
        if step is None:
            return
        sum_ref = outs[-1]
        if total is None:
            sum_ref[...] = jnp.zeros(sum_ref.shape, jnp.float32)
        elif final:
            sum_ref[...] = given[-1][...]
        add_pairs(step, table_ref, left_ref, right_ref, sum_ref)
        if final:
            sum_ref[...] = sum_ref[...] * (1.0 / jnp.sqrt(jnp.float32(2 * half * pairs)))

    outs = pl.pallas_call(
        kernel,
        out_shape=tuple(out_shape),
        in_specs=in_specs,
        out_specs=tuple(out_specs),
        scratch_shapes=scratch,
        input_output_aliases=aliases,
        compiler_params=pltpu.CompilerParams(vmem_limit_bytes=LIMIT),
        cost_estimate=pl.CostEstimate(
            flops=len(slots) * 8 * half**3, transcendentals=0, bytes_accessed=len(slots) * 4 * half**2
        ),
        name="work",
    )(*operands)
    if starts:
        return (*outs, None)
    if final:
        return outs[2]
    return (table, outs[0], outs[1], outs[2] if step is not None else total)


def placed(perambulator, meson_ops, diagram_lists):
    sa_count = lax.axis_size("sa")
    ring = sa_count // 2
    far = ring // 2

    def hop(value, step):
        return lax.ppermute(value, "sa", [(i, (i + 2 * step) % sa_count) for i in range(sa_count)])

    def swap(value):
        return lax.ppermute(value, "sa", [(i, i ^ 1) for i in range(sa_count)])

    ids = diagram_lists.reshape(-1)
    me = lax.axis_index("sa").astype(jnp.int32).reshape(1)
    ops = meson_ops[:, :, 0]
    owned = lax.all_to_all(perambulator, "ta", split_axis=1, concat_axis=3, tiled=True)[:, 0, 0]
    up = {0: owned}
    down = {0: owned}
    for d in range(1, far):
        up[d] = hop(up[d - 1], 1)
        down[d] = hop(down[d - 1], -1)
    up[far] = hop(up[far - 1][0], 1)
    down[far] = hop(down[far - 1][1], -1)
    state = (None, None, None, None)
    for d in range(far + 1):
        other_up = swap(up[d])
        other_down = swap(down[d]) if d else None
        if d == far:
            own, other = [(up[d], down[d])], [(other_up, other_down)]
            slots = [2 * d]
        elif d:
            own, other = [(up[d], None), (down[d], None)], [(other_up, None), (other_down, None)]
            slots = [2 * d, 2 * (ring - d)]
        else:
            own, other = [(up[d], None)], [(other_up, None)]
            slots = [0]
        begin = {} if d else {"ids": ids, "me": me, "ring": ring}
        state = work(slots, own, state, ops, **begin)
        state = work([s + 1 for s in slots], other, state, ops, step=d, final=d == far)
    return state[:, None, None]


def solution(mesh):
    in_specs = (
        P(None, None, "sa", "ta", None),
        P(None, None, "ta", None, None),
        P("ta", "sa", None),
    )
    out_specs = P(None, "ta", "sa", None, None)
    return jax.shard_map(placed, mesh=mesh, in_specs=in_specs, out_specs=out_specs, check_vma=False)
```

time: 518 us -> 105 us (0.20)
  the two profiles are of different devices: /device:TPU:1 before, /device:TPU:0 now
where the time goes in v3:
time: 105 us; the launch traced here: 104 us
  waiting for transfers between devices  29.1 us (28%)
  Pallas kernels  28.6 us (27%)
  starting transfers between devices  24 us (23%)
  blocking collectives  17.4 us (17%)
  local copies, waits for them, and re-layouts  5.24 us (5%)
    ppermute x8, waiting for transfers between devices, hop(): lax.ppermute(value, 'sa', [(i, (i + 2 * step) % sa_count) for i in range(...  29.1 us
    pallas_call x10, Pallas kernels, work(): pl.pallas_call(kernel, out_shape=tuple(out_shape), in_specs=in_specs, out...  28.6 us
    all_to_all x1, blocking collectives, placed(): lax.all_to_all(perambulator, 'ta', split_axis=1, concat_axis=3, tiled=True)  17.4 us
    ppermute x8, starting transfers between devices, hop(): lax.ppermute(value, 'sa', [(i, (i + 2 * step) % sa_count) for i in range(...  16.3 us
    ppermute x9, starting transfers between devices, swap(): return lax.ppermute(value, 'sa', [(i, i ^ 1) for i in range(sa_count)])  7.61 us
    unnamed x10, local copies, waits for them, and re-layouts  5.04 us
  transfers between devices with their start and end apart: 17, of which 4 were waited for; matrix products, arithmetic and copies ran while one was open for 1% of the time, Pallas kernels for 23%

profile of v3, /device:TPU:0, one launch (start us, length us, event | category | flops | bytes accessed | tf_op | source)
XLA Modules:
  0.0 104.5 jit_solution(9345273697244285979)
XLA Ops:
  0.0 1.1 %copy.30 = bf16[2,16,1,24,384]{4,3,2,0,1:T(8,128)(2,1)S(1)} copy(bf16[2,16,1,24,384]{4,3,2,1,0:T(8,128)(2,1)} %param.3) | data formatting | bytes 1179648 | tf_op args[0]
  1.1 17.4 %all_to_all.4 = bf16[2,16,1,24,384]{4,3,2,0,1:T(8,128)(2,1)S(1)} all-to-all(bf16[2,16,1,24,384]{4,3,2,0,1:T(8,128)(2,1)S(1)} %copy.30), channel_id=1, replica_groups=mesh['ta'=16,'sa'=16] {'ta'}, dimensions={1} | all-to-all | bytes 1179648 | tf_op jit(solution)/shard_map/all_to_all | solution.py:195
  18.5 0.1 copy.31
  18.6 2.0 %collective-permute-start = (bf16[2,384,384]{2,1,0:T(8,128)(2,1)S(1)}, bf16[2,384,384]{2,1,0:T(8,128)(2,1)S(1)}, u32[]{:S(2)}, u32[]{:S(2)}) collective-permute-start(bf16[2,384,384]{2,1,0:T(8,128)(2,1)S(1)} %bitcast.20), channel_id=1, source_target_pairs={{0,2},{1,3},{2,4},{3,5},{4,6},{5,7},{6,8},{7,9},{8,10},{9,11},{10,... | collective-permute-start | bytes 1769480 | tf_op jit(solution)/shard_map/ppermute | solution.py:187
  20.6 4.0 %collective-permute-start.5 = (bf16[2,384,384]{2,1,0:T(8,128)(2,1)S(1)}, bf16[2,384,384]{2,1,0:T(8,128)(2,1)}, u32[]{:S(2)}, u32[]{:S(2)}) collective-permute-start(bf16[2,384,384]{2,1,0:T(8,128)(2,1)S(1)} %bitcast.21), channel_id=1, source_target_pairs={{0,14},{1,15},{2,0},{3,1},{4,2},{5,3},{6,4},{7,5},{8,6},{9,7},{10,... | collective-permute-start | bytes 1769480 | tf_op jit(solution)/shard_map/ppermute | solution.py:187
  24.6 12.0 %collective-permute-done.refs_2_ = bf16[2,384,384]{2,1,0:T(8,128)(2,1)S(1)} collective-permute-done((bf16[2,384,384]{2,1,0:T(8,128)(2,1)S(1)}, bf16[2,384,384]{2,1,0:T(8,128)(2,1)S(1)}, u32[]{:S(2)}, u32[]{:S(2)}) %collective-permute-start) | collective-permute-done | bytes 589856 | tf_op jit(solution)/shard_map/ppermute | solution.py:187
  36.6 0.0 collective-permute-start.1
  36.6 0.0 collective-permute-done.5.refs_3_
  36.6 3.2 %collective-permute-start.6 = (bf16[2,384,384]{2,1,0:T(8,128)(2,1)}, bf16[2,384,384]{2,1,0:T(8,128)(2,1)S(1)}, u32[]{:S(2)}, u32[]{:S(2)}) collective-permute-start(bf16[2,384,384]{2,1,0:T(8,128)(2,1)} %collective-permute-done.5.refs_3_), channel_id=1, source_target_pairs={{0,14},{1,15},{2,0},{3,1},{4,2},{5,3},{6,4},{7,5},{8,6},{9,7},{10,... | collective-permute-start | bytes 1769480 | tf_op jit(solution)/shard_map/ppermute | solution.py:187
  39.9 0.0 collective-permute-start.16
  39.9 11.2 %collective-permute-done.1.refs_2_ = bf16[2,384,384]{2,1,0:T(8,128)(2,1)S(1)} collective-permute-done((bf16[2,384,384]{2,1,0:T(8,128)(2,1)S(1)}, bf16[2,384,384]{2,1,0:T(8,128)(2,1)S(1)}, u32[]{:S(2)}, u32[]{:S(2)}) %collective-permute-start.1) | collective-permute-done | bytes 589856 | tf_op jit(solution)/shard_map/ppermute | solution.py:187
  51.1 0.0 collective-permute-start.2
  51.1 0.0 collective-permute-start.14
  51.1 0.0 collective-permute-done.6.refs_3_
  51.1 3.2 %collective-permute-start.7 = (bf16[2,384,384]{2,1,0:T(8,128)(2,1)S(1)}, bf16[2,384,384]{2,1,0:T(8,128)(2,1)S(1)}, u32[]{:S(2)}, u32[]{:S(2)}) collective-permute-start(bf16[2,384,384]{2,1,0:T(8,128)(2,1)S(1)} %collective-permute-done.6.refs_3_), channel_id=1, source_target_pairs={{0,14},{1,15},{2,0},{3,1},{4,2},{5,3},{6,4},{7,5},{8,6},{9,7},{10,... | collective-permute-start | bytes 1769480 | tf_op jit(solution)/shard_map/ppermute | solution.py:187
  54.3 0.2 collective-permute-start.15
  54.6 0.0 collective-permute-done.16.refs_2_
  54.6 0.8 copy-done.2
  55.4 0.3 collective-permute-start.12
  55.7 0.8 copy.29
  56.4 0.1 reshape.10.refs_0_
  56.5 2.3 %copy-done = bf16[2,8,1,384,384]{4,3,2,1,0:T(8,128)(2,1)S(1)} copy-done((bf16[2,8,1,384,384]{4,3,2,1,0:T(8,128)(2,1)S(1)}, bf16[2,8,1,384,384]{4,3,2,1,0:T(8,128)(2,1)}, u32[]{:S(2)}) %copy-start) | copy-done | bytes 4718616
  58.9 2.3 %work.10 = (s32[128]{0:T(128)S(1)}, bf16[8,384,768]{2,1,0:T(8,128)(2,1)S(1)}, bf16[8,768,768]{2,1,0:T(8,128)(2,1)S(1)}) custom-call(s32[16]{0:T(128)S(1)} %reshape.10.refs_0_, s32[1]{0:T(128)} %bitcast.refs_1_, bf16[2,8,384,384]{3,2,1,0:T(8,128)(2,1)S(1)} %bitcast.10, bf16[2,384,384]{2,1,0:T(8,128)(2,1)S(1)} %bitcast.23), custom_call_target="tpu_custom_call" | custom-call | flops 452984832 | bytes 589824 | tf_op jit(solution)/shard_map/work/pallas_call | solution.py:161
  61.2 3.6 %collective-permute-done.2.refs_2_ = bf16[2,384,384]{2,1,0:T(8,128)(2,1)S(1)} collective-permute-done((bf16[2,384,384]{2,1,0:T(8,128)(2,1)S(1)}, bf16[2,384,384]{2,1,0:T(8,128)(2,1)S(1)}, u32[]{:S(2)}, u32[]{:S(2)}) %collective-permute-start.2) | collective-permute-done | bytes 589856 | tf_op jit(solution)/shard_map/ppermute | solution.py:187
  64.7 0.0 collective-permute-start.13
  64.8 0.0 collective-permute-done.14.refs_2_
  64.8 0.6 collective-permute-start.10
  65.4 2.2 %collective-permute-done.7.refs_3_ = bf16[2,384,384]{2,1,0:T(8,128)(2,1)S(1)} collective-permute-done((bf16[2,384,384]{2,1,0:T(8,128)(2,1)S(1)}, bf16[2,384,384]{2,1,0:T(8,128)(2,1)S(1)}, u32[]{:S(2)}, u32[]{:S(2)}) %collective-permute-start.7) | collective-permute-done | bytes 589856 | tf_op jit(solution)/shard_map/ppermute | solution.py:187
  67.6 0.0 collective-permute-start.11
  67.6 0.0 collective-permute-done.15.refs_3_
  67.7 0.1 collective-permute-start.3
  67.7 0.0 collective-permute-done.12.refs_2_
  67.8 3.8 %collective-permute-start.8 = (bf16[384,384]{1,0:T(8,128)(2,1)S(1)}, bf16[384,384]{1,0:T(8,128)(2,1)S(1)}, u32[]{:S(2)}, u32[]{:S(2)}) collective-permute-start(bf16[384,384]{1,0:T(8,128)(2,1)S(1)} %slice_bitcast_fusion), channel_id=1, source_target_pairs={{0,14},{1,15},{2,0},{3,1},{4,2},{5,3},{6,4},{7,5},{8,6},{9,7},{10,... | collective-permute-start | bytes 884744 | tf_op jit(solution)/shard_map/ppermute | solution.py:187
  71.5 1.8 %work.11 = (bf16[8,384,768]{2,1,0:T(8,128)(2,1)S(1)}, bf16[8,768,768]{2,1,0:T(8,128)(2,1)S(1)}, f32[2,384,384]{2,1,0:T(8,128)S(1)}) custom-call(s32[128]{0:T(128)S(1)} %get-tuple-element.29.refs_0_, bf16[2,8,384,384]{3,2,1,0:T(8,128)(2,1)S(1)} %bitcast.11, bf16[2,384,384]{2,1,0:T(8,128)(2,1)S(1)} %copy-done.3, ...), custom_call_target="tpu_custom_call", output_to_operand_aliasing={{0}: (3, {}), {1}: (4, {})} | custom-call | flops 452984832 | bytes 589824 | tf_op jit(solution)/shard_map/work/pallas_call | solution.py:161
  73.3 2.0 %work.12 = (bf16[8,384,768]{2,1,0:T(8,128)(2,1)S(1)}, bf16[8,768,768]{2,1,0:T(8,128)(2,1)S(1)}) custom-call(s32[128]{0:T(128)S(1)} %get-tuple-element.29.refs_0_, bf16[2,8,384,384]{3,2,1,0:T(8,128)(2,1)S(1)} %bitcast.12, bf16[2,384,384]{2,1,0:T(8,128)(2,1)S(1)} %collective-permute-done.refs_2_, ...), custom_call_target="tpu_custom_call", output_to_operand_aliasing={{0}: (4, {}), {1}: (5, {})} | custom-call | flops 905969664 | bytes 1179648 | tf_op jit(solution)/shard_map/work/pallas_call | solution.py:161
  75.3 3.8 %work.13 = (bf16[8,384,768]{2,1,0:T(8,128)(2,1)S(1)}, bf16[8,768,768]{2,1,0:T(8,128)(2,1)S(1)}, f32[2,384,384]{2,1,0:T(8,128)S(1)}) custom-call(s32[128]{0:T(128)S(1)} %get-tuple-element.29.refs_0_, bf16[2,8,384,384]{3,2,1,0:T(8,128)(2,1)S(1)} %bitcast.13, ...), custom_call_target="tpu_custom_call", output_to_operand_aliasing={{0}: (4, {}), {1}: (5, {}), {2}: (6, {})} | custom-call | flops 905969664 | bytes 1179648 | tf_op jit(solution)/shard_map/work/pallas_call | solution.py:161
  79.0 0.6 work.14
  79.6 0.0 collective-permute-done.3.refs_2_
  79.6 6.4 %collective-permute-start.4 = (bf16[384,384]{1,0:T(8,128)(2,1)S(1)}, bf16[384,384]{1,0:T(8,128)(2,1)S(1)}, u32[]{:S(2)}, u32[]{:S(2)}) collective-permute-start(bf16[384,384]{1,0:T(8,128)(2,1)S(1)} %collective-permute-done.3.refs_2_), channel_id=1, source_target_pairs={{0,1},{1,0},{2,3},{3,2},{4,5},{5,4},{6,7},{7,6},{8,9},{9,8},{10,11... | collective-permute-start | bytes 884744 | tf_op jit(solution)/shard_map/ppermute | solution.py:190
  86.0 0.0 collective-permute-done.8.refs_3_
  86.0 0.1 collective-permute-start.9
  86.1 4.9 %work.15 = (bf16[8,384,768]{2,1,0:T(8,128)(2,1)S(1)}, bf16[8,768,768]{2,1,0:T(8,128)(2,1)S(1)}, f32[2,384,384]{2,1,0:T(8,128)S(1)}) custom-call(s32[128]{0:T(128)S(1)} %get-tuple-element.29.refs_0_, bf16[2,8,384,384]{3,2,1,0:T(8,128)(2,1)S(1)} %bitcast.15, ...), custom_call_target="tpu_custom_call", output_to_operand_aliasing={{0}: (4, {}), {1}: (5, {}), {2}: (6, {})} | custom-call | flops 905969664 | bytes 1179648 | tf_op jit(solution)/shard_map/work/pallas_call | solution.py:161
  91.0 2.9 %work.16 = (bf16[8,384,768]{2,1,0:T(8,128)(2,1)S(1)}, bf16[8,768,768]{2,1,0:T(8,128)(2,1)S(1)}) custom-call(s32[128]{0:T(128)S(1)} %get-tuple-element.29.refs_0_, bf16[2,8,384,384]{3,2,1,0:T(8,128)(2,1)S(1)} %bitcast.16, bf16[2,384,384]{2,1,0:T(8,128)(2,1)S(1)} %collective-permute-done.2.refs_2_, ...), custom_call_target="tpu_custom_call", output_to_operand_aliasing={{0}: (4, {}), {1}: (5, {})} | custom-call | flops 905969664 | bytes 1179648 | tf_op jit(solution)/shard_map/work/pallas_call | solution.py:161
  93.9 0.0 collective-permute-done.10.refs_2_
  94.0 4.7 %work.17 = (bf16[8,384,768]{2,1,0:T(8,128)(2,1)S(1)}, bf16[8,768,768]{2,1,0:T(8,128)(2,1)S(1)}, f32[2,384,384]{2,1,0:T(8,128)S(1)}) custom-call(s32[128]{0:T(128)S(1)} %get-tuple-element.29.refs_0_, bf16[2,8,384,384]{3,2,1,0:T(8,128)(2,1)S(1)} %bitcast.17, ...), custom_call_target="tpu_custom_call", output_to_operand_aliasing={{0}: (4, {}), {1}: (5, {}), {2}: (6, {})} | custom-call | flops 905969664 | bytes 1179648 | tf_op jit(solution)/shard_map/work/pallas_call | solution.py:161
  98.7 1.4 %work.18 = (bf16[8,384,768]{2,1,0:T(8,128)(2,1)S(1)}, bf16[8,768,768]{2,1,0:T(8,128)(2,1)S(1)}) custom-call(s32[128]{0:T(128)S(1)} %get-tuple-element.29.refs_0_, bf16[2,8,384,384]{3,2,1,0:T(8,128)(2,1)S(1)} %bitcast.18, bf16[384,384]{1,0:T(8,128)(2,1)S(1)} %collective-permute-done.3.refs_2_, ...), custom_call_target="tpu_custom_call", output_to_operand_aliasing={{0}: (4, {}), {1}: (5, {})} | custom-call | flops 452984832 | bytes 589824 | tf_op jit(solution)/shard_map/work/pallas_call | solution.py:161
  100.1 0.0 collective-permute-done.9.refs_3_
  100.1 4.4 %work.19 = (bf16[8,384,768]{2,1,0:T(8,128)(2,1)S(1)}, bf16[8,768,768]{2,1,0:T(8,128)(2,1)S(1)}, f32[2,384,384]{2,1,0:T(8,128)}) custom-call(s32[128]{0:T(128)S(1)} %get-tuple-element.29.refs_0_, bf16[2,8,384,384]{3,2,1,0:T(8,128)(2,1)S(1)} %bitcast.19, ...), custom_call_target="tpu_custom_call", output_to_operand_aliasing={{0}: (4, {}), {1}: (5, {})} | custom-call | flops 452984832 | bytes 589824 | tf_op jit(solution)/shard_map/work/pallas_call | solution.py:161
  (11 shorter events, 0.1 us)
Async XLA Ops:
  18.6 18.0 %collective-permute-start = (bf16[2,384,384]{2,1,0:T(8,128)(2,1)S(1)}, bf16[2,384,384]{2,1,0:T(8,128)(2,1)S(1)}, u32[]{:S(2)}, u32[]{:S(2)}) collective-permute-start(bf16[2,384,384]{2,1,0:T(8,128)(2,1)S(1)} %bitcast.20), channel_id=1, source_target_pairs={{0,2},{1,3},{2,4},{3,5},{4,6},{5,7},{6,8},{7,9},{8,10},{9,11},{10,... | collective-permute-start | bytes 1769480 | tf_op jit(solution)/shard_map/ppermute | solution.py:187
  20.6 16.1 %collective-permute-start.5 = (bf16[2,384,384]{2,1,0:T(8,128)(2,1)S(1)}, bf16[2,384,384]{2,1,0:T(8,128)(2,1)}, u32[]{:S(2)}, u32[]{:S(2)}) collective-permute-start(bf16[2,384,384]{2,1,0:T(8,128)(2,1)S(1)} %bitcast.21), channel_id=1, source_target_pairs={{0,14},{1,15},{2,0},{3,1},{4,2},{5,3},{6,4},{7,5},{8,6},{9,7},{10,... | collective-permute-start | bytes 1769480 | tf_op jit(solution)/shard_map/ppermute | solution.py:187
  36.6 14.5 %collective-permute-start.1 = (bf16[2,384,384]{2,1,0:T(8,128)(2,1)S(1)}, bf16[2,384,384]{2,1,0:T(8,128)(2,1)S(1)}, u32[]{:S(2)}, u32[]{:S(2)}) collective-permute-start(bf16[2,384,384]{2,1,0:T(8,128)(2,1)S(1)} %collective-permute-done.refs_2_), channel_id=1, source_target_pairs={{0,2},{1,3},{2,4},{3,5},{4,6},{5,7},{6,8},{7,9},{8,10},{9,11},{10,... | collective-permute-start | bytes 1769480 | tf_op jit(solution)/shard_map/ppermute | solution.py:187
  36.6 14.5 %collective-permute-start.6 = (bf16[2,384,384]{2,1,0:T(8,128)(2,1)}, bf16[2,384,384]{2,1,0:T(8,128)(2,1)S(1)}, u32[]{:S(2)}, u32[]{:S(2)}) collective-permute-start(bf16[2,384,384]{2,1,0:T(8,128)(2,1)} %collective-permute-done.5.refs_3_), channel_id=1, source_target_pairs={{0,14},{1,15},{2,0},{3,1},{4,2},{5,3},{6,4},{7,5},{8,6},{9,7},{10,... | collective-permute-start | bytes 1769480 | tf_op jit(solution)/shard_map/ppermute | solution.py:187
  39.9 14.7 %collective-permute-start.16 = (bf16[2,384,384]{2,1,0:T(8,128)(2,1)S(1)}, bf16[2,384,384]{2,1,0:T(8,128)(2,1)S(1)}, u32[]{:S(2)}, u32[]{:S(2)}) collective-permute-start(bf16[2,384,384]{2,1,0:T(8,128)(2,1)S(1)} %bitcast.22), channel_id=1, source_target_pairs={{0,1},{1,0},{2,3},{3,2},{4,5},{5,4},{6,7},{7,6},{8,9},{9,8},{10,11... | collective-permute-start | bytes 1769480 | tf_op jit(solution)/shard_map/ppermute | solution.py:190
  51.1 13.6 %collective-permute-start.2 = (bf16[2,384,384]{2,1,0:T(8,128)(2,1)S(1)}, bf16[2,384,384]{2,1,0:T(8,128)(2,1)S(1)}, u32[]{:S(2)}, u32[]{:S(2)}) collective-permute-start(bf16[2,384,384]{2,1,0:T(8,128)(2,1)S(1)} %collective-permute-done.1.refs_2_), channel_id=1, source_target_pairs={{0,2},{1,3},{2,4},{3,5},{4,6},{5,7},{6,8},{7,9},{8,10},{9,11},{10,... | collective-permute-start | bytes 1769480 | tf_op jit(solution)/shard_map/ppermute | solution.py:187
  51.1 13.7 %collective-permute-start.14 = (bf16[2,384,384]{2,1,0:T(8,128)(2,1)S(1)}, bf16[2,384,384]{2,1,0:T(8,128)(2,1)}, u32[]{:S(2)}, u32[]{:S(2)}) collective-permute-start(bf16[2,384,384]{2,1,0:T(8,128)(2,1)S(1)} %collective-permute-done.refs_2_), channel_id=1, source_target_pairs={{0,1},{1,0},{2,3},{3,2},{4,5},{5,4},{6,7},{7,6},{8,9},{9,8},{10,11... | collective-permute-start | bytes 1769480 | tf_op jit(solution)/shard_map/ppermute | solution.py:190
  51.1 16.5 %collective-permute-start.7 = (bf16[2,384,384]{2,1,0:T(8,128)(2,1)S(1)}, bf16[2,384,384]{2,1,0:T(8,128)(2,1)S(1)}, u32[]{:S(2)}, u32[]{:S(2)}) collective-permute-start(bf16[2,384,384]{2,1,0:T(8,128)(2,1)S(1)} %collective-permute-done.6.refs_3_), channel_id=1, source_target_pairs={{0,14},{1,15},{2,0},{3,1},{4,2},{5,3},{6,4},{7,5},{8,6},{9,7},{10,... | collective-permute-start | bytes 1769480 | tf_op jit(solution)/shard_map/ppermute | solution.py:187
  54.3 13.3 %collective-permute-start.15 = (bf16[2,384,384]{2,1,0:T(8,128)(2,1)}, bf16[2,384,384]{2,1,0:T(8,128)(2,1)}, u32[]{:S(2)}, u32[]{:S(2)}) collective-permute-start(bf16[2,384,384]{2,1,0:T(8,128)(2,1)} %collective-permute-done.5.refs_3_), channel_id=1, source_target_pairs={{0,1},{1,0},{2,3},{3,2},{4,5},{5,4},{6,7},{7,6},{8,9},{9,8},{10,11... | collective-permute-start | bytes 1769480 | tf_op jit(solution)/shard_map/ppermute | solution.py:190
  54.6 0.8 copy-start.2
  55.4 12.4 %collective-permute-start.12 = (bf16[2,384,384]{2,1,0:T(8,128)(2,1)S(1)}, bf16[2,384,384]{2,1,0:T(8,128)(2,1)}, u32[]{:S(2)}, u32[]{:S(2)}) collective-permute-start(bf16[2,384,384]{2,1,0:T(8,128)(2,1)S(1)} %collective-permute-done.1.refs_2_), channel_id=1, source_target_pairs={{0,1},{1,0},{2,3},{3,2},{4,5},{5,4},{6,7},{7,6},{8,9},{9,8},{10,11... | collective-permute-start | bytes 1769480 | tf_op jit(solution)/shard_map/ppermute | solution.py:190
  56.5 2.3 %copy-start = (bf16[2,8,1,384,384]{4,3,2,1,0:T(8,128)(2,1)S(1)}, bf16[2,8,1,384,384]{4,3,2,1,0:T(8,128)(2,1)}, u32[]{:S(2)}) copy-start(bf16[2,8,1,384,384]{4,3,2,1,0:T(8,128)(2,1)} %param.4) | copy-start | bytes 14155780
  58.9 12.7 %copy-start.1 = (bf16[2,8,1,384,384]{4,3,2,1,0:T(8,128)(2,1)S(1)}, bf16[2,8,1,384,384]{4,3,2,1,0:T(8,128)(2,1)}, u32[]{:S(2)}) copy-start(bf16[2,8,1,384,384]{4,3,2,1,0:T(8,128)(2,1)} %param.4) | copy-start | bytes 14155780
  58.9 12.7 %copy-start.3 = (bf16[2,384,384]{2,1,0:T(8,128)(2,1)S(1)}, bf16[2,384,384]{2,1,0:T(8,128)(2,1)}, u32[]{:S(2)}) copy-start(bf16[2,384,384]{2,1,0:T(8,128)(2,1)} %copy-done.2) | copy-start | bytes 1769476
  64.7 21.4 %collective-permute-start.13 = (bf16[2,384,384]{2,1,0:T(8,128)(2,1)S(1)}, bf16[2,384,384]{2,1,0:T(8,128)(2,1)S(1)}, u32[]{:S(2)}, u32[]{:S(2)}) collective-permute-start(bf16[2,384,384]{2,1,0:T(8,128)(2,1)S(1)} %collective-permute-done.6.refs_3_), channel_id=1, source_target_pairs={{0,1},{1,0},{2,3},{3,2},{4,5},{5,4},{6,7},{7,6},{8,9},{9,8},{10,11... | collective-permute-start | bytes 1769480 | tf_op jit(solution)/shard_map/ppermute | solution.py:190
  64.8 29.2 %collective-permute-start.10 = (bf16[2,384,384]{2,1,0:T(8,128)(2,1)S(1)}, bf16[2,384,384]{2,1,0:T(8,128)(2,1)S(1)}, u32[]{:S(2)}, u32[]{:S(2)}) collective-permute-start(bf16[2,384,384]{2,1,0:T(8,128)(2,1)S(1)} %collective-permute-done.2.refs_2_), channel_id=1, source_target_pairs={{0,1},{1,0},{2,3},{3,2},{4,5},{5,4},{6,7},{7,6},{8,9},{9,8},{10,11... | collective-permute-start | bytes 1769480 | tf_op jit(solution)/shard_map/ppermute | solution.py:190
  67.6 26.3 %collective-permute-start.11 = (bf16[2,384,384]{2,1,0:T(8,128)(2,1)S(1)}, bf16[2,384,384]{2,1,0:T(8,128)(2,1)S(1)}, u32[]{:S(2)}, u32[]{:S(2)}) collective-permute-start(bf16[2,384,384]{2,1,0:T(8,128)(2,1)S(1)} %collective-permute-done.7.refs_3_), channel_id=1, source_target_pairs={{0,1},{1,0},{2,3},{3,2},{4,5},{5,4},{6,7},{7,6},{8,9},{9,8},{10,11... | collective-permute-start | bytes 1769480 | tf_op jit(solution)/shard_map/ppermute | solution.py:190
  67.7 12.0 %collective-permute-start.3 = (bf16[384,384]{1,0:T(8,128)(2,1)S(1)}, bf16[384,384]{1,0:T(8,128)(2,1)S(1)}, u32[]{:S(2)}, u32[]{:S(2)}) collective-permute-start(bf16[384,384]{1,0:T(8,128)(2,1)S(1)} %slice_bitcast_fusion.1), channel_id=1, source_target_pairs={{0,2},{1,3},{2,4},{3,5},{4,6},{5,7},{6,8},{7,9},{8,10},{9,11},{10,... | collective-permute-start | bytes 884744 | tf_op jit(solution)/shard_map/ppermute | solution.py:187
  67.8 18.3 %collective-permute-start.8 = (bf16[384,384]{1,0:T(8,128)(2,1)S(1)}, bf16[384,384]{1,0:T(8,128)(2,1)S(1)}, u32[]{:S(2)}, u32[]{:S(2)}) collective-permute-start(bf16[384,384]{1,0:T(8,128)(2,1)S(1)} %slice_bitcast_fusion), channel_id=1, source_target_pairs={{0,14},{1,15},{2,0},{3,1},{4,2},{5,3},{6,4},{7,5},{8,6},{9,7},{10,... | collective-permute-start | bytes 884744 | tf_op jit(solution)/shard_map/ppermute | solution.py:187
  79.6 20.5 %collective-permute-start.4 = (bf16[384,384]{1,0:T(8,128)(2,1)S(1)}, bf16[384,384]{1,0:T(8,128)(2,1)S(1)}, u32[]{:S(2)}, u32[]{:S(2)}) collective-permute-start(bf16[384,384]{1,0:T(8,128)(2,1)S(1)} %collective-permute-done.3.refs_2_), channel_id=1, source_target_pairs={{0,1},{1,0},{2,3},{3,2},{4,5},{5,4},{6,7},{7,6},{8,9},{9,8},{10,11... | collective-permute-start | bytes 884744 | tf_op jit(solution)/shard_map/ppermute | solution.py:190
  86.0 14.1 %collective-permute-start.9 = (bf16[384,384]{1,0:T(8,128)(2,1)S(1)}, bf16[384,384]{1,0:T(8,128)(2,1)S(1)}, u32[]{:S(2)}, u32[]{:S(2)}) collective-permute-start(bf16[384,384]{1,0:T(8,128)(2,1)S(1)} %collective-permute-done.8.refs_3_), channel_id=1, source_target_pairs={{0,1},{1,0},{2,3},{3,2},{4,5},{5,4},{6,7},{7,6},{8,9},{9,8},{10,11... | collective-permute-start | bytes 884744 | tf_op jit(solution)/shard_map/ppermute | solution.py:190

commit v4 on v3

v4 whole, which is shorter than its diff:
```python
import jax
import jax.numpy as jnp
from jax import lax
from jax.experimental import pallas as pl
from jax.experimental.pallas import tpu as pltpu
from jax.sharding import PartitionSpec as P

LIMIT = 16 << 20
OPERATOR, FIRST, LAST, USES, KIND, WHEN, TAKE, TABLE = 0, 16, 32, 48, 64, 80, 88, 128
LEFT, RIGHT, LATE = 0, 1, 2


def dot(left, right, dims):
    return lax.dot_general(left, right, (dims, ((), ())), preferred_element_type=jnp.float32)


def fill_table(table, ids_ref, me, ring, ops_count, positions):
    for slot in range(2 * ring):
        table[USES + slot] = 0
    arrival = []
    for q in range(positions):
        ident = ids_ref[q]
        spin = lax.div(ident, ops_count)
        table[OPERATOR + q] = ident - spin * ops_count
        behind = jnp.bitwise_and((me >> 1) - (spin >> 1), ring - 1)
        slot = 2 * behind + jnp.bitwise_xor(jnp.bitwise_and(me, 1), jnp.bitwise_and(spin, 1))
        count = table[USES + slot]
        table[FIRST + slot] = jnp.where(count == 0, q, table[FIRST + slot])
        table[LAST + slot] = q
        table[USES + slot] = count + 1
        arrival.append(jnp.minimum(behind, ring - behind))
    for p in range(positions // 2):
        left_at, right_at = arrival[2 * p], arrival[2 * p + 1]
        late = right_at > left_at
        table[KIND + 2 * p] = LEFT
        table[KIND + 2 * p + 1] = jnp.where(late, LATE, RIGHT)
        table[TAKE + p] = jnp.where(late, left_at, -1)
        table[WHEN + p] = jnp.where(late, -1, left_at)


def place_weights(parts, weight):
    half = weight.shape[-1] // 2
    for n, (real, imag) in enumerate(parts):
        weight[n, :half, :half] = real[...]
        weight[n, :half, half:] = -imag[...]
        weight[n, half:, :half] = imag[...]
        weight[n, half:, half:] = real[...]


def make_blocks(slots, table, ops_ref, left_ref, right_ref, sum_ref, weight, late_too):
    half = ops_ref.shape[-1]

    def one(at, carry):
        n = at >> 1
        use = jnp.bitwise_and(at, 1)
        slot = jnp.int32(slots[0])
        for other, value in enumerate(slots[1:], 1):
            slot = jnp.where(n == other, value, slot)

        @pl.when(use < table[USES + slot])
        def _():
            q = jnp.where(use == 0, table[FIRST + slot], table[LAST + slot])
            kind = table[KIND + q]
            p = q >> 1

            @pl.when(kind != LATE)
            def _():
                op = table[OPERATOR + q]
                stacked = jnp.concatenate([ops_ref[0, op], ops_ref[1, op]], axis=1)
                block = dot(stacked, weight[n], ((1,), (1,))).astype(jnp.bfloat16)

                @pl.when(kind == LEFT)
                def _():
                    left_ref[p] = block

                @pl.when(kind == RIGHT)
                def _():
                    right_ref[p, :half] = block
                    right_ref[p, half:, :half] = -block[:, half:]
                    right_ref[p, half:, half:] = block[:, :half]

            if late_too:

                @pl.when(kind == LATE)
                def _():
                    product = dot(left_ref[p], weight[n], ((1,), (1,)))
                    sum_ref[0] += product[:, :half]
                    sum_ref[1] += product[:, half:]

        return carry

    lax.fori_loop(0, 2 * len(slots), one, 0)


def take_operators(step, table, ops_ref, left_ref, weight):
    half = ops_ref.shape[-1]

    def pair(p, carry):
        @pl.when(table[TAKE + p] == step)
        def _():
            op = table[OPERATOR + 2 * p + 1]
            weight[0, :half, :half] = ops_ref[0, op]
            weight[0, :half, half:] = ops_ref[1, op]
            weight[0, half:, :half] = -ops_ref[1, op]
            weight[0, half:, half:] = ops_ref[0, op]
            left_ref[p] = dot(left_ref[p], weight[0], ((1,), (0,))).astype(jnp.bfloat16)

        return carry

    lax.fori_loop(0, left_ref.shape[0], pair, 0)


def add_pairs(step, table, left_ref, right_ref, sum_ref, rows):
    half = sum_ref.shape[-1]

    def pair(p, carry):
        @pl.when(table[WHEN + p] == step)
        def _():
            product = dot(left_ref[p, rows], right_ref[p], ((1,), (0,)))
            sum_ref[0, rows] += product[:, :half]
            sum_ref[1, rows] += product[:, half:]

        return carry

    lax.fori_loop(0, left_ref.shape[0], pair, 0)


def work(slots, parts, state, ops, step=None, final=False, begin=None):
    half = ops.shape[-1]
    smem = pl.BlockSpec(memory_space=pltpu.SMEM)
    vmem = pl.BlockSpec(memory_space=pltpu.VMEM)
    arrays = [array for pair in parts for array in pair if array is not None]
    if begin:
        ids, me, ring = begin
        pairs = ids.shape[0] // 2
        operands, in_specs = [ids, me, ops, *arrays], [smem, smem]
        out_shape = [jax.ShapeDtypeStruct((TABLE,), jnp.int32)]
        out_specs, aliases = [smem, vmem, vmem, vmem], {}
    else:
        pairs = state[1].shape[0]
        operands, in_specs = [state[0], ops, *arrays, *state[1:]], []
        out_shape, out_specs = [], [vmem, vmem, vmem]
        aliases = {2 + len(arrays) + n: n for n in range(3)}
    in_specs += [vmem] * (len(operands) - len(in_specs))
    out_shape += [
        jax.ShapeDtypeStruct((pairs, half, 2 * half), jnp.bfloat16),
        jax.ShapeDtypeStruct((pairs, 2 * half, 2 * half), jnp.bfloat16),
        jax.ShapeDtypeStruct((2, half, half), jnp.float32),
    ]
    scratch = [pltpu.VMEM((len(slots), 2 * half, 2 * half), jnp.bfloat16)]
    chunks = 3
    if not begin:
        scratch += [pltpu.SMEM((TABLE,), jnp.int32), pltpu.SemaphoreType.DMA]
    if final:
        out_shape.append(jax.ShapeDtypeStruct((2, half, half), jnp.float32))
        out_specs.append(pl.BlockSpec(memory_space=pl.ANY))
        scratch.append(pltpu.SemaphoreType.DMA((chunks,)))

    def kernel(*refs):
        given = refs[: len(operands)]
        outs = refs[len(operands) : len(operands) + len(out_shape)]
        weight = refs[len(operands) + len(out_shape)]
        if begin:
            ids_ref, me_ref, ops_ref = given[:3]
            at = 3
            table, left_ref, right_ref, sum_ref = outs
            fill_table(table, ids_ref, me_ref[0], ring, ops_ref.shape[1], ids_ref.shape[0])
            sum_ref[...] = jnp.zeros(sum_ref.shape, jnp.float32)
        else:
            ops_ref = given[1]
            at = 2
            table = refs[len(operands) + len(out_shape) + 1]
            fetch = pltpu.make_async_copy(given[0], table, refs[len(operands) + len(out_shape) + 2])
            fetch.start()
            left_ref, right_ref, sum_ref = outs[:3]
        sources = []
        for pair in parts:
            if pair[1] is None:
                sources.append((given[at].at[0], given[at].at[1]))
                at += 1
            else:
                sources.append((given[at], given[at + 1]))
                at += 2
        place_weights(sources, weight)
        if not begin:
            fetch.wait()
        make_blocks(slots, table, ops_ref, left_ref, right_ref, sum_ref, weight, slots[0] > 1)
        if step is None:
            return
        if not final:
            take_operators(step, table, ops_ref, left_ref, weight)
            add_pairs(step, table, left_ref, right_ref, sum_ref, slice(None))
            return
        copies = []
        for n in range(chunks):
            rows = slice(n * half // chunks, (n + 1) * half // chunks)
            add_pairs(step, table, left_ref, right_ref, sum_ref, rows)
            scale = 1.0 / jnp.sqrt(jnp.float32(2 * half * pairs))
            sum_ref[:, rows] = sum_ref[:, rows] * scale
            copies.append(
                pltpu.make_async_copy(
                    sum_ref.at[:, rows], outs[3].at[:, rows], refs[-1].at[n]
                )
            )
            copies[-1].start()
        for copy in copies:
            copy.wait()

    outs = pl.pallas_call(
        kernel,
        out_shape=tuple(out_shape),
        in_specs=in_specs,
        out_specs=tuple(out_specs),
        scratch_shapes=scratch,
        input_output_aliases=aliases,
        compiler_params=pltpu.CompilerParams(vmem_limit_bytes=LIMIT),
        cost_estimate=pl.CostEstimate(
            flops=len(slots) * 8 * half**3, transcendentals=0, bytes_accessed=len(slots) * 4 * half**2
        ),
        name="work",
    )(*operands)
    if final:
        return outs[3]
    return tuple(outs) if begin else (state[0], *outs)


def placed(perambulator, meson_ops, diagram_lists):
    sa_count = lax.axis_size("sa")
    ring = sa_count // 2
    far = ring // 2

    def hop(value, step):
        return lax.ppermute(value, "sa", [(i, (i + 2 * step) % sa_count) for i in range(sa_count)])

    def swap(value):
        return lax.ppermute(value, "sa", [(i, i ^ 1) for i in range(sa_count)])

    ids = diagram_lists.reshape(-1)
    me = lax.axis_index("sa").astype(jnp.int32).reshape(1)
    ops = meson_ops[:, :, 0]
    owned = lax.all_to_all(perambulator, "ta", split_axis=1, concat_axis=3, tiled=True)[:, 0, 0]
    up = {0: owned}
    down = {0: owned}
    for d in range(1, far):
        up[d] = hop(up[d - 1], 1)
        down[d] = hop(down[d - 1], -1)
    up[far] = hop(up[far - 1][0], 1)
    down[far] = hop(down[far - 1][1], -1)
    state = None
    for d in range(far + 1):
        other_up = swap(up[d])
        other_down = swap(down[d]) if d else None
        if d == far:
            own, other = [(up[d], down[d])], [(other_up, other_down)]
            slots = [2 * d]
        elif d:
            own, other = [(up[d], None), (down[d], None)], [(other_up, None), (other_down, None)]
            slots = [2 * d, 2 * (ring - d)]
        else:
            own, other = [(up[d], None)], [(other_up, None)]
            slots = [0]
        state = work(slots, own, state, ops, begin=None if d else (ids, me, ring))
        state = work([s + 1 for s in slots], other, state, ops, step=d, final=d == far)
    return state[:, None, None]


def solution(mesh):
    in_specs = (
        P(None, None, "sa", "ta", None),
        P(None, None, "ta", None, None),
        P("ta", "sa", None),
    )
    out_specs = P(None, "ta", "sa", None, None)
    return jax.shard_map(placed, mesh=mesh, in_specs=in_specs, out_specs=out_specs, check_vma=False)
```

time: 105 us -> 107 us (1.019)
  starting transfers between devices: 24 us -> 25.4 us
    ppermute x9, starting transfers between devices: 7.61 us -> 8.9 us  [swap(): return lax.ppermute(value, 'sa', [(i, i ^ 1) for i in range(sa_count)])]
  transfers between devices with their start and end apart: 17 -> 17, of which waited for: 4 -> 4; matrix products, arithmetic and copies ran while one was open for 1% -> 1% of each run, Pallas kernels for 23% -> 26%
where the time goes in v4:
time: 107 us
  waiting for transfers between devices  29.3 us (27%)
  Pallas kernels  29.2 us (27%)
  starting transfers between devices  25.4 us (24%)
  blocking collectives  17.4 us (16%)
  local copies, waits for them, and re-layouts  5.24 us (5%)
    ppermute x8, waiting for transfers between devices, hop(): lax.ppermute(value, 'sa', [(i, (i + 2 * step) % sa_count) for i in range(...  29.3 us
    pallas_call x10, Pallas kernels, work(): pl.pallas_call(kernel, out_shape=tuple(out_shape), in_specs=in_specs, out...  29.2 us
    all_to_all x1, blocking collectives, placed(): lax.all_to_all(perambulator, 'ta', split_axis=1, concat_axis=3, tiled=True)  17.4 us
    ppermute x8, starting transfers between devices, hop(): lax.ppermute(value, 'sa', [(i, (i + 2 * step) % sa_count) for i in range(...  16.5 us
    ppermute x9, starting transfers between devices, swap(): return lax.ppermute(value, 'sa', [(i, i ^ 1) for i in range(sa_count)])  8.9 us
    unnamed x10, local copies, waits for them, and re-layouts  5.04 us
  transfers between devices with their start and end apart: 17, of which 4 were waited for; matrix products, arithmetic and copies ran while one was open for 1% of the time, Pallas kernels for 26%

profile of v4, /device:TPU:0, one launch (start us, length us, event | category | flops | bytes accessed | tf_op | source)
XLA Modules:
  0.0 107.0 jit_solution(14401082953106769729)
XLA Ops:
  0.0 1.1 %copy.36 = bf16[2,16,1,24,384]{4,3,2,0,1:T(8,128)(2,1)S(1)} copy(bf16[2,16,1,24,384]{4,3,2,1,0:T(8,128)(2,1)} %param.3) | data formatting | bytes 1179648 | tf_op args[0]
  1.1 17.4 %all_to_all.4 = bf16[2,16,1,24,384]{4,3,2,0,1:T(8,128)(2,1)S(1)} all-to-all(bf16[2,16,1,24,384]{4,3,2,0,1:T(8,128)(2,1)S(1)} %copy.36), channel_id=1, replica_groups=mesh['ta'=16,'sa'=16] {'ta'}, dimensions={1} | all-to-all | bytes 1179648 | tf_op jit(solution)/shard_map/all_to_all | solution.py:241
  18.5 0.1 copy.37
  18.6 2.0 %collective-permute-start = (bf16[2,384,384]{2,1,0:T(8,128)(2,1)S(1)}, bf16[2,384,384]{2,1,0:T(8,128)(2,1)S(1)}, u32[]{:S(2)}, u32[]{:S(2)}) collective-permute-start(bf16[2,384,384]{2,1,0:T(8,128)(2,1)S(1)} %bitcast.20), channel_id=1, source_target_pairs={{0,2},{1,3},{2,4},{3,5},{4,6},{5,7},{6,8},{7,9},{8,10},{9,11},{10,... | collective-permute-start | bytes 1769480 | tf_op jit(solution)/shard_map/ppermute | solution.py:233
  20.6 4.0 %collective-permute-start.5 = (bf16[2,384,384]{2,1,0:T(8,128)(2,1)S(1)}, bf16[2,384,384]{2,1,0:T(8,128)(2,1)}, u32[]{:S(2)}, u32[]{:S(2)}) collective-permute-start(bf16[2,384,384]{2,1,0:T(8,128)(2,1)S(1)} %bitcast.21), channel_id=1, source_target_pairs={{0,14},{1,15},{2,0},{3,1},{4,2},{5,3},{6,4},{7,5},{8,6},{9,7},{10,... | collective-permute-start | bytes 1769480 | tf_op jit(solution)/shard_map/ppermute | solution.py:233
  24.6 12.0 %collective-permute-done.refs_2_ = bf16[2,384,384]{2,1,0:T(8,128)(2,1)S(1)} collective-permute-done((bf16[2,384,384]{2,1,0:T(8,128)(2,1)S(1)}, bf16[2,384,384]{2,1,0:T(8,128)(2,1)S(1)}, u32[]{:S(2)}, u32[]{:S(2)}) %collective-permute-start) | collective-permute-done | bytes 589856 | tf_op jit(solution)/shard_map/ppermute | solution.py:233
  36.6 0.0 collective-permute-start.1
  36.6 0.0 collective-permute-done.5.refs_3_
  36.6 3.2 %collective-permute-start.6 = (bf16[2,384,384]{2,1,0:T(8,128)(2,1)}, bf16[2,384,384]{2,1,0:T(8,128)(2,1)S(1)}, u32[]{:S(2)}, u32[]{:S(2)}) collective-permute-start(bf16[2,384,384]{2,1,0:T(8,128)(2,1)} %collective-permute-done.5.refs_3_), channel_id=1, source_target_pairs={{0,14},{1,15},{2,0},{3,1},{4,2},{5,3},{6,4},{7,5},{8,6},{9,7},{10,... | collective-permute-start | bytes 1769480 | tf_op jit(solution)/shard_map/ppermute | solution.py:233
  39.9 0.0 collective-permute-start.16
  39.9 11.2 %collective-permute-done.1.refs_2_ = bf16[2,384,384]{2,1,0:T(8,128)(2,1)S(1)} collective-permute-done((bf16[2,384,384]{2,1,0:T(8,128)(2,1)S(1)}, bf16[2,384,384]{2,1,0:T(8,128)(2,1)S(1)}, u32[]{:S(2)}, u32[]{:S(2)}) %collective-permute-start.1) | collective-permute-done | bytes 589856 | tf_op jit(solution)/shard_map/ppermute | solution.py:233
  51.1 0.0 collective-permute-start.2
  51.1 0.0 collective-permute-start.14
  51.1 0.0 collective-permute-done.6.refs_3_
  51.1 3.2 %collective-permute-start.7 = (bf16[2,384,384]{2,1,0:T(8,128)(2,1)S(1)}, bf16[2,384,384]{2,1,0:T(8,128)(2,1)S(1)}, u32[]{:S(2)}, u32[]{:S(2)}) collective-permute-start(bf16[2,384,384]{2,1,0:T(8,128)(2,1)S(1)} %collective-permute-done.6.refs_3_), channel_id=1, source_target_pairs={{0,14},{1,15},{2,0},{3,1},{4,2},{5,3},{6,4},{7,5},{8,6},{9,7},{10,... | collective-permute-start | bytes 1769480 | tf_op jit(solution)/shard_map/ppermute | solution.py:233
  54.3 0.2 collective-permute-start.15
  54.6 0.0 collective-permute-done.16.refs_2_
  54.6 0.8 copy-done.2
  55.4 0.3 collective-permute-start.12
  55.7 0.8 copy.35
  56.4 0.1 reshape.10.refs_0_
  56.5 2.3 %copy-done = bf16[2,8,1,384,384]{4,3,2,1,0:T(8,128)(2,1)S(1)} copy-done((bf16[2,8,1,384,384]{4,3,2,1,0:T(8,128)(2,1)S(1)}, bf16[2,8,1,384,384]{4,3,2,1,0:T(8,128)(2,1)}, u32[]{:S(2)}) %copy-start) | copy-done | bytes 4718616
  58.9 2.1 %work.10 = (s32[128]{0:T(128)S(1)}, bf16[8,384,768]{2,1,0:T(8,128)(2,1)S(1)}, bf16[8,768,768]{2,1,0:T(8,128)(2,1)S(1)}, f32[2,384,384]{2,1,0:T(8,128)S(1)}) custom-call(s32[16]{0:T(128)S(1)} %reshape.10.refs_0_, s32[1]{0:T(128)} %bitcast.refs_1_, bf16[2,8,384,384]{3,2,1,0:T(8,128)(2,1)S(1)} %bitcast.10, bf16[2,384,384]{2,1,0:T(8,128)(2,1)S(1)} %bitcast.23), custom_call_target="tpu_custom_call" | custom-call | flops 452984832 | bytes 589824 | tf_op jit(solution)/shard_map/work/pallas_call | solution.py:209
  60.9 3.8 %collective-permute-done.2.refs_2_ = bf16[2,384,384]{2,1,0:T(8,128)(2,1)S(1)} collective-permute-done((bf16[2,384,384]{2,1,0:T(8,128)(2,1)S(1)}, bf16[2,384,384]{2,1,0:T(8,128)(2,1)S(1)}, u32[]{:S(2)}, u32[]{:S(2)}) %collective-permute-start.2) | collective-permute-done | bytes 589856 | tf_op jit(solution)/shard_map/ppermute | solution.py:233
  64.7 0.0 collective-permute-start.13
  64.8 0.0 collective-permute-done.14.refs_2_
  64.8 0.6 collective-permute-start.10
  65.4 2.2 %collective-permute-done.7.refs_3_ = bf16[2,384,384]{2,1,0:T(8,128)(2,1)S(1)} collective-permute-done((bf16[2,384,384]{2,1,0:T(8,128)(2,1)S(1)}, bf16[2,384,384]{2,1,0:T(8,128)(2,1)S(1)}, u32[]{:S(2)}, u32[]{:S(2)}) %collective-permute-start.7) | collective-permute-done | bytes 589856 | tf_op jit(solution)/shard_map/ppermute | solution.py:233
  67.6 0.0 collective-permute-start.11
  67.6 0.0 collective-permute-done.15.refs_3_
  67.7 0.1 collective-permute-start.3
  67.7 0.0 collective-permute-done.12.refs_2_
  67.8 3.9 %collective-permute-start.8 = (bf16[384,384]{1,0:T(8,128)(2,1)S(1)}, bf16[384,384]{1,0:T(8,128)(2,1)S(1)}, u32[]{:S(2)}, u32[]{:S(2)}) collective-permute-start(bf16[384,384]{1,0:T(8,128)(2,1)S(1)} %slice_bitcast_fusion), channel_id=1, source_target_pairs={{0,14},{1,15},{2,0},{3,1},{4,2},{5,3},{6,4},{7,5},{8,6},{9,7},{10,... | collective-permute-start | bytes 884744 | tf_op jit(solution)/shard_map/ppermute | solution.py:233
  71.7 2.2 %work.11 = (bf16[8,384,768]{2,1,0:T(8,128)(2,1)S(1)}, bf16[8,768,768]{2,1,0:T(8,128)(2,1)S(1)}, f32[2,384,384]{2,1,0:T(8,128)S(1)}) custom-call(s32[128]{0:T(128)S(1)} %get-tuple-element.34.refs_0_, bf16[2,8,384,384]{3,2,1,0:T(8,128)(2,1)S(1)} %bitcast.11, ...), custom_call_target="tpu_custom_call", output_to_operand_aliasing={{0}: (3, {}), {1}: (4, {}), {2}: (5, {})} | custom-call | flops 452984832 | bytes 589824 | tf_op jit(solution)/shard_map/work/pallas_call | solution.py:209
  73.9 2.5 %work.12 = (bf16[8,384,768]{2,1,0:T(8,128)(2,1)S(1)}, bf16[8,768,768]{2,1,0:T(8,128)(2,1)S(1)}, f32[2,384,384]{2,1,0:T(8,128)S(1)}) custom-call(s32[128]{0:T(128)S(1)} %get-tuple-element.34.refs_0_, bf16[2,8,384,384]{3,2,1,0:T(8,128)(2,1)S(1)} %bitcast.12, ...), custom_call_target="tpu_custom_call", output_to_operand_aliasing={{0}: (4, {}), {1}: (5, {}), {2}: (6, {})} | custom-call | flops 905969664 | bytes 1179648 | tf_op jit(solution)/shard_map/work/pallas_call | solution.py:209
  76.4 3.6 %work.13 = (bf16[8,384,768]{2,1,0:T(8,128)(2,1)S(1)}, bf16[8,768,768]{2,1,0:T(8,128)(2,1)S(1)}, f32[2,384,384]{2,1,0:T(8,128)S(1)}) custom-call(s32[128]{0:T(128)S(1)} %get-tuple-element.34.refs_0_, bf16[2,8,384,384]{3,2,1,0:T(8,128)(2,1)S(1)} %bitcast.13, ...), custom_call_target="tpu_custom_call", output_to_operand_aliasing={{0}: (4, {}), {1}: (5, {}), {2}: (6, {})} | custom-call | flops 905969664 | bytes 1179648 | tf_op jit(solution)/shard_map/work/pallas_call | solution.py:209
  80.0 0.6 work.14
  80.6 0.0 collective-permute-done.3.refs_2_
  80.6 7.5 %collective-permute-start.4 = (bf16[384,384]{1,0:T(8,128)(2,1)S(1)}, bf16[384,384]{1,0:T(8,128)(2,1)S(1)}, u32[]{:S(2)}, u32[]{:S(2)}) collective-permute-start(bf16[384,384]{1,0:T(8,128)(2,1)S(1)} %collective-permute-done.3.refs_2_), channel_id=1, source_target_pairs={{0,1},{1,0},{2,3},{3,2},{4,5},{5,4},{6,7},{7,6},{8,9},{9,8},{10,11... | collective-permute-start | bytes 884744 | tf_op jit(solution)/shard_map/ppermute | solution.py:236
  88.1 0.3 collective-permute-start.9
  88.4 5.4 %work.15 = (bf16[8,384,768]{2,1,0:T(8,128)(2,1)S(1)}, bf16[8,768,768]{2,1,0:T(8,128)(2,1)S(1)}, f32[2,384,384]{2,1,0:T(8,128)S(1)}) custom-call(s32[128]{0:T(128)S(1)} %get-tuple-element.34.refs_0_, bf16[2,8,384,384]{3,2,1,0:T(8,128)(2,1)S(1)} %bitcast.15, ...), custom_call_target="tpu_custom_call", output_to_operand_aliasing={{0}: (4, {}), {1}: (5, {}), {2}: (6, {})} | custom-call | flops 905969664 | bytes 1179648 | tf_op jit(solution)/shard_map/work/pallas_call | solution.py:209
  93.8 2.8 %work.16 = (bf16[8,384,768]{2,1,0:T(8,128)(2,1)S(1)}, bf16[8,768,768]{2,1,0:T(8,128)(2,1)S(1)}, f32[2,384,384]{2,1,0:T(8,128)S(1)}) custom-call(s32[128]{0:T(128)S(1)} %get-tuple-element.34.refs_0_, bf16[2,8,384,384]{3,2,1,0:T(8,128)(2,1)S(1)} %bitcast.16, ...), custom_call_target="tpu_custom_call", output_to_operand_aliasing={{0}: (4, {}), {1}: (5, {}), {2}: (6, {})} | custom-call | flops 905969664 | bytes 1179648 | tf_op jit(solution)/shard_map/work/pallas_call | solution.py:209
  96.6 0.0 collective-permute-done.10.refs_2_
  96.6 7.0 %work.17 = (bf16[8,384,768]{2,1,0:T(8,128)(2,1)S(1)}, bf16[8,768,768]{2,1,0:T(8,128)(2,1)S(1)}, f32[2,384,384]{2,1,0:T(8,128)S(1)}) custom-call(s32[128]{0:T(128)S(1)} %get-tuple-element.34.refs_0_, bf16[2,8,384,384]{3,2,1,0:T(8,128)(2,1)S(1)} %bitcast.17, ...), custom_call_target="tpu_custom_call", output_to_operand_aliasing={{0}: (4, {}), {1}: (5, {}), {2}: (6, {})} | custom-call | flops 905969664 | bytes 1179648 | tf_op jit(solution)/shard_map/work/pallas_call | solution.py:209
  103.7 1.3 %work.18 = (bf16[8,384,768]{2,1,0:T(8,128)(2,1)S(1)}, bf16[8,768,768]{2,1,0:T(8,128)(2,1)S(1)}, f32[2,384,384]{2,1,0:T(8,128)S(1)}) custom-call(s32[128]{0:T(128)S(1)} %get-tuple-element.34.refs_0_, bf16[2,8,384,384]{3,2,1,0:T(8,128)(2,1)S(1)} %bitcast.18, ...), custom_call_target="tpu_custom_call", output_to_operand_aliasing={{0}: (4, {}), {1}: (5, {}), {2}: (6, {})} | custom-call | flops 452984832 | bytes 589824 | tf_op jit(solution)/shard_map/work/pallas_call | solution.py:209
  105.0 0.0 collective-permute-done.4.refs_2_
  105.0 0.0 collective-permute-done.9.refs_3_
  105.0 1.8 %work.19 = (bf16[8,384,768]{2,1,0:T(8,128)(2,1)S(1)}, bf16[8,768,768]{2,1,0:T(8,128)(2,1)S(1)}, f32[2,384,384]{2,1,0:T(8,128)S(1)}, f32[2,384,384]{2,1,0:T(8,128)}) custom-call(s32[128]{0:T(128)S(1)} %get-tuple-element.34.refs_0_, bf16[2,8,384,384]{3,2,1,0:T(8,128)(2,1)S(1)} %bitcast.19, ...), custom_call_target="tpu_custom_call", output_to_operand_aliasing={{0}: (4, {}), {1}: (5, {}), {2}: (6, {})} | custom-call | flops 452984832 | bytes 589824 | tf_op jit(solution)/shard_map/work/pallas_call | solution.py:209
  (11 shorter events, 0.1 us)
Async XLA Ops:
  18.6 18.0 %collective-permute-start = (bf16[2,384,384]{2,1,0:T(8,128)(2,1)S(1)}, bf16[2,384,384]{2,1,0:T(8,128)(2,1)S(1)}, u32[]{:S(2)}, u32[]{:S(2)}) collective-permute-start(bf16[2,384,384]{2,1,0:T(8,128)(2,1)S(1)} %bitcast.20), channel_id=1, source_target_pairs={{0,2},{1,3},{2,4},{3,5},{4,6},{5,7},{6,8},{7,9},{8,10},{9,11},{10,... | collective-permute-start | bytes 1769480 | tf_op jit(solution)/shard_map/ppermute | solution.py:233
  20.6 16.1 %collective-permute-start.5 = (bf16[2,384,384]{2,1,0:T(8,128)(2,1)S(1)}, bf16[2,384,384]{2,1,0:T(8,128)(2,1)}, u32[]{:S(2)}, u32[]{:S(2)}) collective-permute-start(bf16[2,384,384]{2,1,0:T(8,128)(2,1)S(1)} %bitcast.21), channel_id=1, source_target_pairs={{0,14},{1,15},{2,0},{3,1},{4,2},{5,3},{6,4},{7,5},{8,6},{9,7},{10,... | collective-permute-start | bytes 1769480 | tf_op jit(solution)/shard_map/ppermute | solution.py:233
  36.6 14.5 %collective-permute-start.1 = (bf16[2,384,384]{2,1,0:T(8,128)(2,1)S(1)}, bf16[2,384,384]{2,1,0:T(8,128)(2,1)S(1)}, u32[]{:S(2)}, u32[]{:S(2)}) collective-permute-start(bf16[2,384,384]{2,1,0:T(8,128)(2,1)S(1)} %collective-permute-done.refs_2_), channel_id=1, source_target_pairs={{0,2},{1,3},{2,4},{3,5},{4,6},{5,7},{6,8},{7,9},{8,10},{9,11},{10,... | collective-permute-start | bytes 1769480 | tf_op jit(solution)/shard_map/ppermute | solution.py:233
  36.6 14.5 %collective-permute-start.6 = (bf16[2,384,384]{2,1,0:T(8,128)(2,1)}, bf16[2,384,384]{2,1,0:T(8,128)(2,1)S(1)}, u32[]{:S(2)}, u32[]{:S(2)}) collective-permute-start(bf16[2,384,384]{2,1,0:T(8,128)(2,1)} %collective-permute-done.5.refs_3_), channel_id=1, source_target_pairs={{0,14},{1,15},{2,0},{3,1},{4,2},{5,3},{6,4},{7,5},{8,6},{9,7},{10,... | collective-permute-start | bytes 1769480 | tf_op jit(solution)/shard_map/ppermute | solution.py:233
  39.9 14.7 %collective-permute-start.16 = (bf16[2,384,384]{2,1,0:T(8,128)(2,1)S(1)}, bf16[2,384,384]{2,1,0:T(8,128)(2,1)S(1)}, u32[]{:S(2)}, u32[]{:S(2)}) collective-permute-start(bf16[2,384,384]{2,1,0:T(8,128)(2,1)S(1)} %bitcast.22), channel_id=1, source_target_pairs={{0,1},{1,0},{2,3},{3,2},{4,5},{5,4},{6,7},{7,6},{8,9},{9,8},{10,11... | collective-permute-start | bytes 1769480 | tf_op jit(solution)/shard_map/ppermute | solution.py:236
  51.1 13.6 %collective-permute-start.2 = (bf16[2,384,384]{2,1,0:T(8,128)(2,1)S(1)}, bf16[2,384,384]{2,1,0:T(8,128)(2,1)S(1)}, u32[]{:S(2)}, u32[]{:S(2)}) collective-permute-start(bf16[2,384,384]{2,1,0:T(8,128)(2,1)S(1)} %collective-permute-done.1.refs_2_), channel_id=1, source_target_pairs={{0,2},{1,3},{2,4},{3,5},{4,6},{5,7},{6,8},{7,9},{8,10},{9,11},{10,... | collective-permute-start | bytes 1769480 | tf_op jit(solution)/shard_map/ppermute | solution.py:233
  51.1 13.7 %collective-permute-start.14 = (bf16[2,384,384]{2,1,0:T(8,128)(2,1)S(1)}, bf16[2,384,384]{2,1,0:T(8,128)(2,1)}, u32[]{:S(2)}, u32[]{:S(2)}) collective-permute-start(bf16[2,384,384]{2,1,0:T(8,128)(2,1)S(1)} %collective-permute-done.refs_2_), channel_id=1, source_target_pairs={{0,1},{1,0},{2,3},{3,2},{4,5},{5,4},{6,7},{7,6},{8,9},{9,8},{10,11... | collective-permute-start | bytes 1769480 | tf_op jit(solution)/shard_map/ppermute | solution.py:236
  51.1 16.5 %collective-permute-start.7 = (bf16[2,384,384]{2,1,0:T(8,128)(2,1)S(1)}, bf16[2,384,384]{2,1,0:T(8,128)(2,1)S(1)}, u32[]{:S(2)}, u32[]{:S(2)}) collective-permute-start(bf16[2,384,384]{2,1,0:T(8,128)(2,1)S(1)} %collective-permute-done.6.refs_3_), channel_id=1, source_target_pairs={{0,14},{1,15},{2,0},{3,1},{4,2},{5,3},{6,4},{7,5},{8,6},{9,7},{10,... | collective-permute-start | bytes 1769480 | tf_op jit(solution)/shard_map/ppermute | solution.py:233
  54.3 13.3 %collective-permute-start.15 = (bf16[2,384,384]{2,1,0:T(8,128)(2,1)}, bf16[2,384,384]{2,1,0:T(8,128)(2,1)}, u32[]{:S(2)}, u32[]{:S(2)}) collective-permute-start(bf16[2,384,384]{2,1,0:T(8,128)(2,1)} %collective-permute-done.5.refs_3_), channel_id=1, source_target_pairs={{0,1},{1,0},{2,3},{3,2},{4,5},{5,4},{6,7},{7,6},{8,9},{9,8},{10,11... | collective-permute-start | bytes 1769480 | tf_op jit(solution)/shard_map/ppermute | solution.py:236
  54.6 0.8 copy-start.2
  55.4 12.4 %collective-permute-start.12 = (bf16[2,384,384]{2,1,0:T(8,128)(2,1)S(1)}, bf16[2,384,384]{2,1,0:T(8,128)(2,1)}, u32[]{:S(2)}, u32[]{:S(2)}) collective-permute-start(bf16[2,384,384]{2,1,0:T(8,128)(2,1)S(1)} %collective-permute-done.1.refs_2_), channel_id=1, source_target_pairs={{0,1},{1,0},{2,3},{3,2},{4,5},{5,4},{6,7},{7,6},{8,9},{9,8},{10,11... | collective-permute-start | bytes 1769480 | tf_op jit(solution)/shard_map/ppermute | solution.py:236
  56.5 2.3 %copy-start = (bf16[2,8,1,384,384]{4,3,2,1,0:T(8,128)(2,1)S(1)}, bf16[2,8,1,384,384]{4,3,2,1,0:T(8,128)(2,1)}, u32[]{:S(2)}) copy-start(bf16[2,8,1,384,384]{4,3,2,1,0:T(8,128)(2,1)} %param.4) | copy-start | bytes 14155780
  58.9 12.9 %copy-start.1 = (bf16[2,8,1,384,384]{4,3,2,1,0:T(8,128)(2,1)S(1)}, bf16[2,8,1,384,384]{4,3,2,1,0:T(8,128)(2,1)}, u32[]{:S(2)}) copy-start(bf16[2,8,1,384,384]{4,3,2,1,0:T(8,128)(2,1)} %param.4) | copy-start | bytes 14155780
  58.9 12.9 %copy-start.3 = (bf16[2,384,384]{2,1,0:T(8,128)(2,1)S(1)}, bf16[2,384,384]{2,1,0:T(8,128)(2,1)}, u32[]{:S(2)}) copy-start(bf16[2,384,384]{2,1,0:T(8,128)(2,1)} %copy-done.2) | copy-start | bytes 1769476
  64.7 23.7 %collective-permute-start.13 = (bf16[2,384,384]{2,1,0:T(8,128)(2,1)S(1)}, bf16[2,384,384]{2,1,0:T(8,128)(2,1)S(1)}, u32[]{:S(2)}, u32[]{:S(2)}) collective-permute-start(bf16[2,384,384]{2,1,0:T(8,128)(2,1)S(1)} %collective-permute-done.6.refs_3_), channel_id=1, source_target_pairs={{0,1},{1,0},{2,3},{3,2},{4,5},{5,4},{6,7},{7,6},{8,9},{9,8},{10,11... | collective-permute-start | bytes 1769480 | tf_op jit(solution)/shard_map/ppermute | solution.py:236
  64.8 31.8 %collective-permute-start.10 = (bf16[2,384,384]{2,1,0:T(8,128)(2,1)S(1)}, bf16[2,384,384]{2,1,0:T(8,128)(2,1)S(1)}, u32[]{:S(2)}, u32[]{:S(2)}) collective-permute-start(bf16[2,384,384]{2,1,0:T(8,128)(2,1)S(1)} %collective-permute-done.2.refs_2_), channel_id=1, source_target_pairs={{0,1},{1,0},{2,3},{3,2},{4,5},{5,4},{6,7},{7,6},{8,9},{9,8},{10,11... | collective-permute-start | bytes 1769480 | tf_op jit(solution)/shard_map/ppermute | solution.py:236
  67.6 29.0 %collective-permute-start.11 = (bf16[2,384,384]{2,1,0:T(8,128)(2,1)S(1)}, bf16[2,384,384]{2,1,0:T(8,128)(2,1)S(1)}, u32[]{:S(2)}, u32[]{:S(2)}) collective-permute-start(bf16[2,384,384]{2,1,0:T(8,128)(2,1)S(1)} %collective-permute-done.7.refs_3_), channel_id=1, source_target_pairs={{0,1},{1,0},{2,3},{3,2},{4,5},{5,4},{6,7},{7,6},{8,9},{9,8},{10,11... | collective-permute-start | bytes 1769480 | tf_op jit(solution)/shard_map/ppermute | solution.py:236
  67.7 12.9 %collective-permute-start.3 = (bf16[384,384]{1,0:T(8,128)(2,1)S(1)}, bf16[384,384]{1,0:T(8,128)(2,1)S(1)}, u32[]{:S(2)}, u32[]{:S(2)}) collective-permute-start(bf16[384,384]{1,0:T(8,128)(2,1)S(1)} %slice_bitcast_fusion.1), channel_id=1, source_target_pairs={{0,2},{1,3},{2,4},{3,5},{4,6},{5,7},{6,8},{7,9},{8,10},{9,11},{10,... | collective-permute-start | bytes 884744 | tf_op jit(solution)/shard_map/ppermute | solution.py:233
  67.8 20.3 %collective-permute-start.8 = (bf16[384,384]{1,0:T(8,128)(2,1)S(1)}, bf16[384,384]{1,0:T(8,128)(2,1)S(1)}, u32[]{:S(2)}, u32[]{:S(2)}) collective-permute-start(bf16[384,384]{1,0:T(8,128)(2,1)S(1)} %slice_bitcast_fusion), channel_id=1, source_target_pairs={{0,14},{1,15},{2,0},{3,1},{4,2},{5,3},{6,4},{7,5},{8,6},{9,7},{10,... | collective-permute-start | bytes 884744 | tf_op jit(solution)/shard_map/ppermute | solution.py:233
  80.6 24.4 %collective-permute-start.4 = (bf16[384,384]{1,0:T(8,128)(2,1)S(1)}, bf16[384,384]{1,0:T(8,128)(2,1)S(1)}, u32[]{:S(2)}, u32[]{:S(2)}) collective-permute-start(bf16[384,384]{1,0:T(8,128)(2,1)S(1)} %collective-permute-done.3.refs_2_), channel_id=1, source_target_pairs={{0,1},{1,0},{2,3},{3,2},{4,5},{5,4},{6,7},{7,6},{8,9},{9,8},{10,11... | collective-permute-start | bytes 884744 | tf_op jit(solution)/shard_map/ppermute | solution.py:236
  88.1 16.9 %collective-permute-start.9 = (bf16[384,384]{1,0:T(8,128)(2,1)S(1)}, bf16[384,384]{1,0:T(8,128)(2,1)S(1)}, u32[]{:S(2)}, u32[]{:S(2)}) collective-permute-start(bf16[384,384]{1,0:T(8,128)(2,1)S(1)} %collective-permute-done.8.refs_3_), channel_id=1, source_target_pairs={{0,1},{1,0},{2,3},{3,2},{4,5},{5,4},{6,7},{7,6},{8,9},{9,8},{10,11... | collective-permute-start | bytes 884744 | tf_op jit(solution)/shard_map/ppermute | solution.py:236

commit v5 on v4

--- a/solution.py
+++ b/solution.py
@@ -6,36 +6,59 @@
 from jax.sharding import PartitionSpec as P
 
 LIMIT = 16 << 20
-OPERATOR, FIRST, LAST, USES, KIND, WHEN, TAKE, TABLE = 0, 16, 32, 48, 64, 80, 88, 128
+FIRST, LAST, USES, SCALARS = 0, 16, 32, 128
+WHEN, TAKE, OPERATORS = 16, 24, 32
 LEFT, RIGHT, LATE = 0, 1, 2
+ROW, LANES = 8, 128
 
 
 def dot(left, right, dims):
     return lax.dot_general(left, right, (dims, ((), ())), preferred_element_type=jnp.float32)
 
 
-def fill_table(table, ids_ref, me, ring, ops_count, positions):
+def fill_table(table, scalars, ids_ref, me, ring, ops_count, positions):
     for slot in range(2 * ring):
-        table[USES + slot] = 0
-    arrival = []
+        scalars[FIRST + slot] = 0
+        scalars[LAST + slot] = 0
+        scalars[USES + slot] = 0
+    arrival, operators = [], []
     for q in range(positions):
         ident = ids_ref[q]
         spin = lax.div(ident, ops_count)
-        table[OPERATOR + q] = ident - spin * ops_count
+        operators.append(ident - spin * ops_count)
         behind = jnp.bitwise_and((me >> 1) - (spin >> 1), ring - 1)
         slot = 2 * behind + jnp.bitwise_xor(jnp.bitwise_and(me, 1), jnp.bitwise_and(spin, 1))
-        count = table[USES + slot]
-        table[FIRST + slot] = jnp.where(count == 0, q, table[FIRST + slot])
-        table[LAST + slot] = q
-        table[USES + slot] = count + 1
         arrival.append(jnp.minimum(behind, ring - behind))
+        count = scalars[USES + slot]
+        scalars[USES + slot] = count + 1
+        scalars[FIRST + slot] = jnp.where(count == 0, q, scalars[FIRST + slot])
+        scalars[LAST + slot] = q
+    steps = ring // 2 + 1
+    when, take = [jnp.int32(0)] * steps, [jnp.int32(0)] * steps
+    taken = jnp.int32(0)
     for p in range(positions // 2):
         left_at, right_at = arrival[2 * p], arrival[2 * p + 1]
         late = right_at > left_at
-        table[KIND + 2 * p] = LEFT
-        table[KIND + 2 * p + 1] = jnp.where(late, LATE, RIGHT)
-        table[TAKE + p] = jnp.where(late, left_at, -1)
-        table[WHEN + p] = jnp.where(late, -1, left_at)
+        entry = p * 8 + operators[2 * p]
+        scalars[48 + 2 * p] = LEFT * 64 + entry
+        entry = p * 8 + operators[2 * p + 1]
+        scalars[48 + 2 * p + 1] = jnp.where(late, LATE * 64, RIGHT * 64) + entry
+        taken = taken + (operators[2 * p + 1] << (3 * p))
+        for d in range(steps):
+            at = left_at == d
+            when[d] = when[d] + jnp.where(at & jnp.logical_not(late), 1 << p, 0)
+            take[d] = take[d] + jnp.where(at & late, 1 << p, 0)
+    lane = lax.broadcasted_iota(jnp.int32, (ROW, LANES), 1)
+    row = jnp.zeros((ROW, LANES), jnp.int32)
+    for slot in range(2 * ring):
+        one = scalars[48 + scalars[FIRST + slot]]
+        two = scalars[48 + scalars[LAST + slot]]
+        packed = scalars[USES + slot] + (one << 2) + (two << 10)
+        row = jnp.where(lane == slot, packed, row)
+    for d in range(steps):
+        row = jnp.where(lane == WHEN + d, when[d], row)
+        row = jnp.where(lane == TAKE + d, take[d], row)
+    table[...] = jnp.where(lane == OPERATORS, taken, row)
 
 
 def place_weights(parts, weight):
@@ -47,25 +70,25 @@
         weight[n, half:, half:] = real[...]
 
 
-def make_blocks(slots, table, ops_ref, left_ref, right_ref, sum_ref, weight, late_too):
+def make_blocks(entries, ops_ref, left_ref, right_ref, sum_ref, weight, late_too):
     half = ops_ref.shape[-1]
 
     def one(at, carry):
         n = at >> 1
         use = jnp.bitwise_and(at, 1)
-        slot = jnp.int32(slots[0])
-        for other, value in enumerate(slots[1:], 1):
-            slot = jnp.where(n == other, value, slot)
-
-        @pl.when(use < table[USES + slot])
+        packed = entries[0]
+        for other, value in enumerate(entries[1:], 1):
+            packed = jnp.where(n == other, value, packed)
+
+        @pl.when(use < jnp.bitwise_and(packed, 3))
         def _():
-            q = jnp.where(use == 0, table[FIRST + slot], table[LAST + slot])
-            kind = table[KIND + q]
-            p = q >> 1
+            entry = jnp.bitwise_and(jnp.where(use == 0, packed >> 2, packed >> 10), 255)
+            kind = entry >> 6
+            p = jnp.bitwise_and(entry >> 3, 7)
 
             @pl.when(kind != LATE)
             def _():
-                op = table[OPERATOR + q]
+                op = jnp.bitwise_and(entry, 7)
                 stacked = jnp.concatenate([ops_ref[0, op], ops_ref[1, op]], axis=1)
                 block = dot(stacked, weight[n], ((1,), (1,))).astype(jnp.bfloat16)
 
@@ -89,16 +112,16 @@
 
         return carry
 
-    lax.fori_loop(0, 2 * len(slots), one, 0)
-
-
-def take_operators(step, table, ops_ref, left_ref, weight):
+    lax.fori_loop(0, 2 * len(entries), one, 0)
+
+
+def take_operators(mask, operators, ops_ref, left_ref, weight):
     half = ops_ref.shape[-1]
 
     def pair(p, carry):
-        @pl.when(table[TAKE + p] == step)
+        @pl.when(jnp.bitwise_and(mask >> p, 1) == 1)
         def _():
-            op = table[OPERATOR + 2 * p + 1]
+            op = jnp.bitwise_and(operators >> (3 * p), 7)
             weight[0, :half, :half] = ops_ref[0, op]
             weight[0, :half, half:] = ops_ref[1, op]
             weight[0, half:, :half] = -ops_ref[1, op]
@@ -107,14 +130,16 @@
 
         return carry
 
-    lax.fori_loop(0, left_ref.shape[0], pair, 0)
-
-
-def add_pairs(step, table, left_ref, right_ref, sum_ref, rows):
+    @pl.when(mask > 0)
+    def _():
+        lax.fori_loop(0, left_ref.shape[0], pair, 0)
+
+
+def add_pairs(mask, left_ref, right_ref, sum_ref, rows):
     half = sum_ref.shape[-1]
 
     def pair(p, carry):
-        @pl.when(table[WHEN + p] == step)
+        @pl.when(jnp.bitwise_and(mask >> p, 1) == 1)
         def _():
             product = dot(left_ref[p, rows], right_ref[p], ((1,), (0,)))
             sum_ref[0, rows] += product[:, :half]
@@ -122,7 +147,9 @@
 
         return carry
 
-    lax.fori_loop(0, left_ref.shape[0], pair, 0)
+    @pl.when(mask > 0)
+    def _():
+        lax.fori_loop(0, left_ref.shape[0], pair, 0)
 
 
 def work(slots, parts, state, ops, step=None, final=False, begin=None):
@@ -134,8 +161,8 @@
         ids, me, ring = begin
         pairs = ids.shape[0] // 2
         operands, in_specs = [ids, me, ops, *arrays], [smem, smem]
-        out_shape = [jax.ShapeDtypeStruct((TABLE,), jnp.int32)]
-        out_specs, aliases = [smem, vmem, vmem, vmem], {}
+        out_shape = [jax.ShapeDtypeStruct((ROW, LANES), jnp.int32)]
+        out_specs, aliases = [vmem, vmem, vmem, vmem], {}
     else:
         pairs = state[1].shape[0]
         operands, in_specs = [state[0], ops, *arrays, *state[1:]], []
@@ -149,8 +176,8 @@
     ]
     scratch = [pltpu.VMEM((len(slots), 2 * half, 2 * half), jnp.bfloat16)]
     chunks = 3
-    if not begin:
-        scratch += [pltpu.SMEM((TABLE,), jnp.int32), pltpu.SemaphoreType.DMA]
+    if begin:
+        scratch.append(pltpu.SMEM((SCALARS,), jnp.int32))
     if final:
         out_shape.append(jax.ShapeDtypeStruct((2, half, half), jnp.float32))
         out_specs.append(pl.BlockSpec(memory_space=pl.ANY))
@@ -164,14 +191,12 @@
             ids_ref, me_ref, ops_ref = given[:3]
             at = 3
             table, left_ref, right_ref, sum_ref = outs
-            fill_table(table, ids_ref, me_ref[0], ring, ops_ref.shape[1], ids_ref.shape[0])
+            fill_table(table, refs[-1], ids_ref, me_ref[0], ring, ops_ref.shape[1], ids_ref.shape[0])
             sum_ref[...] = jnp.zeros(sum_ref.shape, jnp.float32)
         else:
             ops_ref = given[1]
             at = 2
-            table = refs[len(operands) + len(out_shape) + 1]
-            fetch = pltpu.make_async_copy(given[0], table, refs[len(operands) + len(out_shape) + 2])
-            fetch.start()
+            table = given[0]
             left_ref, right_ref, sum_ref = outs[:3]
         sources = []
         for pair in parts:
@@ -181,20 +206,24 @@
             else:
                 sources.append((given[at], given[at + 1]))
                 at += 2
+        row = table[...]
+        entries = [row[0, slot] for slot in slots]
+        if step is not None:
+            when = row[0, WHEN + step]
+            if not final:
+                take, operators = row[0, TAKE + step], row[0, OPERATORS]
         place_weights(sources, weight)
-        if not begin:
-            fetch.wait()
-        make_blocks(slots, table, ops_ref, left_ref, right_ref, sum_ref, weight, slots[0] > 1)
+        make_blocks(entries, ops_ref, left_ref, right_ref, sum_ref, weight, slots[0] > 1)
         if step is None:
             return
         if not final:
-            take_operators(step, table, ops_ref, left_ref, weight)
-            add_pairs(step, table, left_ref, right_ref, sum_ref, slice(None))
+            take_operators(take, operators, ops_ref, left_ref, weight)
+            add_pairs(when, left_ref, right_ref, sum_ref, slice(None))
             return
         copies = []
         for n in range(chunks):
             rows = slice(n * half // chunks, (n + 1) * half // chunks)
-            add_pairs(step, table, left_ref, right_ref, sum_ref, rows)
+            add_pairs(when, left_ref, right_ref, sum_ref, rows)
             scale = 1.0 / jnp.sqrt(jnp.float32(2 * half * pairs))
             sum_ref[:, rows] = sum_ref[:, rows] * scale
             copies.append(

time: 107 us -> 103 us (0.963)
  Pallas kernels: 29.2 us -> 25.1 us
    pallas_call x10, Pallas kernels: 29.2 us -> 25.1 us  [work(): pl.pallas_call(kernel, out_shape=tuple(out_shape), in_specs=in_specs, out...]
  transfers between devices with their start and end apart: 17 -> 17, of which waited for: 4 -> 5; matrix products, arithmetic and copies ran while one was open for 1% -> 1% of each run, Pallas kernels for 26% -> 23%
where the time goes in v5:
time: 103 us
  waiting for transfers between devices  30 us (29%)
  Pallas kernels  25.1 us (24%)
  starting transfers between devices  25 us (24%)
  blocking collectives  17.4 us (17%)
  local copies, waits for them, and re-layouts  5.24 us (5%)
    ppermute x8, waiting for transfers between devices, hop(): lax.ppermute(value, 'sa', [(i, (i + 2 * step) % sa_count) for i in range(...  30 us
    pallas_call x10, Pallas kernels, work(): pl.pallas_call(kernel, out_shape=tuple(out_shape), in_specs=in_specs, out...  25.1 us
    all_to_all x1, blocking collectives, placed(): lax.all_to_all(perambulator, 'ta', split_axis=1, concat_axis=3, tiled=True)  17.4 us
    ppermute x8, starting transfers between devices, hop(): lax.ppermute(value, 'sa', [(i, (i + 2 * step) % sa_count) for i in range(...  16.5 us
    ppermute x9, starting transfers between devices, swap(): return lax.ppermute(value, 'sa', [(i, i ^ 1) for i in range(sa_count)])  8.51 us
    unnamed x10, local copies, waits for them, and re-layouts  5.04 us
  transfers between devices with their start and end apart: 17, of which 5 were waited for; matrix products, arithmetic and copies ran while one was open for 1% of the time, Pallas kernels for 23%

profile of v5, /device:TPU:0, one launch (start us, length us, event | category | flops | bytes accessed | tf_op | source)
XLA Modules:
  0.0 103.1 jit_solution(7022374000185253168)
XLA Ops:
  0.0 1.1 %copy.36 = bf16[2,16,1,24,384]{4,3,2,0,1:T(8,128)(2,1)S(1)} copy(bf16[2,16,1,24,384]{4,3,2,1,0:T(8,128)(2,1)} %param.3) | data formatting | bytes 1179648 | tf_op args[0]
  1.1 17.4 %all_to_all.4 = bf16[2,16,1,24,384]{4,3,2,0,1:T(8,128)(2,1)S(1)} all-to-all(bf16[2,16,1,24,384]{4,3,2,0,1:T(8,128)(2,1)S(1)} %copy.36), channel_id=1, replica_groups=mesh['ta'=16,'sa'=16] {'ta'}, dimensions={1} | all-to-all | bytes 1179648 | tf_op jit(solution)/shard_map/all_to_all | solution.py:270
  18.5 0.1 copy.37
  18.6 2.0 %collective-permute-start = (bf16[2,384,384]{2,1,0:T(8,128)(2,1)S(1)}, bf16[2,384,384]{2,1,0:T(8,128)(2,1)S(1)}, u32[]{:S(2)}, u32[]{:S(2)}) collective-permute-start(bf16[2,384,384]{2,1,0:T(8,128)(2,1)S(1)} %bitcast.20), channel_id=1, source_target_pairs={{0,2},{1,3},{2,4},{3,5},{4,6},{5,7},{6,8},{7,9},{8,10},{9,11},{10,... | collective-permute-start | bytes 1769480 | tf_op jit(solution)/shard_map/ppermute | solution.py:262
  20.6 4.0 %collective-permute-start.5 = (bf16[2,384,384]{2,1,0:T(8,128)(2,1)S(1)}, bf16[2,384,384]{2,1,0:T(8,128)(2,1)}, u32[]{:S(2)}, u32[]{:S(2)}) collective-permute-start(bf16[2,384,384]{2,1,0:T(8,128)(2,1)S(1)} %bitcast.21), channel_id=1, source_target_pairs={{0,14},{1,15},{2,0},{3,1},{4,2},{5,3},{6,4},{7,5},{8,6},{9,7},{10,... | collective-permute-start | bytes 1769480 | tf_op jit(solution)/shard_map/ppermute | solution.py:262
  24.6 12.0 %collective-permute-done.refs_2_ = bf16[2,384,384]{2,1,0:T(8,128)(2,1)S(1)} collective-permute-done((bf16[2,384,384]{2,1,0:T(8,128)(2,1)S(1)}, bf16[2,384,384]{2,1,0:T(8,128)(2,1)S(1)}, u32[]{:S(2)}, u32[]{:S(2)}) %collective-permute-start) | collective-permute-done | bytes 589856 | tf_op jit(solution)/shard_map/ppermute | solution.py:262
  36.6 0.0 collective-permute-start.1
  36.6 0.0 collective-permute-done.5.refs_3_
  36.6 3.2 %collective-permute-start.6 = (bf16[2,384,384]{2,1,0:T(8,128)(2,1)}, bf16[2,384,384]{2,1,0:T(8,128)(2,1)S(1)}, u32[]{:S(2)}, u32[]{:S(2)}) collective-permute-start(bf16[2,384,384]{2,1,0:T(8,128)(2,1)} %collective-permute-done.5.refs_3_), channel_id=1, source_target_pairs={{0,14},{1,15},{2,0},{3,1},{4,2},{5,3},{6,4},{7,5},{8,6},{9,7},{10,... | collective-permute-start | bytes 1769480 | tf_op jit(solution)/shard_map/ppermute | solution.py:262
  39.9 0.0 collective-permute-start.16
  39.9 11.2 %collective-permute-done.1.refs_2_ = bf16[2,384,384]{2,1,0:T(8,128)(2,1)S(1)} collective-permute-done((bf16[2,384,384]{2,1,0:T(8,128)(2,1)S(1)}, bf16[2,384,384]{2,1,0:T(8,128)(2,1)S(1)}, u32[]{:S(2)}, u32[]{:S(2)}) %collective-permute-start.1) | collective-permute-done | bytes 589856 | tf_op jit(solution)/shard_map/ppermute | solution.py:262
  51.1 0.0 collective-permute-start.2
  51.1 0.0 collective-permute-start.14
  51.1 0.0 collective-permute-done.6.refs_3_
  51.1 3.2 %collective-permute-start.7 = (bf16[2,384,384]{2,1,0:T(8,128)(2,1)S(1)}, bf16[2,384,384]{2,1,0:T(8,128)(2,1)S(1)}, u32[]{:S(2)}, u32[]{:S(2)}) collective-permute-start(bf16[2,384,384]{2,1,0:T(8,128)(2,1)S(1)} %collective-permute-done.6.refs_3_), channel_id=1, source_target_pairs={{0,14},{1,15},{2,0},{3,1},{4,2},{5,3},{6,4},{7,5},{8,6},{9,7},{10,... | collective-permute-start | bytes 1769480 | tf_op jit(solution)/shard_map/ppermute | solution.py:262
  54.3 0.2 collective-permute-start.15
  54.6 0.0 collective-permute-done.16.refs_2_
  54.6 0.8 copy-done.2
  55.4 0.3 collective-permute-start.12
  55.7 0.8 copy.35
  56.4 0.1 reshape.10.refs_0_
  56.5 2.3 %copy-done = bf16[2,8,1,384,384]{4,3,2,1,0:T(8,128)(2,1)S(1)} copy-done((bf16[2,8,1,384,384]{4,3,2,1,0:T(8,128)(2,1)S(1)}, bf16[2,8,1,384,384]{4,3,2,1,0:T(8,128)(2,1)}, u32[]{:S(2)}) %copy-start) | copy-done | bytes 4718616
  58.9 1.8 %work.10 = (s32[8,128]{1,0:T(8,128)S(1)}, bf16[8,384,768]{2,1,0:T(8,128)(2,1)S(1)}, bf16[8,768,768]{2,1,0:T(8,128)(2,1)S(1)}, f32[2,384,384]{2,1,0:T(8,128)S(1)}) custom-call(s32[16]{0:T(128)S(1)} %reshape.10.refs_0_, s32[1]{0:T(128)} %bitcast.refs_1_, bf16[2,8,384,384]{3,2,1,0:T(8,128)(2,1)S(1)} %bitcast.10, bf16[2,384,384]{2,1,0:T(8,128)(2,1)S(1)} %bitcast.23), custom_call_target="tpu_custom_call" | custom-call | flops 452984832 | bytes 589824 | tf_op jit(solution)/shard_map/work/pallas_call | solution.py:238
  60.6 4.1 %collective-permute-done.2.refs_2_ = bf16[2,384,384]{2,1,0:T(8,128)(2,1)S(1)} collective-permute-done((bf16[2,384,384]{2,1,0:T(8,128)(2,1)S(1)}, bf16[2,384,384]{2,1,0:T(8,128)(2,1)S(1)}, u32[]{:S(2)}, u32[]{:S(2)}) %collective-permute-start.2) | collective-permute-done | bytes 589856 | tf_op jit(solution)/shard_map/ppermute | solution.py:262
  64.7 0.0 collective-permute-start.13
  64.8 0.0 collective-permute-done.14.refs_2_
  64.8 0.6 collective-permute-start.10
  65.4 2.2 %collective-permute-done.7.refs_3_ = bf16[2,384,384]{2,1,0:T(8,128)(2,1)S(1)} collective-permute-done((bf16[2,384,384]{2,1,0:T(8,128)(2,1)S(1)}, bf16[2,384,384]{2,1,0:T(8,128)(2,1)S(1)}, u32[]{:S(2)}, u32[]{:S(2)}) %collective-permute-start.7) | collective-permute-done | bytes 589856 | tf_op jit(solution)/shard_map/ppermute | solution.py:262
  67.6 0.0 collective-permute-start.11
  67.6 0.0 collective-permute-done.15.refs_3_
  67.7 0.1 collective-permute-start.3
  67.7 0.0 collective-permute-done.12.refs_2_
  67.8 3.9 %collective-permute-start.8 = (bf16[384,384]{1,0:T(8,128)(2,1)S(1)}, bf16[384,384]{1,0:T(8,128)(2,1)S(1)}, u32[]{:S(2)}, u32[]{:S(2)}) collective-permute-start(bf16[384,384]{1,0:T(8,128)(2,1)S(1)} %slice_bitcast_fusion), channel_id=1, source_target_pairs={{0,14},{1,15},{2,0},{3,1},{4,2},{5,3},{6,4},{7,5},{8,6},{9,7},{10,... | collective-permute-start | bytes 884744 | tf_op jit(solution)/shard_map/ppermute | solution.py:262
  71.7 1.7 %work.11 = (bf16[8,384,768]{2,1,0:T(8,128)(2,1)S(1)}, bf16[8,768,768]{2,1,0:T(8,128)(2,1)S(1)}, f32[2,384,384]{2,1,0:T(8,128)S(1)}) custom-call(s32[8,128]{1,0:T(8,128)S(1)} %get-tuple-element.34.refs_0_, bf16[2,8,384,384]{3,2,1,0:T(8,128)(2,1)S(1)} %bitcast.11, ...), custom_call_target="tpu_custom_call", output_to_operand_aliasing={{0}: (3, {}), {1}: (4, {}), {2}: (5, {})} | custom-call | flops 452984832 | bytes 589824 | tf_op jit(solution)/shard_map/work/pallas_call | solution.py:238
  73.4 2.1 %work.12 = (bf16[8,384,768]{2,1,0:T(8,128)(2,1)S(1)}, bf16[8,768,768]{2,1,0:T(8,128)(2,1)S(1)}, f32[2,384,384]{2,1,0:T(8,128)S(1)}) custom-call(s32[8,128]{1,0:T(8,128)S(1)} %get-tuple-element.34.refs_0_, bf16[2,8,384,384]{3,2,1,0:T(8,128)(2,1)S(1)} %bitcast.12, ...), custom_call_target="tpu_custom_call", output_to_operand_aliasing={{0}: (4, {}), {1}: (5, {}), {2}: (6, {})} | custom-call | flops 905969664 | bytes 1179648 | tf_op jit(solution)/shard_map/work/pallas_call | solution.py:238
  75.5 3.0 %work.13 = (bf16[8,384,768]{2,1,0:T(8,128)(2,1)S(1)}, bf16[8,768,768]{2,1,0:T(8,128)(2,1)S(1)}, f32[2,384,384]{2,1,0:T(8,128)S(1)}) custom-call(s32[8,128]{1,0:T(8,128)S(1)} %get-tuple-element.34.refs_0_, bf16[2,8,384,384]{3,2,1,0:T(8,128)(2,1)S(1)} %bitcast.13, ...), custom_call_target="tpu_custom_call", output_to_operand_aliasing={{0}: (4, {}), {1}: (5, {}), {2}: (6, {})} | custom-call | flops 905969664 | bytes 1179648 | tf_op jit(solution)/shard_map/work/pallas_call | solution.py:238
  78.5 0.3 work.14
  78.7 0.4 collective-permute-done.3.refs_2_
  79.1 7.3 %collective-permute-start.4 = (bf16[384,384]{1,0:T(8,128)(2,1)S(1)}, bf16[384,384]{1,0:T(8,128)(2,1)S(1)}, u32[]{:S(2)}, u32[]{:S(2)}) collective-permute-start(bf16[384,384]{1,0:T(8,128)(2,1)S(1)} %collective-permute-done.3.refs_2_), channel_id=1, source_target_pairs={{0,1},{1,0},{2,3},{3,2},{4,5},{5,4},{6,7},{7,6},{8,9},{9,8},{10,11... | collective-permute-start | bytes 884744 | tf_op jit(solution)/shard_map/ppermute | solution.py:265
  86.4 0.0 collective-permute-done.8.refs_3_
  86.4 0.1 collective-permute-start.9
  86.5 5.2 %work.15 = (bf16[8,384,768]{2,1,0:T(8,128)(2,1)S(1)}, bf16[8,768,768]{2,1,0:T(8,128)(2,1)S(1)}, f32[2,384,384]{2,1,0:T(8,128)S(1)}) custom-call(s32[8,128]{1,0:T(8,128)S(1)} %get-tuple-element.34.refs_0_, bf16[2,8,384,384]{3,2,1,0:T(8,128)(2,1)S(1)} %bitcast.15, ...), custom_call_target="tpu_custom_call", output_to_operand_aliasing={{0}: (4, {}), {1}: (5, {}), {2}: (6, {})} | custom-call | flops 905969664 | bytes 1179648 | tf_op jit(solution)/shard_map/work/pallas_call | solution.py:238
  91.7 2.4 %work.16 = (bf16[8,384,768]{2,1,0:T(8,128)(2,1)S(1)}, bf16[8,768,768]{2,1,0:T(8,128)(2,1)S(1)}, f32[2,384,384]{2,1,0:T(8,128)S(1)}) custom-call(s32[8,128]{1,0:T(8,128)S(1)} %get-tuple-element.34.refs_0_, bf16[2,8,384,384]{3,2,1,0:T(8,128)(2,1)S(1)} %bitcast.16, ...), custom_call_target="tpu_custom_call", output_to_operand_aliasing={{0}: (4, {}), {1}: (5, {}), {2}: (6, {})} | custom-call | flops 905969664 | bytes 1179648 | tf_op jit(solution)/shard_map/work/pallas_call | solution.py:238
  94.1 0.0 collective-permute-done.10.refs_2_
  94.1 6.7 %work.17 = (bf16[8,384,768]{2,1,0:T(8,128)(2,1)S(1)}, bf16[8,768,768]{2,1,0:T(8,128)(2,1)S(1)}, f32[2,384,384]{2,1,0:T(8,128)S(1)}) custom-call(s32[8,128]{1,0:T(8,128)S(1)} %get-tuple-element.34.refs_0_, bf16[2,8,384,384]{3,2,1,0:T(8,128)(2,1)S(1)} %bitcast.17, ...), custom_call_target="tpu_custom_call", output_to_operand_aliasing={{0}: (4, {}), {1}: (5, {}), {2}: (6, {})} | custom-call | flops 905969664 | bytes 1179648 | tf_op jit(solution)/shard_map/work/pallas_call | solution.py:238
  100.8 0.8 work.18
  101.7 0.0 collective-permute-done.9.refs_3_
  101.7 1.2 %work.19 = (bf16[8,384,768]{2,1,0:T(8,128)(2,1)S(1)}, bf16[8,768,768]{2,1,0:T(8,128)(2,1)S(1)}, f32[2,384,384]{2,1,0:T(8,128)S(1)}, f32[2,384,384]{2,1,0:T(8,128)}) custom-call(s32[8,128]{1,0:T(8,128)S(1)} %get-tuple-element.34.refs_0_, bf16[2,8,384,384]{3,2,1,0:T(8,128)(2,1)S(1)} %bitcast.19, ...), custom_call_target="tpu_custom_call", output_to_operand_aliasing={{0}: (4, {}), {1}: (5, {}), {2}: (6, {})} | custom-call | flops 452984832 | bytes 589824 | tf_op jit(solution)/shard_map/work/pallas_call | solution.py:238
  (11 shorter events, 0.1 us)
Async XLA Ops:
  18.6 18.0 %collective-permute-start = (bf16[2,384,384]{2,1,0:T(8,128)(2,1)S(1)}, bf16[2,384,384]{2,1,0:T(8,128)(2,1)S(1)}, u32[]{:S(2)}, u32[]{:S(2)}) collective-permute-start(bf16[2,384,384]{2,1,0:T(8,128)(2,1)S(1)} %bitcast.20), channel_id=1, source_target_pairs={{0,2},{1,3},{2,4},{3,5},{4,6},{5,7},{6,8},{7,9},{8,10},{9,11},{10,... | collective-permute-start | bytes 1769480 | tf_op jit(solution)/shard_map/ppermute | solution.py:262
  20.6 16.1 %collective-permute-start.5 = (bf16[2,384,384]{2,1,0:T(8,128)(2,1)S(1)}, bf16[2,384,384]{2,1,0:T(8,128)(2,1)}, u32[]{:S(2)}, u32[]{:S(2)}) collective-permute-start(bf16[2,384,384]{2,1,0:T(8,128)(2,1)S(1)} %bitcast.21), channel_id=1, source_target_pairs={{0,14},{1,15},{2,0},{3,1},{4,2},{5,3},{6,4},{7,5},{8,6},{9,7},{10,... | collective-permute-start | bytes 1769480 | tf_op jit(solution)/shard_map/ppermute | solution.py:262
  36.6 14.5 %collective-permute-start.1 = (bf16[2,384,384]{2,1,0:T(8,128)(2,1)S(1)}, bf16[2,384,384]{2,1,0:T(8,128)(2,1)S(1)}, u32[]{:S(2)}, u32[]{:S(2)}) collective-permute-start(bf16[2,384,384]{2,1,0:T(8,128)(2,1)S(1)} %collective-permute-done.refs_2_), channel_id=1, source_target_pairs={{0,2},{1,3},{2,4},{3,5},{4,6},{5,7},{6,8},{7,9},{8,10},{9,11},{10,... | collective-permute-start | bytes 1769480 | tf_op jit(solution)/shard_map/ppermute | solution.py:262
  36.6 14.5 %collective-permute-start.6 = (bf16[2,384,384]{2,1,0:T(8,128)(2,1)}, bf16[2,384,384]{2,1,0:T(8,128)(2,1)S(1)}, u32[]{:S(2)}, u32[]{:S(2)}) collective-permute-start(bf16[2,384,384]{2,1,0:T(8,128)(2,1)} %collective-permute-done.5.refs_3_), channel_id=1, source_target_pairs={{0,14},{1,15},{2,0},{3,1},{4,2},{5,3},{6,4},{7,5},{8,6},{9,7},{10,... | collective-permute-start | bytes 1769480 | tf_op jit(solution)/shard_map/ppermute | solution.py:262
  39.9 14.7 %collective-permute-start.16 = (bf16[2,384,384]{2,1,0:T(8,128)(2,1)S(1)}, bf16[2,384,384]{2,1,0:T(8,128)(2,1)S(1)}, u32[]{:S(2)}, u32[]{:S(2)}) collective-permute-start(bf16[2,384,384]{2,1,0:T(8,128)(2,1)S(1)} %bitcast.22), channel_id=1, source_target_pairs={{0,1},{1,0},{2,3},{3,2},{4,5},{5,4},{6,7},{7,6},{8,9},{9,8},{10,11... | collective-permute-start | bytes 1769480 | tf_op jit(solution)/shard_map/ppermute | solution.py:265
  51.1 13.6 %collective-permute-start.2 = (bf16[2,384,384]{2,1,0:T(8,128)(2,1)S(1)}, bf16[2,384,384]{2,1,0:T(8,128)(2,1)S(1)}, u32[]{:S(2)}, u32[]{:S(2)}) collective-permute-start(bf16[2,384,384]{2,1,0:T(8,128)(2,1)S(1)} %collective-permute-done.1.refs_2_), channel_id=1, source_target_pairs={{0,2},{1,3},{2,4},{3,5},{4,6},{5,7},{6,8},{7,9},{8,10},{9,11},{10,... | collective-permute-start | bytes 1769480 | tf_op jit(solution)/shard_map/ppermute | solution.py:262
  51.1 13.7 %collective-permute-start.14 = (bf16[2,384,384]{2,1,0:T(8,128)(2,1)S(1)}, bf16[2,384,384]{2,1,0:T(8,128)(2,1)}, u32[]{:S(2)}, u32[]{:S(2)}) collective-permute-start(bf16[2,384,384]{2,1,0:T(8,128)(2,1)S(1)} %collective-permute-done.refs_2_), channel_id=1, source_target_pairs={{0,1},{1,0},{2,3},{3,2},{4,5},{5,4},{6,7},{7,6},{8,9},{9,8},{10,11... | collective-permute-start | bytes 1769480 | tf_op jit(solution)/shard_map/ppermute | solution.py:265
  51.1 16.5 %collective-permute-start.7 = (bf16[2,384,384]{2,1,0:T(8,128)(2,1)S(1)}, bf16[2,384,384]{2,1,0:T(8,128)(2,1)S(1)}, u32[]{:S(2)}, u32[]{:S(2)}) collective-permute-start(bf16[2,384,384]{2,1,0:T(8,128)(2,1)S(1)} %collective-permute-done.6.refs_3_), channel_id=1, source_target_pairs={{0,14},{1,15},{2,0},{3,1},{4,2},{5,3},{6,4},{7,5},{8,6},{9,7},{10,... | collective-permute-start | bytes 1769480 | tf_op jit(solution)/shard_map/ppermute | solution.py:262
  54.3 13.3 %collective-permute-start.15 = (bf16[2,384,384]{2,1,0:T(8,128)(2,1)}, bf16[2,384,384]{2,1,0:T(8,128)(2,1)}, u32[]{:S(2)}, u32[]{:S(2)}) collective-permute-start(bf16[2,384,384]{2,1,0:T(8,128)(2,1)} %collective-permute-done.5.refs_3_), channel_id=1, source_target_pairs={{0,1},{1,0},{2,3},{3,2},{4,5},{5,4},{6,7},{7,6},{8,9},{9,8},{10,11... | collective-permute-start | bytes 1769480 | tf_op jit(solution)/shard_map/ppermute | solution.py:265
  54.6 0.8 copy-start.2
  55.4 12.4 %collective-permute-start.12 = (bf16[2,384,384]{2,1,0:T(8,128)(2,1)S(1)}, bf16[2,384,384]{2,1,0:T(8,128)(2,1)}, u32[]{:S(2)}, u32[]{:S(2)}) collective-permute-start(bf16[2,384,384]{2,1,0:T(8,128)(2,1)S(1)} %collective-permute-done.1.refs_2_), channel_id=1, source_target_pairs={{0,1},{1,0},{2,3},{3,2},{4,5},{5,4},{6,7},{7,6},{8,9},{9,8},{10,11... | collective-permute-start | bytes 1769480 | tf_op jit(solution)/shard_map/ppermute | solution.py:265
  56.5 2.3 %copy-start = (bf16[2,8,1,384,384]{4,3,2,1,0:T(8,128)(2,1)S(1)}, bf16[2,8,1,384,384]{4,3,2,1,0:T(8,128)(2,1)}, u32[]{:S(2)}) copy-start(bf16[2,8,1,384,384]{4,3,2,1,0:T(8,128)(2,1)} %param.4) | copy-start | bytes 14155780
  58.9 12.9 %copy-start.1 = (bf16[2,8,1,384,384]{4,3,2,1,0:T(8,128)(2,1)S(1)}, bf16[2,8,1,384,384]{4,3,2,1,0:T(8,128)(2,1)}, u32[]{:S(2)}) copy-start(bf16[2,8,1,384,384]{4,3,2,1,0:T(8,128)(2,1)} %param.4) | copy-start | bytes 14155780
  58.9 12.9 %copy-start.3 = (bf16[2,384,384]{2,1,0:T(8,128)(2,1)S(1)}, bf16[2,384,384]{2,1,0:T(8,128)(2,1)}, u32[]{:S(2)}) copy-start(bf16[2,384,384]{2,1,0:T(8,128)(2,1)} %copy-done.2) | copy-start | bytes 1769476
  64.7 21.8 %collective-permute-start.13 = (bf16[2,384,384]{2,1,0:T(8,128)(2,1)S(1)}, bf16[2,384,384]{2,1,0:T(8,128)(2,1)S(1)}, u32[]{:S(2)}, u32[]{:S(2)}) collective-permute-start(bf16[2,384,384]{2,1,0:T(8,128)(2,1)S(1)} %collective-permute-done.6.refs_3_), channel_id=1, source_target_pairs={{0,1},{1,0},{2,3},{3,2},{4,5},{5,4},{6,7},{7,6},{8,9},{9,8},{10,11... | collective-permute-start | bytes 1769480 | tf_op jit(solution)/shard_map/ppermute | solution.py:265
  64.8 29.3 %collective-permute-start.10 = (bf16[2,384,384]{2,1,0:T(8,128)(2,1)S(1)}, bf16[2,384,384]{2,1,0:T(8,128)(2,1)S(1)}, u32[]{:S(2)}, u32[]{:S(2)}) collective-permute-start(bf16[2,384,384]{2,1,0:T(8,128)(2,1)S(1)} %collective-permute-done.2.refs_2_), channel_id=1, source_target_pairs={{0,1},{1,0},{2,3},{3,2},{4,5},{5,4},{6,7},{7,6},{8,9},{9,8},{10,11... | collective-permute-start | bytes 1769480 | tf_op jit(solution)/shard_map/ppermute | solution.py:265
  67.6 26.5 %collective-permute-start.11 = (bf16[2,384,384]{2,1,0:T(8,128)(2,1)S(1)}, bf16[2,384,384]{2,1,0:T(8,128)(2,1)S(1)}, u32[]{:S(2)}, u32[]{:S(2)}) collective-permute-start(bf16[2,384,384]{2,1,0:T(8,128)(2,1)S(1)} %collective-permute-done.7.refs_3_), channel_id=1, source_target_pairs={{0,1},{1,0},{2,3},{3,2},{4,5},{5,4},{6,7},{7,6},{8,9},{9,8},{10,11... | collective-permute-start | bytes 1769480 | tf_op jit(solution)/shard_map/ppermute | solution.py:265
  67.7 11.4 %collective-permute-start.3 = (bf16[384,384]{1,0:T(8,128)(2,1)S(1)}, bf16[384,384]{1,0:T(8,128)(2,1)S(1)}, u32[]{:S(2)}, u32[]{:S(2)}) collective-permute-start(bf16[384,384]{1,0:T(8,128)(2,1)S(1)} %slice_bitcast_fusion.1), channel_id=1, source_target_pairs={{0,2},{1,3},{2,4},{3,5},{4,6},{5,7},{6,8},{7,9},{8,10},{9,11},{10,... | collective-permute-start | bytes 884744 | tf_op jit(solution)/shard_map/ppermute | solution.py:262
  67.8 18.6 %collective-permute-start.8 = (bf16[384,384]{1,0:T(8,128)(2,1)S(1)}, bf16[384,384]{1,0:T(8,128)(2,1)S(1)}, u32[]{:S(2)}, u32[]{:S(2)}) collective-permute-start(bf16[384,384]{1,0:T(8,128)(2,1)S(1)} %slice_bitcast_fusion), channel_id=1, source_target_pairs={{0,14},{1,15},{2,0},{3,1},{4,2},{5,3},{6,4},{7,5},{8,6},{9,7},{10,... | collective-permute-start | bytes 884744 | tf_op jit(solution)/shard_map/ppermute | solution.py:262
  79.1 22.5 %collective-permute-start.4 = (bf16[384,384]{1,0:T(8,128)(2,1)S(1)}, bf16[384,384]{1,0:T(8,128)(2,1)S(1)}, u32[]{:S(2)}, u32[]{:S(2)}) collective-permute-start(bf16[384,384]{1,0:T(8,128)(2,1)S(1)} %collective-permute-done.3.refs_2_), channel_id=1, source_target_pairs={{0,1},{1,0},{2,3},{3,2},{4,5},{5,4},{6,7},{7,6},{8,9},{9,8},{10,11... | collective-permute-start | bytes 884744 | tf_op jit(solution)/shard_map/ppermute | solution.py:265
  86.4 15.3 %collective-permute-start.9 = (bf16[384,384]{1,0:T(8,128)(2,1)S(1)}, bf16[384,384]{1,0:T(8,128)(2,1)S(1)}, u32[]{:S(2)}, u32[]{:S(2)}) collective-permute-start(bf16[384,384]{1,0:T(8,128)(2,1)S(1)} %collective-permute-done.8.refs_3_), channel_id=1, source_target_pairs={{0,1},{1,0},{2,3},{3,2},{4,5},{5,4},{6,7},{7,6},{8,9},{9,8},{10,11... | collective-permute-start | bytes 884744 | tf_op jit(solution)/shard_map/ppermute | solution.py:265

commit v6 on v5

--- a/solution.py
+++ b/solution.py
@@ -152,7 +152,7 @@
         lax.fori_loop(0, left_ref.shape[0], pair, 0)
 
 
-def work(slots, parts, state, ops, step=None, final=False, begin=None):
+def work(slots, parts, state, ops, step=None, behind=None, final=False, begin=None):
     half = ops.shape[-1]
     smem = pl.BlockSpec(memory_space=pltpu.SMEM)
     vmem = pl.BlockSpec(memory_space=pltpu.VMEM)
@@ -175,7 +175,7 @@
         jax.ShapeDtypeStruct((2, half, half), jnp.float32),
     ]
     scratch = [pltpu.VMEM((len(slots), 2 * half, 2 * half), jnp.bfloat16)]
-    chunks = 3
+    chunks = 1
     if begin:
         scratch.append(pltpu.SMEM((SCALARS,), jnp.int32))
     if final:
@@ -208,6 +208,9 @@
                 at += 2
         row = table[...]
         entries = [row[0, slot] for slot in slots]
+        if behind is not None:
+            take_operators(row[0, TAKE + behind], row[0, OPERATORS], ops_ref, left_ref, weight)
+            add_pairs(row[0, WHEN + behind], left_ref, right_ref, sum_ref, slice(None))
         if step is not None:
             when = row[0, WHEN + step]
             if not final:
@@ -288,8 +291,10 @@
         else:
             own, other = [(up[d], None)], [(other_up, None)]
             slots = [0]
-        state = work(slots, own, state, ops, begin=None if d else (ids, me, ring))
-        state = work([s + 1 for s in slots], other, state, ops, step=d, final=d == far)
+        begin = None if d else (ids, me, ring)
+        state = work(slots, own, state, ops, behind=d - 1 if d == far else None, begin=begin)
+        step = None if d == far - 1 else d
+        state = work([s + 1 for s in slots], other, state, ops, step=step, final=d == far)
     return state[:, None, None]
 
 

time: 103 us -> 104 us (level)
  no operation moved by 1% of the time
where the time goes in v6:
time: 104 us; the launch traced here: 103 us
  waiting for transfers between devices  30 us (29%)
  Pallas kernels  25.3 us (24%)
  starting transfers between devices  25 us (24%)
  blocking collectives  17.4 us (17%)
  local copies, waits for them, and re-layouts  5.24 us (5%)
    ppermute x8, waiting for transfers between devices, hop(): lax.ppermute(value, 'sa', [(i, (i + 2 * step) % sa_count) for i in range(...  30 us
    pallas_call x10, Pallas kernels, work(): pl.pallas_call(kernel, out_shape=tuple(out_shape), in_specs=in_specs, out...  25.3 us
    all_to_all x1, blocking collectives, placed(): lax.all_to_all(perambulator, 'ta', split_axis=1, concat_axis=3, tiled=True)  17.4 us
    ppermute x8, starting transfers between devices, hop(): lax.ppermute(value, 'sa', [(i, (i + 2 * step) % sa_count) for i in range(...  16.5 us
    ppermute x9, starting transfers between devices, swap(): return lax.ppermute(value, 'sa', [(i, i ^ 1) for i in range(sa_count)])  8.51 us
    unnamed x10, local copies, waits for them, and re-layouts  5.04 us
  transfers between devices with their start and end apart: 17, of which 5 were waited for; matrix products, arithmetic and copies ran while one was open for 1% of the time, Pallas kernels for 23%

profile of v6, /device:TPU:0, one launch (start us, length us, event | category | flops | bytes accessed | tf_op | source)
XLA Modules:
  0.0 103.3 jit_solution(13299242731028218510)
XLA Ops:
  0.0 1.1 %copy.36 = bf16[2,16,1,24,384]{4,3,2,0,1:T(8,128)(2,1)S(1)} copy(bf16[2,16,1,24,384]{4,3,2,1,0:T(8,128)(2,1)} %param.3) | data formatting | bytes 1179648 | tf_op args[0]
  1.1 17.4 %all_to_all.4 = bf16[2,16,1,24,384]{4,3,2,0,1:T(8,128)(2,1)S(1)} all-to-all(bf16[2,16,1,24,384]{4,3,2,0,1:T(8,128)(2,1)S(1)} %copy.36), channel_id=1, replica_groups=mesh['ta'=16,'sa'=16] {'ta'}, dimensions={1} | all-to-all | bytes 1179648 | tf_op jit(solution)/shard_map/all_to_all | solution.py:273
  18.5 0.1 copy.37
  18.6 2.0 %collective-permute-start = (bf16[2,384,384]{2,1,0:T(8,128)(2,1)S(1)}, bf16[2,384,384]{2,1,0:T(8,128)(2,1)S(1)}, u32[]{:S(2)}, u32[]{:S(2)}) collective-permute-start(bf16[2,384,384]{2,1,0:T(8,128)(2,1)S(1)} %bitcast.20), channel_id=1, source_target_pairs={{0,2},{1,3},{2,4},{3,5},{4,6},{5,7},{6,8},{7,9},{8,10},{9,11},{10,... | collective-permute-start | bytes 1769480 | tf_op jit(solution)/shard_map/ppermute | solution.py:265
  20.6 4.0 %collective-permute-start.5 = (bf16[2,384,384]{2,1,0:T(8,128)(2,1)S(1)}, bf16[2,384,384]{2,1,0:T(8,128)(2,1)}, u32[]{:S(2)}, u32[]{:S(2)}) collective-permute-start(bf16[2,384,384]{2,1,0:T(8,128)(2,1)S(1)} %bitcast.21), channel_id=1, source_target_pairs={{0,14},{1,15},{2,0},{3,1},{4,2},{5,3},{6,4},{7,5},{8,6},{9,7},{10,... | collective-permute-start | bytes 1769480 | tf_op jit(solution)/shard_map/ppermute | solution.py:265
  24.6 12.0 %collective-permute-done.refs_2_ = bf16[2,384,384]{2,1,0:T(8,128)(2,1)S(1)} collective-permute-done((bf16[2,384,384]{2,1,0:T(8,128)(2,1)S(1)}, bf16[2,384,384]{2,1,0:T(8,128)(2,1)S(1)}, u32[]{:S(2)}, u32[]{:S(2)}) %collective-permute-start) | collective-permute-done | bytes 589856 | tf_op jit(solution)/shard_map/ppermute | solution.py:265
  36.6 0.0 collective-permute-start.1
  36.6 0.0 collective-permute-done.5.refs_3_
  36.6 3.2 %collective-permute-start.6 = (bf16[2,384,384]{2,1,0:T(8,128)(2,1)}, bf16[2,384,384]{2,1,0:T(8,128)(2,1)S(1)}, u32[]{:S(2)}, u32[]{:S(2)}) collective-permute-start(bf16[2,384,384]{2,1,0:T(8,128)(2,1)} %collective-permute-done.5.refs_3_), channel_id=1, source_target_pairs={{0,14},{1,15},{2,0},{3,1},{4,2},{5,3},{6,4},{7,5},{8,6},{9,7},{10,... | collective-permute-start | bytes 1769480 | tf_op jit(solution)/shard_map/ppermute | solution.py:265
  39.9 0.0 collective-permute-start.16
  39.9 11.2 %collective-permute-done.1.refs_2_ = bf16[2,384,384]{2,1,0:T(8,128)(2,1)S(1)} collective-permute-done((bf16[2,384,384]{2,1,0:T(8,128)(2,1)S(1)}, bf16[2,384,384]{2,1,0:T(8,128)(2,1)S(1)}, u32[]{:S(2)}, u32[]{:S(2)}) %collective-permute-start.1) | collective-permute-done | bytes 589856 | tf_op jit(solution)/shard_map/ppermute | solution.py:265
  51.1 0.0 collective-permute-start.2
  51.1 0.0 collective-permute-start.14
  51.1 0.0 collective-permute-done.6.refs_3_
  51.1 3.2 %collective-permute-start.7 = (bf16[2,384,384]{2,1,0:T(8,128)(2,1)S(1)}, bf16[2,384,384]{2,1,0:T(8,128)(2,1)S(1)}, u32[]{:S(2)}, u32[]{:S(2)}) collective-permute-start(bf16[2,384,384]{2,1,0:T(8,128)(2,1)S(1)} %collective-permute-done.6.refs_3_), channel_id=1, source_target_pairs={{0,14},{1,15},{2,0},{3,1},{4,2},{5,3},{6,4},{7,5},{8,6},{9,7},{10,... | collective-permute-start | bytes 1769480 | tf_op jit(solution)/shard_map/ppermute | solution.py:265
  54.3 0.2 collective-permute-start.15
  54.6 0.0 collective-permute-done.16.refs_2_
  54.6 0.8 copy-done.2
  55.4 0.3 collective-permute-start.12
  55.7 0.8 copy.35
  56.4 0.1 reshape.10.refs_0_
  56.5 2.3 %copy-done = bf16[2,8,1,384,384]{4,3,2,1,0:T(8,128)(2,1)S(1)} copy-done((bf16[2,8,1,384,384]{4,3,2,1,0:T(8,128)(2,1)S(1)}, bf16[2,8,1,384,384]{4,3,2,1,0:T(8,128)(2,1)}, u32[]{:S(2)}) %copy-start) | copy-done | bytes 4718616
  58.9 1.8 %work.10 = (s32[8,128]{1,0:T(8,128)S(1)}, bf16[8,384,768]{2,1,0:T(8,128)(2,1)S(1)}, bf16[8,768,768]{2,1,0:T(8,128)(2,1)S(1)}, f32[2,384,384]{2,1,0:T(8,128)S(1)}) custom-call(s32[16]{0:T(128)S(1)} %reshape.10.refs_0_, s32[1]{0:T(128)} %bitcast.refs_1_, bf16[2,8,384,384]{3,2,1,0:T(8,128)(2,1)S(1)} %bitcast.10, bf16[2,384,384]{2,1,0:T(8,128)(2,1)S(1)} %bitcast.23), custom_call_target="tpu_custom_call" | custom-call | flops 452984832 | bytes 589824 | tf_op jit(solution)/shard_map/work/pallas_call | solution.py:241
  60.6 4.1 %collective-permute-done.2.refs_2_ = bf16[2,384,384]{2,1,0:T(8,128)(2,1)S(1)} collective-permute-done((bf16[2,384,384]{2,1,0:T(8,128)(2,1)S(1)}, bf16[2,384,384]{2,1,0:T(8,128)(2,1)S(1)}, u32[]{:S(2)}, u32[]{:S(2)}) %collective-permute-start.2) | collective-permute-done | bytes 589856 | tf_op jit(solution)/shard_map/ppermute | solution.py:265
  64.7 0.0 collective-permute-start.13
  64.8 0.0 collective-permute-done.14.refs_2_
  64.8 0.6 collective-permute-start.10
  65.4 2.2 %collective-permute-done.7.refs_3_ = bf16[2,384,384]{2,1,0:T(8,128)(2,1)S(1)} collective-permute-done((bf16[2,384,384]{2,1,0:T(8,128)(2,1)S(1)}, bf16[2,384,384]{2,1,0:T(8,128)(2,1)S(1)}, u32[]{:S(2)}, u32[]{:S(2)}) %collective-permute-start.7) | collective-permute-done | bytes 589856 | tf_op jit(solution)/shard_map/ppermute | solution.py:265
  67.6 0.0 collective-permute-start.11
  67.6 0.0 collective-permute-done.15.refs_3_
  67.7 0.1 collective-permute-start.3
  67.7 0.0 collective-permute-done.12.refs_2_
  67.8 3.9 %collective-permute-start.8 = (bf16[384,384]{1,0:T(8,128)(2,1)S(1)}, bf16[384,384]{1,0:T(8,128)(2,1)S(1)}, u32[]{:S(2)}, u32[]{:S(2)}) collective-permute-start(bf16[384,384]{1,0:T(8,128)(2,1)S(1)} %slice_bitcast_fusion), channel_id=1, source_target_pairs={{0,14},{1,15},{2,0},{3,1},{4,2},{5,3},{6,4},{7,5},{8,6},{9,7},{10,... | collective-permute-start | bytes 884744 | tf_op jit(solution)/shard_map/ppermute | solution.py:265
  71.7 1.7 %work.11 = (bf16[8,384,768]{2,1,0:T(8,128)(2,1)S(1)}, bf16[8,768,768]{2,1,0:T(8,128)(2,1)S(1)}, f32[2,384,384]{2,1,0:T(8,128)S(1)}) custom-call(s32[8,128]{1,0:T(8,128)S(1)} %get-tuple-element.34.refs_0_, bf16[2,8,384,384]{3,2,1,0:T(8,128)(2,1)S(1)} %bitcast.11, ...), custom_call_target="tpu_custom_call", output_to_operand_aliasing={{0}: (3, {}), {1}: (4, {}), {2}: (5, {})} | custom-call | flops 452984832 | bytes 589824 | tf_op jit(solution)/shard_map/work/pallas_call | solution.py:241
  73.4 2.1 %work.12 = (bf16[8,384,768]{2,1,0:T(8,128)(2,1)S(1)}, bf16[8,768,768]{2,1,0:T(8,128)(2,1)S(1)}, f32[2,384,384]{2,1,0:T(8,128)S(1)}) custom-call(s32[8,128]{1,0:T(8,128)S(1)} %get-tuple-element.34.refs_0_, bf16[2,8,384,384]{3,2,1,0:T(8,128)(2,1)S(1)} %bitcast.12, ...), custom_call_target="tpu_custom_call", output_to_operand_aliasing={{0}: (4, {}), {1}: (5, {}), {2}: (6, {})} | custom-call | flops 905969664 | bytes 1179648 | tf_op jit(solution)/shard_map/work/pallas_call | solution.py:241
  75.5 3.0 %work.13 = (bf16[8,384,768]{2,1,0:T(8,128)(2,1)S(1)}, bf16[8,768,768]{2,1,0:T(8,128)(2,1)S(1)}, f32[2,384,384]{2,1,0:T(8,128)S(1)}) custom-call(s32[8,128]{1,0:T(8,128)S(1)} %get-tuple-element.34.refs_0_, bf16[2,8,384,384]{3,2,1,0:T(8,128)(2,1)S(1)} %bitcast.13, ...), custom_call_target="tpu_custom_call", output_to_operand_aliasing={{0}: (4, {}), {1}: (5, {}), {2}: (6, {})} | custom-call | flops 905969664 | bytes 1179648 | tf_op jit(solution)/shard_map/work/pallas_call | solution.py:241
  78.5 0.3 work.14
  78.7 0.4 collective-permute-done.3.refs_2_
  79.1 7.3 %collective-permute-start.4 = (bf16[384,384]{1,0:T(8,128)(2,1)S(1)}, bf16[384,384]{1,0:T(8,128)(2,1)S(1)}, u32[]{:S(2)}, u32[]{:S(2)}) collective-permute-start(bf16[384,384]{1,0:T(8,128)(2,1)S(1)} %collective-permute-done.3.refs_2_), channel_id=1, source_target_pairs={{0,1},{1,0},{2,3},{3,2},{4,5},{5,4},{6,7},{7,6},{8,9},{9,8},{10,11... | collective-permute-start | bytes 884744 | tf_op jit(solution)/shard_map/ppermute | solution.py:268
  86.4 0.0 collective-permute-done.8.refs_3_
  86.4 0.1 collective-permute-start.9
  86.5 5.2 %work.15 = (bf16[8,384,768]{2,1,0:T(8,128)(2,1)S(1)}, bf16[8,768,768]{2,1,0:T(8,128)(2,1)S(1)}, f32[2,384,384]{2,1,0:T(8,128)S(1)}) custom-call(s32[8,128]{1,0:T(8,128)S(1)} %get-tuple-element.34.refs_0_, bf16[2,8,384,384]{3,2,1,0:T(8,128)(2,1)S(1)} %bitcast.15, ...), custom_call_target="tpu_custom_call", output_to_operand_aliasing={{0}: (4, {}), {1}: (5, {}), {2}: (6, {})} | custom-call | flops 905969664 | bytes 1179648 | tf_op jit(solution)/shard_map/work/pallas_call | solution.py:241
  91.7 2.4 %work.16 = (bf16[8,384,768]{2,1,0:T(8,128)(2,1)S(1)}, bf16[8,768,768]{2,1,0:T(8,128)(2,1)S(1)}, f32[2,384,384]{2,1,0:T(8,128)S(1)}) custom-call(s32[8,128]{1,0:T(8,128)S(1)} %get-tuple-element.34.refs_0_, bf16[2,8,384,384]{3,2,1,0:T(8,128)(2,1)S(1)} %bitcast.16, ...), custom_call_target="tpu_custom_call", output_to_operand_aliasing={{0}: (4, {}), {1}: (5, {}), {2}: (6, {})} | custom-call | flops 905969664 | bytes 1179648 | tf_op jit(solution)/shard_map/work/pallas_call | solution.py:241
  94.1 0.0 collective-permute-done.10.refs_2_
  94.1 3.3 %work.17 = (bf16[8,384,768]{2,1,0:T(8,128)(2,1)S(1)}, bf16[8,768,768]{2,1,0:T(8,128)(2,1)S(1)}, f32[2,384,384]{2,1,0:T(8,128)S(1)}) custom-call(s32[8,128]{1,0:T(8,128)S(1)} %get-tuple-element.34.refs_0_, bf16[2,8,384,384]{3,2,1,0:T(8,128)(2,1)S(1)} %bitcast.17, ...), custom_call_target="tpu_custom_call", output_to_operand_aliasing={{0}: (4, {}), {1}: (5, {}), {2}: (6, {})} | custom-call | flops 905969664 | bytes 1179648 | tf_op jit(solution)/shard_map/work/pallas_call | solution.py:241
  97.4 4.4 %work.18 = (bf16[8,384,768]{2,1,0:T(8,128)(2,1)S(1)}, bf16[8,768,768]{2,1,0:T(8,128)(2,1)S(1)}, f32[2,384,384]{2,1,0:T(8,128)S(1)}) custom-call(s32[8,128]{1,0:T(8,128)S(1)} %get-tuple-element.34.refs_0_, bf16[2,8,384,384]{3,2,1,0:T(8,128)(2,1)S(1)} %bitcast.18, ...), custom_call_target="tpu_custom_call", output_to_operand_aliasing={{0}: (4, {}), {1}: (5, {}), {2}: (6, {})} | custom-call | flops 452984832 | bytes 589824 | tf_op jit(solution)/shard_map/work/pallas_call | solution.py:241
  101.8 0.0 collective-permute-done.9.refs_3_
  101.8 1.3 %work.19 = (bf16[8,384,768]{2,1,0:T(8,128)(2,1)S(1)}, bf16[8,768,768]{2,1,0:T(8,128)(2,1)S(1)}, f32[2,384,384]{2,1,0:T(8,128)S(1)}, f32[2,384,384]{2,1,0:T(8,128)}) custom-call(s32[8,128]{1,0:T(8,128)S(1)} %get-tuple-element.34.refs_0_, bf16[2,8,384,384]{3,2,1,0:T(8,128)(2,1)S(1)} %bitcast.19, ...), custom_call_target="tpu_custom_call", output_to_operand_aliasing={{0}: (4, {}), {1}: (5, {}), {2}: (6, {})} | custom-call | flops 452984832 | bytes 589824 | tf_op jit(solution)/shard_map/work/pallas_call | solution.py:241
  (11 shorter events, 0.1 us)
Async XLA Ops:
  18.6 18.0 %collective-permute-start = (bf16[2,384,384]{2,1,0:T(8,128)(2,1)S(1)}, bf16[2,384,384]{2,1,0:T(8,128)(2,1)S(1)}, u32[]{:S(2)}, u32[]{:S(2)}) collective-permute-start(bf16[2,384,384]{2,1,0:T(8,128)(2,1)S(1)} %bitcast.20), channel_id=1, source_target_pairs={{0,2},{1,3},{2,4},{3,5},{4,6},{5,7},{6,8},{7,9},{8,10},{9,11},{10,... | collective-permute-start | bytes 1769480 | tf_op jit(solution)/shard_map/ppermute | solution.py:265
  20.6 16.1 %collective-permute-start.5 = (bf16[2,384,384]{2,1,0:T(8,128)(2,1)S(1)}, bf16[2,384,384]{2,1,0:T(8,128)(2,1)}, u32[]{:S(2)}, u32[]{:S(2)}) collective-permute-start(bf16[2,384,384]{2,1,0:T(8,128)(2,1)S(1)} %bitcast.21), channel_id=1, source_target_pairs={{0,14},{1,15},{2,0},{3,1},{4,2},{5,3},{6,4},{7,5},{8,6},{9,7},{10,... | collective-permute-start | bytes 1769480 | tf_op jit(solution)/shard_map/ppermute | solution.py:265
  36.6 14.5 %collective-permute-start.1 = (bf16[2,384,384]{2,1,0:T(8,128)(2,1)S(1)}, bf16[2,384,384]{2,1,0:T(8,128)(2,1)S(1)}, u32[]{:S(2)}, u32[]{:S(2)}) collective-permute-start(bf16[2,384,384]{2,1,0:T(8,128)(2,1)S(1)} %collective-permute-done.refs_2_), channel_id=1, source_target_pairs={{0,2},{1,3},{2,4},{3,5},{4,6},{5,7},{6,8},{7,9},{8,10},{9,11},{10,... | collective-permute-start | bytes 1769480 | tf_op jit(solution)/shard_map/ppermute | solution.py:265
  36.6 14.5 %collective-permute-start.6 = (bf16[2,384,384]{2,1,0:T(8,128)(2,1)}, bf16[2,384,384]{2,1,0:T(8,128)(2,1)S(1)}, u32[]{:S(2)}, u32[]{:S(2)}) collective-permute-start(bf16[2,384,384]{2,1,0:T(8,128)(2,1)} %collective-permute-done.5.refs_3_), channel_id=1, source_target_pairs={{0,14},{1,15},{2,0},{3,1},{4,2},{5,3},{6,4},{7,5},{8,6},{9,7},{10,... | collective-permute-start | bytes 1769480 | tf_op jit(solution)/shard_map/ppermute | solution.py:265
  39.9 14.7 %collective-permute-start.16 = (bf16[2,384,384]{2,1,0:T(8,128)(2,1)S(1)}, bf16[2,384,384]{2,1,0:T(8,128)(2,1)S(1)}, u32[]{:S(2)}, u32[]{:S(2)}) collective-permute-start(bf16[2,384,384]{2,1,0:T(8,128)(2,1)S(1)} %bitcast.22), channel_id=1, source_target_pairs={{0,1},{1,0},{2,3},{3,2},{4,5},{5,4},{6,7},{7,6},{8,9},{9,8},{10,11... | collective-permute-start | bytes 1769480 | tf_op jit(solution)/shard_map/ppermute | solution.py:268
  51.1 13.6 %collective-permute-start.2 = (bf16[2,384,384]{2,1,0:T(8,128)(2,1)S(1)}, bf16[2,384,384]{2,1,0:T(8,128)(2,1)S(1)}, u32[]{:S(2)}, u32[]{:S(2)}) collective-permute-start(bf16[2,384,384]{2,1,0:T(8,128)(2,1)S(1)} %collective-permute-done.1.refs_2_), channel_id=1, source_target_pairs={{0,2},{1,3},{2,4},{3,5},{4,6},{5,7},{6,8},{7,9},{8,10},{9,11},{10,... | collective-permute-start | bytes 1769480 | tf_op jit(solution)/shard_map/ppermute | solution.py:265
  51.1 13.7 %collective-permute-start.14 = (bf16[2,384,384]{2,1,0:T(8,128)(2,1)S(1)}, bf16[2,384,384]{2,1,0:T(8,128)(2,1)}, u32[]{:S(2)}, u32[]{:S(2)}) collective-permute-start(bf16[2,384,384]{2,1,0:T(8,128)(2,1)S(1)} %collective-permute-done.refs_2_), channel_id=1, source_target_pairs={{0,1},{1,0},{2,3},{3,2},{4,5},{5,4},{6,7},{7,6},{8,9},{9,8},{10,11... | collective-permute-start | bytes 1769480 | tf_op jit(solution)/shard_map/ppermute | solution.py:268
  51.1 16.5 %collective-permute-start.7 = (bf16[2,384,384]{2,1,0:T(8,128)(2,1)S(1)}, bf16[2,384,384]{2,1,0:T(8,128)(2,1)S(1)}, u32[]{:S(2)}, u32[]{:S(2)}) collective-permute-start(bf16[2,384,384]{2,1,0:T(8,128)(2,1)S(1)} %collective-permute-done.6.refs_3_), channel_id=1, source_target_pairs={{0,14},{1,15},{2,0},{3,1},{4,2},{5,3},{6,4},{7,5},{8,6},{9,7},{10,... | collective-permute-start | bytes 1769480 | tf_op jit(solution)/shard_map/ppermute | solution.py:265
  54.3 13.3 %collective-permute-start.15 = (bf16[2,384,384]{2,1,0:T(8,128)(2,1)}, bf16[2,384,384]{2,1,0:T(8,128)(2,1)}, u32[]{:S(2)}, u32[]{:S(2)}) collective-permute-start(bf16[2,384,384]{2,1,0:T(8,128)(2,1)} %collective-permute-done.5.refs_3_), channel_id=1, source_target_pairs={{0,1},{1,0},{2,3},{3,2},{4,5},{5,4},{6,7},{7,6},{8,9},{9,8},{10,11... | collective-permute-start | bytes 1769480 | tf_op jit(solution)/shard_map/ppermute | solution.py:268
  54.6 0.8 copy-start.2
  55.4 12.4 %collective-permute-start.12 = (bf16[2,384,384]{2,1,0:T(8,128)(2,1)S(1)}, bf16[2,384,384]{2,1,0:T(8,128)(2,1)}, u32[]{:S(2)}, u32[]{:S(2)}) collective-permute-start(bf16[2,384,384]{2,1,0:T(8,128)(2,1)S(1)} %collective-permute-done.1.refs_2_), channel_id=1, source_target_pairs={{0,1},{1,0},{2,3},{3,2},{4,5},{5,4},{6,7},{7,6},{8,9},{9,8},{10,11... | collective-permute-start | bytes 1769480 | tf_op jit(solution)/shard_map/ppermute | solution.py:268
  56.5 2.3 %copy-start = (bf16[2,8,1,384,384]{4,3,2,1,0:T(8,128)(2,1)S(1)}, bf16[2,8,1,384,384]{4,3,2,1,0:T(8,128)(2,1)}, u32[]{:S(2)}) copy-start(bf16[2,8,1,384,384]{4,3,2,1,0:T(8,128)(2,1)} %param.4) | copy-start | bytes 14155780
  58.9 12.9 %copy-start.1 = (bf16[2,8,1,384,384]{4,3,2,1,0:T(8,128)(2,1)S(1)}, bf16[2,8,1,384,384]{4,3,2,1,0:T(8,128)(2,1)}, u32[]{:S(2)}) copy-start(bf16[2,8,1,384,384]{4,3,2,1,0:T(8,128)(2,1)} %param.4) | copy-start | bytes 14155780
  58.9 12.9 %copy-start.3 = (bf16[2,384,384]{2,1,0:T(8,128)(2,1)S(1)}, bf16[2,384,384]{2,1,0:T(8,128)(2,1)}, u32[]{:S(2)}) copy-start(bf16[2,384,384]{2,1,0:T(8,128)(2,1)} %copy-done.2) | copy-start | bytes 1769476
  64.7 21.8 %collective-permute-start.13 = (bf16[2,384,384]{2,1,0:T(8,128)(2,1)S(1)}, bf16[2,384,384]{2,1,0:T(8,128)(2,1)S(1)}, u32[]{:S(2)}, u32[]{:S(2)}) collective-permute-start(bf16[2,384,384]{2,1,0:T(8,128)(2,1)S(1)} %collective-permute-done.6.refs_3_), channel_id=1, source_target_pairs={{0,1},{1,0},{2,3},{3,2},{4,5},{5,4},{6,7},{7,6},{8,9},{9,8},{10,11... | collective-permute-start | bytes 1769480 | tf_op jit(solution)/shard_map/ppermute | solution.py:268
  64.8 29.3 %collective-permute-start.10 = (bf16[2,384,384]{2,1,0:T(8,128)(2,1)S(1)}, bf16[2,384,384]{2,1,0:T(8,128)(2,1)S(1)}, u32[]{:S(2)}, u32[]{:S(2)}) collective-permute-start(bf16[2,384,384]{2,1,0:T(8,128)(2,1)S(1)} %collective-permute-done.2.refs_2_), channel_id=1, source_target_pairs={{0,1},{1,0},{2,3},{3,2},{4,5},{5,4},{6,7},{7,6},{8,9},{9,8},{10,11... | collective-permute-start | bytes 1769480 | tf_op jit(solution)/shard_map/ppermute | solution.py:268
  67.6 26.5 %collective-permute-start.11 = (bf16[2,384,384]{2,1,0:T(8,128)(2,1)S(1)}, bf16[2,384,384]{2,1,0:T(8,128)(2,1)S(1)}, u32[]{:S(2)}, u32[]{:S(2)}) collective-permute-start(bf16[2,384,384]{2,1,0:T(8,128)(2,1)S(1)} %collective-permute-done.7.refs_3_), channel_id=1, source_target_pairs={{0,1},{1,0},{2,3},{3,2},{4,5},{5,4},{6,7},{7,6},{8,9},{9,8},{10,11... | collective-permute-start | bytes 1769480 | tf_op jit(solution)/shard_map/ppermute | solution.py:268
  67.7 11.4 %collective-permute-start.3 = (bf16[384,384]{1,0:T(8,128)(2,1)S(1)}, bf16[384,384]{1,0:T(8,128)(2,1)S(1)}, u32[]{:S(2)}, u32[]{:S(2)}) collective-permute-start(bf16[384,384]{1,0:T(8,128)(2,1)S(1)} %slice_bitcast_fusion.1), channel_id=1, source_target_pairs={{0,2},{1,3},{2,4},{3,5},{4,6},{5,7},{6,8},{7,9},{8,10},{9,11},{10,... | collective-permute-start | bytes 884744 | tf_op jit(solution)/shard_map/ppermute | solution.py:265
  67.8 18.6 %collective-permute-start.8 = (bf16[384,384]{1,0:T(8,128)(2,1)S(1)}, bf16[384,384]{1,0:T(8,128)(2,1)S(1)}, u32[]{:S(2)}, u32[]{:S(2)}) collective-permute-start(bf16[384,384]{1,0:T(8,128)(2,1)S(1)} %slice_bitcast_fusion), channel_id=1, source_target_pairs={{0,14},{1,15},{2,0},{3,1},{4,2},{5,3},{6,4},{7,5},{8,6},{9,7},{10,... | collective-permute-start | bytes 884744 | tf_op jit(solution)/shard_map/ppermute | solution.py:265
  79.1 22.7 %collective-permute-start.4 = (bf16[384,384]{1,0:T(8,128)(2,1)S(1)}, bf16[384,384]{1,0:T(8,128)(2,1)S(1)}, u32[]{:S(2)}, u32[]{:S(2)}) collective-permute-start(bf16[384,384]{1,0:T(8,128)(2,1)S(1)} %collective-permute-done.3.refs_2_), channel_id=1, source_target_pairs={{0,1},{1,0},{2,3},{3,2},{4,5},{5,4},{6,7},{7,6},{8,9},{9,8},{10,11... | collective-permute-start | bytes 884744 | tf_op jit(solution)/shard_map/ppermute | solution.py:268
  86.4 15.4 %collective-permute-start.9 = (bf16[384,384]{1,0:T(8,128)(2,1)S(1)}, bf16[384,384]{1,0:T(8,128)(2,1)S(1)}, u32[]{:S(2)}, u32[]{:S(2)}) collective-permute-start(bf16[384,384]{1,0:T(8,128)(2,1)S(1)} %collective-permute-done.8.refs_3_), channel_id=1, source_target_pairs={{0,1},{1,0},{2,3},{3,2},{4,5},{5,4},{6,7},{7,6},{8,9},{9,8},{10,11... | collective-permute-start | bytes 884744 | tf_op jit(solution)/shard_map/ppermute | solution.py:268
